TPU v7x, 32 devices: a whole 2x2x4 slice. The times are simulated.
32 devices in a mesh: expert: 16 (over z, y, core), tensor: 2 (over x).
Axes of the slice: x: 2, y: 2, z: 4, core: 2. Of those that a mesh axis runs over, the one named last changes fastest.
Arguments:
- tokens: bfloat16 [18912, 768], P('expert'), may hold values from -6 to 6
- teacher: bfloat16 [18912, 768], P('expert'), may hold values from -12 to 12
- valid_flags: int32 [96], P('expert'), may hold values from 0 to 1, as said below
- routes: int32 [18912, 2], P('expert'), may hold values from 0 to 7, all different within a row; in each aligned block of 1182 rows (0 to 1181, 1182 to 2363, ...) at most 440 rows name the same one
- capacity: int32 [8], replicated, may hold values from 220 to 440, as said below
- norm_gains: bfloat16 [4, 768], replicated, may hold values from 0.5 to 1.5
- norm_biases: bfloat16 [4, 768], replicated, may hold values from -0.59765625 to 0.59765625
- attn_qkv: bfloat16 [2, 3, 768, 768], P(None, None, None, 'tensor'), may hold values from -0.21875 to 0.21875
- attn_out: bfloat16 [2, 768, 768], P(None, 'tensor'), may hold values from -1.75 to 1.75
- mlp_in: bfloat16 [768, 3072], P(None, 'tensor'), may hold values from -0.21875 to 0.21875
- mlp_out: bfloat16 [3072, 768], P('tensor'), may hold values from -0.109375 to 0.109375
- router: bfloat16 [768, 8], replicated, may hold values from -0.15625 to 0.15625
- expert_in: bfloat16 [16, 768, 1536], P('expert', None, 'tensor'), may hold values from -0.21875 to 0.21875
- expert_out: bfloat16 [16, 1536, 768], P('expert', 'tensor'), may hold values from -0.109375 to 0.109375
Outputs:
- activations: bfloat16 [18912, 768], P('expert')
- input_grad: bfloat16 [18912, 768], P('expert')
- gain_grad: float32 [4, 768], P(None, 'expert')
- bias_grad: float32 [3, 768], P(None, 'expert')
- expert_norm_bias_grad: float32 [768], P('expert')
- qkv_grad: float32 [2, 3, 768, 768], P(None, None, 'expert', 'tensor')
- out_proj_grad: float32 [2, 768, 768], P(None, 'tensor', 'expert')
- mlp_in_grad: float32 [768, 3072], P('expert', 'tensor')
- mlp_out_grad: float32 [3072, 768], P('tensor', 'expert')
- router_grad: float32 [768, 8], P('expert')
- expert_in_grad: float32 [16, 768, 1536], P('expert', None, 'tensor')
- expert_out_grad: float32 [16, 1536, 768], P('expert', 'tensor')
Inputs may be any that keep to these rules, and one draw needn't show every extreme that they name: `valid_flags`: 1 marks an image whose tokens count in the loss; image 0 is always valid. `routes`: the two experts of a token differ; among the rows of one index of expert no expert is named by more than 440 rows, and exactly 440 in some. `capacity`: exactly 440 for at least one expert.
All inputs are finite; a program needn't handle non-finite values.
Results may differ from a plain program's by a relative error of at most 0.035.
Values may be sent and summed in bfloat16 or wider, within the bound.
No kernel may reach another device: no remote copies, remote signals or barrier semaphores. Data moves between devices by JAX's collectives and lax.ppermute only.
A program may use at most 256 MiB of HBM per device.

v0:
```python
import jax
import jax.numpy as jnp
from jax import lax
from jax.sharding import PartitionSpec as P

HD = 64
SEQ = 197
IMG_DEV = 6


epsilon = 1e-06


def normalize(values, gain_row, bias_row):
    center = values - jnp.mean(values, axis=-1, keepdims=True)
    scaled = center * lax.rsqrt(jnp.mean(center * center, axis=-1, keepdims=True) + epsilon)
    return scaled * gain_row + bias_row


def norm_backward(values, gain_row, bias_row, grad_normed):
    pull_back = jax.vjp(normalize, values, gain_row, bias_row)[1]
    return pull_back(grad_normed)


def gelu_tanh(values):
    return jax.nn.gelu(values, approximate=True)


def tensor_total(partial_value):
    return lax.psum(partial_value.astype(jnp.bfloat16), "tensor").astype(jnp.float32)


def to_experts(buffer):
    doubled = jnp.repeat(buffer, 2, axis=0)
    arrived = lax.all_to_all(doubled, "expert", split_axis=0, concat_axis=0, tiled=True)
    return arrived


def from_experts(partial_value, experts):
    share_rows = lax.psum_scatter(
        partial_value.astype(jnp.bfloat16), "tensor", scatter_dimension=1, tiled=True
    )
    full_rows = lax.all_gather(share_rows, "tensor", axis=1, tiled=True)
    back_rows = lax.all_to_all(full_rows, "expert", split_axis=0, concat_axis=0, tiled=True)
    slots_each = back_rows.shape[1]
    halves = back_rows.reshape(experts, 2, slots_each, -1).astype(jnp.float32)
    return jnp.sum(halves, axis=1).reshape(experts * slots_each, -1)


def attend_forward(normed_low, qkv_weight, out_weight):
    packed = jnp.einsum(
        "td,sdc->stc", normed_low, qkv_weight, preferred_element_type=jnp.float32
    ).astype(jnp.bfloat16)
    heads_qkv = packed.reshape(3, IMG_DEV, SEQ, -1, HD)
    scores = jnp.einsum(
        "bqhe,bkhe->bhqk", heads_qkv[0], heads_qkv[1], preferred_element_type=jnp.float32
    ) * HD ** (-0.5)
    log_total = jax.nn.logsumexp(scores, axis=-1, keepdims=True)
    attn_probs = jnp.exp(scores - log_total).astype(jnp.bfloat16)
    mixed_rows = jnp.einsum(
        "bhqk,bkhe->bqhe", attn_probs, heads_qkv[2], preferred_element_type=jnp.float32
    )
    mixed_rows = mixed_rows.reshape(normed_low.shape[0], -1).astype(jnp.bfloat16)
    branch = jnp.dot(mixed_rows, out_weight, preferred_element_type=jnp.float32)
    return (branch, (packed, log_total, mixed_rows))


def attend_backward(grad_residual, normed_low, qkv_weight, out_weight, kept_state):
    packed, log_total, mixed_rows = kept_state
    grad_low = grad_residual.astype(jnp.bfloat16)
    grad_out = jnp.einsum("tc,td->cd", mixed_rows, grad_low, preferred_element_type=jnp.float32)
    heads_qkv = packed.reshape(3, IMG_DEV, SEQ, -1, HD)
    grad_mixed = jnp.einsum("td,cd->tc", grad_low, out_weight, preferred_element_type=jnp.float32)
    grad_mixed = grad_mixed.astype(jnp.bfloat16).reshape(heads_qkv.shape[1:])
    scores = jnp.einsum(
        "bqhe,bkhe->bhqk", heads_qkv[0], heads_qkv[1], preferred_element_type=jnp.float32
    ) * HD ** (-0.5)
    attn_probs = jnp.exp(scores - log_total)
    grad_probs = jnp.einsum(
        "bqhe,bkhe->bhqk", grad_mixed, heads_qkv[2], preferred_element_type=jnp.float32
    )
    grad_scores = attn_probs * (
        grad_probs - jnp.sum(grad_probs * attn_probs, axis=-1, keepdims=True)
    )
    grad_scores = grad_scores.astype(jnp.bfloat16)
    grad_query = jnp.einsum(
        "bhqk,bkhe->bqhe", grad_scores, heads_qkv[1], preferred_element_type=jnp.float32
    ) * HD ** (-0.5)
    grad_key = jnp.einsum(
        "bhqk,bqhe->bkhe", grad_scores, heads_qkv[0], preferred_element_type=jnp.float32
    ) * HD ** (-0.5)
    grad_value = jnp.einsum(
        "bhqk,bqhe->bkhe",
        attn_probs.astype(jnp.bfloat16),
        grad_mixed,
        preferred_element_type=jnp.float32,
    )
    grad_packed = (
        jnp.stack([grad_query, grad_key, grad_value]).reshape(packed.shape).astype(jnp.bfloat16)
    )
    grad_weight = jnp.einsum(
        "td,stc->sdc", normed_low, grad_packed, preferred_element_type=jnp.float32
    )
    grad_normed = jnp.einsum(
        "stc,sdc->td", grad_packed, qkv_weight, preferred_element_type=jnp.float32
    )
    return (grad_normed, grad_weight, grad_out)


def ffn_forward(rows_in, weight_in, weight_out):
    hidden = jnp.dot(rows_in, weight_in, preferred_element_type=jnp.float32)
    active = gelu_tanh(hidden).astype(jnp.bfloat16)
    return (jnp.dot(active, weight_out, preferred_element_type=jnp.float32), hidden, active)


def ffn_backward(grad_low, rows_in, weight_in, weight_out, hidden, active):
    grad_out = jnp.einsum("tf,td->fd", active, grad_low, preferred_element_type=jnp.float32)
    grad_active = jnp.einsum("td,fd->tf", grad_low, weight_out, preferred_element_type=jnp.float32)
    grad_hidden = jax.vjp(gelu_tanh, hidden)[1](grad_active)[0].astype(jnp.bfloat16)
    grad_in = jnp.einsum("td,tf->df", rows_in, grad_hidden, preferred_element_type=jnp.float32)
    grad_rows = jnp.einsum("tf,df->td", grad_hidden, weight_in, preferred_element_type=jnp.float32)
    return (grad_rows, grad_in, grad_out)


def body(
    tokens,
    teacher,
    valid_flags,
    routes,
    capacity,
    norm_gains,
    norm_biases,
    attn_qkv,
    attn_out,
    mlp_in,
    mlp_out,
    router,
    expert_in,
    expert_out,
):
    local_rows = tokens.shape[0]
    experts = router.shape[1]
    slots_each = 4 * (3 * local_rows // (4 * experts))
    all_slots = experts * slots_each
    owners = lax.axis_size("expert")
    gain_rows = norm_gains.astype(jnp.float32)
    bias_rows = norm_biases.astype(jnp.float32)
    local_count = SEQ * jnp.sum(valid_flags.astype(jnp.float32))
    valid_count = lax.psum(local_count, "expert")
    valid_rows = jnp.repeat(valid_flags.astype(jnp.float32), SEQ)[:, None]
    start_rows = tokens.astype(jnp.float32)
    normed_first = normalize(start_rows, gain_rows[0], bias_rows[0]).astype(jnp.bfloat16)
    branch, saved_first = attend_forward(normed_first, attn_qkv[0], attn_out[0])
    after_attn = start_rows + tensor_total(branch)
    normed_dense = normalize(after_attn, gain_rows[1], bias_rows[1]).astype(jnp.bfloat16)
    branch, dense_hidden, dense_active = ffn_forward(normed_dense, mlp_in, mlp_out)
    after_dense = after_attn + tensor_total(branch)
    normed_second = normalize(after_dense, gain_rows[2], bias_rows[2]).astype(jnp.bfloat16)
    branch, saved_second = attend_forward(normed_second, attn_qkv[1], attn_out[1])
    after_second = after_dense + tensor_total(branch)
    normed_expert = normalize(after_second, gain_rows[3], bias_rows[3]).astype(jnp.bfloat16)
    logits = jnp.dot(normed_expert, router, preferred_element_type=jnp.float32)
    picker = routes[:, :, None] == jnp.arange(experts, dtype=jnp.int32)[None, None, :]
    chosen = jnp.sum(jnp.where(picker, logits[:, None, :], 0.0), axis=2)
    gate_vals = jax.nn.softmax(chosen, axis=1)
    expert_of = jnp.concatenate([routes[:, 0], routes[:, 1]])
    onehot = (expert_of[:, None] == jnp.arange(experts, dtype=jnp.int32)[None, :]).astype(jnp.int32)
    earlier = jnp.cumsum(onehot, axis=0) - onehot
    position = jnp.sum(earlier * onehot, axis=1)
    kept_mask = position < jnp.sum(onehot * capacity[None, :], axis=1)
    slot_of = expert_of * slots_each + position
    pair_of = (
        jnp.full((all_slots,), -1, jnp.int32)
        .at[jnp.where(kept_mask, slot_of, all_slots)]
        .set(jnp.arange(2 * local_rows, dtype=jnp.int32), mode="drop")
    )
    slot_used = (pair_of >= 0)[:, None]
    pair_index = jnp.maximum(pair_of, 0)
    fetch_at = jnp.where(kept_mask, slot_of, 0)
    sent_rows = jnp.where(
        slot_used, normed_expert[pair_index % local_rows], jnp.zeros((), jnp.bfloat16)
    )
    rows_in = to_experts(sent_rows.reshape(experts, slots_each, -1)).reshape(
        owners * slots_each, -1
    )
    branch, expert_hidden, expert_active = ffn_forward(rows_in, expert_in[0], expert_out[0])
    merged = from_experts(branch.reshape(owners, slots_each, -1), experts)
    picked = jnp.where(kept_mask[:, None], merged[fetch_at], 0.0).reshape(2, local_rows, -1)
    gate_pairs = gate_vals.T[:, :, None]
    final_rows = after_second + jnp.sum(gate_pairs * picked, axis=0)
    grad_final = (
        local_rows * owners / valid_count * valid_rows * (final_rows - teacher.astype(jnp.float32))
    )
    grad_gates = jnp.sum(picked * grad_final[None], axis=2).T
    grad_pairs = (gate_pairs * grad_final[None]).astype(jnp.bfloat16).reshape(2 * local_rows, -1)
    grad_sent = jnp.where(slot_used, grad_pairs[pair_index], jnp.zeros((), jnp.bfloat16))
    grad_arrived = to_experts(grad_sent.reshape(experts, slots_each, -1)).reshape(
        owners * slots_each, -1
    )
    grad_rows, grad_expert_in, grad_expert_out = ffn_backward(
        grad_arrived, rows_in, expert_in[0], expert_out[0], expert_hidden, expert_active
    )
    grad_merged = from_experts(grad_rows.reshape(owners, slots_each, -1), experts)
    grad_taken = jnp.where(kept_mask[:, None], grad_merged[fetch_at], 0.0).reshape(
        2, local_rows, -1
    )
    grad_chosen = gate_vals * (grad_gates - jnp.sum(gate_vals * grad_gates, axis=1, keepdims=True))
    grad_logits = jnp.sum(jnp.where(picker, grad_chosen[:, :, None], 0.0), axis=1).astype(
        jnp.bfloat16
    )
    grad_router = jnp.einsum(
        "td,te->de", normed_expert, grad_logits, preferred_element_type=jnp.float32
    )
    grad_normed = jnp.sum(grad_taken, axis=0)
    grad_normed = grad_normed + jnp.einsum(
        "te,de->td", grad_logits, router, preferred_element_type=jnp.float32
    )
    grad_back, gain_four, bias_four = norm_backward(
        after_second, gain_rows[3], bias_rows[3], grad_normed
    )
    grad_second = grad_final + grad_back
    grad_part, qkv_two, out_two = attend_backward(
        grad_second, normed_second, attn_qkv[1], attn_out[1], saved_second
    )
    grad_back, gain_three, bias_three = norm_backward(
        after_dense, gain_rows[2], bias_rows[2], tensor_total(grad_part)
    )
    grad_dense = grad_second + grad_back
    grad_part, grad_mlp_in, grad_mlp_out = ffn_backward(
        grad_dense.astype(jnp.bfloat16), normed_dense, mlp_in, mlp_out, dense_hidden, dense_active
    )
    grad_back, gain_two, bias_two = norm_backward(
        after_attn, gain_rows[1], bias_rows[1], tensor_total(grad_part)
    )
    grad_attn = grad_dense + grad_back
    grad_part, qkv_one, out_one = attend_backward(
        grad_attn, normed_first, attn_qkv[0], attn_out[0], saved_first
    )
    grad_back, gain_one, bias_one = norm_backward(
        start_rows, gain_rows[0], bias_rows[0], tensor_total(grad_part)
    )
    grad_start = grad_attn + grad_back
    summed = (
        lax.psum_scatter(
            jnp.stack([gain_one, gain_two, gain_three, gain_four]),
            "expert",
            scatter_dimension=1,
            tiled=True,
        ),
        lax.psum_scatter(
            jnp.stack([bias_one, bias_two, bias_three]), "expert", scatter_dimension=1, tiled=True
        ),
        lax.psum_scatter(bias_four, "expert", scatter_dimension=0, tiled=True),
        lax.psum_scatter(jnp.stack([qkv_one, qkv_two]), "expert", scatter_dimension=2, tiled=True),
        lax.psum_scatter(jnp.stack([out_one, out_two]), "expert", scatter_dimension=2, tiled=True),
        lax.psum_scatter(grad_mlp_in, "expert", scatter_dimension=0, tiled=True),
        lax.psum_scatter(grad_mlp_out, "expert", scatter_dimension=1, tiled=True),
        lax.psum_scatter(grad_router, "expert", scatter_dimension=0, tiled=True),
    )
    return (
        final_rows.astype(jnp.bfloat16),
        grad_start.astype(jnp.bfloat16),
        summed[0],
        summed[1],
        summed[2],
        summed[3],
        summed[4],
        summed[5],
        summed[6],
        summed[7],
        grad_expert_in[None],
        grad_expert_out[None],
    )


def solution(mesh):
    in_specs = (
        P("expert", None),
        P("expert", None),
        P("expert"),
        P("expert", None),
        P(),
        P(),
        P(),
        P(None, None, None, "tensor"),
        P(None, "tensor", None),
        P(None, "tensor"),
        P("tensor", None),
        P(),
        P("expert", None, "tensor"),
        P("expert", "tensor", None),
    )
    out_specs = (
        P("expert", None),
        P("expert", None),
        P(None, "expert"),
        P(None, "expert"),
        P("expert"),
        P(None, None, "expert", "tensor"),
        P(None, "tensor", "expert"),
        P("expert", "tensor"),
        P("tensor", "expert"),
        P("expert", None),
        P("expert", None, "tensor"),
        P("expert", "tensor", None),
    )
    return jax.shard_map(body, mesh=mesh, in_specs=in_specs, out_specs=out_specs, check_vma=False)
```

profile of v0, /device:TPU:0, one launch (start us, length us, event | category | flops | bytes accessed | tf_op | source)
XLA Modules:
  0.0 2914.6 jit_solution(6737565340386454107)
XLA Ops:
  57.4 59.4 %all-reduce.13.cloned.1.call-done = bf16[1182,768]{1,0:T(8,128)(2,1)} async-done(((bf16[1182,768]{1,0:T(8,128)(2,1)}), bf16[1182,768]{1,0:T(8,128)(2,1)}) %all-reduce.13.cloned.1.call-update) | async-done | bytes 1815568 | tf_op jit(solution)/shard_map/psum | solution.py:30
  133.9 56.3 %all-reduce.15.cloned.1.call-done = bf16[1182,768]{1,0:T(8,128)(2,1)} async-done(((bf16[1182,768]{1,0:T(8,128)(2,1)}), bf16[1182,768]{1,0:T(8,128)(2,1)}) %all-reduce.15.cloned.1.call-update) | async-done | bytes 1815568 | tf_op jit(solution)/shard_map/psum | solution.py:30
  242.7 12.3 scatter_custom_fusion
  255.7 40.5 %all-reduce.17.cloned.1.call-done = bf16[1182,768]{1,0:T(8,128)(2,1)} async-done(((bf16[1182,768]{1,0:T(8,128)(2,1)}), bf16[1182,768]{1,0:T(8,128)(2,1)}) %all-reduce.17.cloned.1.call-update) | async-done | bytes 1815568 | tf_op jit(solution)/shard_map/psum | solution.py:30
  302.3 15.6 gather_fusion
  322.4 240.6 %all_to_all.20 = bf16[16,440,768]{2,1,0:T(8,128)(2,1)} all-to-all(bf16[16,440,768]{2,1,0:T(8,128)(2,1)S(1)} %bitcast.188), channel_id=1, replica_groups=mesh['expert'=16,'tensor'=2] {'expert'}, dimensions={0} | all-to-all | bytes 21626880 | tf_op jit(solution)/shard_map/all_to_all | solution.py:35
  562.9 20.0 multiply_convert_fusion
  582.9 13.2 convolution_convert_fusion.1
  596.1 9.1 copy.242
  605.2 125.0 %reduce-scatter.14.cloned.1.call-done = bf16[16,220,768]{2,0,1:T(8,128)(2,1)} async-done(((bf16[16,440,768]{2,0,1:T(8,128)(2,1)}), bf16[16,220,768]{2,0,1:T(8,128)(2,1)}) %reduce-scatter.14.cloned.1.call-update) | async-done | bytes 5406736 | tf_op jit(solution)/shard_map/reduce_scatter | solution.py:40
  730.3 134.6 %all-gather.3.cloned.1.call-done = bf16[16,440,768]{2,0,1:T(8,128)(2,1)} async-done(((bf16[16,220,768]{2,0,1:T(8,128)(2,1)}), bf16[16,440,768]{2,0,1:T(8,128)(2,1)}) %all-gather.3.cloned.1.call-update) | async-done | bytes 10813456 | tf_op jit(solution)/shard_map/all_gather | solution.py:43
  864.9 12.0 copy.243
  876.9 5.8 all-to-all-start.1
  884.0 211.2 %psum.52 = f32[]{:T(128)} all-reduce(f32[]{:T(128)S(6)} %mul_shard_map.3), channel_id=1, replica_groups=mesh['expert'=16,'tensor'=2] {'expert'}, use_global_device_ids=true, to_apply=%region_27.28 | all-reduce | flops 1 | bytes 8 | tf_op jit(solution)/shard_map/psum | solution.py:149
  1099.1 11.0 convert_reduce_fusion.1
  1110.1 14.3 gather_fusion.1
  1124.4 6.6 gather.23
  1142.8 6.6 mul.519
  1149.4 8.4 multiply_reduce_fusion.2
  1157.9 16.4 gather_fusion.2
  1178.7 279.8 %all_to_all.21 = bf16[16,440,768]{2,1,0:T(8,128)(2,1)S(1)} all-to-all(bf16[16,440,768]{2,1,0:T(8,128)(2,1)S(1)} %bitcast.189), channel_id=1, replica_groups=mesh['expert'=16,'tensor'=2] {'expert'}, dimensions={0} | all-to-all | bytes 21626880 | tf_op jit(solution)/shard_map/all_to_all | solution.py:35
  1458.5 28.1 fusion.6
  1486.6 11.8 convolution_convert_fusion
  1498.5 9.2 copy.246
  1507.7 125.0 %reduce-scatter.16.cloned.1.call-done = bf16[16,220,768]{2,0,1:T(8,128)(2,1)} async-done(((bf16[16,440,768]{2,0,1:T(8,128)(2,1)}), bf16[16,220,768]{2,0,1:T(8,128)(2,1)}) %reduce-scatter.16.cloned.1.call-update) | async-done | bytes 5406736 | tf_op jit(solution)/shard_map/reduce_scatter | solution.py:40
  1632.7 134.7 %all-gather.5.cloned.1.call-done = bf16[16,440,768]{2,0,1:T(8,128)(2,1)} async-done(((bf16[16,220,768]{2,0,1:T(8,128)(2,1)}), bf16[16,440,768]{2,0,1:T(8,128)(2,1)}) %all-gather.5.cloned.1.call-update) | async-done | bytes 10813456 | tf_op jit(solution)/shard_map/all_gather | solution.py:43
  1767.4 12.4 copy.247
  1779.9 5.8 all-to-all-start.3
  1785.9 192.7 %all-to-all-done.3 = bf16[16,440,768]{2,1,0:T(8,128)(2,1)} async-done(((bf16[16,440,768]{2,1,0:T(8,128)(2,1)}), bf16[16,440,768]{2,1,0:T(8,128)(2,1)}, u32[]{:S(2)}, u32[]{:S(2)}) %all-to-all-start.3) | async-done | bytes 10813472 | tf_op jit(solution)/shard_map/all_to_all | solution.py:44
  1978.6 10.9 convert_reduce_fusion
  1989.5 14.2 gather_fusion.3
  2003.8 6.8 gather.27
  2031.1 5.6 multiply_reduce_fusion.1
  2079.2 97.6 %all-reduce.19.cloned.1.call-done = bf16[1182,768]{1,0:T(8,128)(2,1)} async-done(((bf16[1182,768]{1,0:T(8,128)(2,1)}), bf16[1182,768]{1,0:T(8,128)(2,1)}) %all-reduce.19.cloned.1.call-update) | async-done | bytes 1815568 | tf_op jit(solution)/shard_map/psum | solution.py:30
  2186.2 7.0 fusion.13
  2199.3 57.0 %all-reduce.21.cloned.1.call-done = bf16[1182,768]{1,0:T(8,128)(2,1)} async-done(((bf16[1182,768]{1,0:T(8,128)(2,1)}), bf16[1182,768]{1,0:T(8,128)(2,1)}) %all-reduce.21.cloned.1.call-update) | async-done | bytes 1815568 | tf_op jit(solution)/shard_map/psum | solution.py:30
  2329.6 6.3 convolution_bitcast_fusion.2
  2348.3 35.2 %all-reduce.23.cloned.1.call-done = bf16[1182,768]{1,0:T(8,128)(2,1)} async-done(((bf16[1182,768]{1,0:T(8,128)(2,1)}), bf16[1182,768]{1,0:T(8,128)(2,1)}) %all-reduce.23.cloned.1.call-update) | async-done | bytes 1815568 | tf_op jit(solution)/shard_map/psum | solution.py:30
  2399.0 13.6 copy.280
  2418.6 8.9 fusion.118
  2427.6 9.7 fusion.70
  2444.6 14.6 convolution_bitcast_fusion.5
  2459.2 14.7 convolution_bitcast_fusion.4
  2473.9 29.6 %all-reduce.1 = f32[768]{0:T(1024)S(1)} all-reduce(f32[768]{0:T(1024)S(1)} %copy-done.118), channel_id=6, replica_groups=mesh['expert'=16,'tensor'=2] {'expert'}, use_global_device_ids=true, to_apply=%region_57.58.clone | all-reduce | flops 768 | bytes 6144
  2510.2 50.1 %reduce-scatter.22.cloned.1.call-done = f32[48,4]{1,0:T(8,128)} async-done(((f32[768,4]{1,0:T(8,128)}), f32[48,4]{1,0:T(8,128)}) %reduce-scatter.22.cloned.1.call-update) | async-done | bytes 784
  2561.6 186.9 %all-reduce.25.cloned.1.call-done = (f32[2,3,768,384]{3,0,1,2:T(2,128)}, f32[2,384,768]{1,0,2:T(2,128)}) async-done(((f32[2,3,768,384]{3,0,1,2:T(2,128)}, f32[2,384,768]{1,0,2:T(2,128)}), (f32[2,3,768,384]{3,0,1,2:T(2,128)}, f32[2,384,768]{1,0,2:T(2,128)})) %all-reduce.25.cloned.1.call-update) | async-done | bytes 9437200
  2752.1 76.4 %reduce-scatter.18.cloned.1.call-done = f32[48,1536]{1,0:T(8,128)} async-done(((f32[768,1536]{1,0:T(8,128)}), f32[48,1536]{1,0:T(8,128)}) %reduce-scatter.18.cloned.1.call-update) | async-done | bytes 294928 | tf_op jit(solution)/shard_map/reduce_scatter | solution.py:256
  2828.4 79.4 %reduce-scatter.20.cloned.1.call-done = f32[1536,48]{0,1:T(8,128)} async-done(((f32[1536,768]{0,1:T(8,128)}), f32[1536,48]{0,1:T(8,128)}) %reduce-scatter.20.cloned.1.call-update) | async-done | bytes 294928 | tf_op jit(solution)/shard_map/reduce_scatter | solution.py:257
  (519 shorter events, 353.8 us)
Async XLA Ops:
  7.2 120.6 %copy-start = (bf16[1536,768]{1,0:T(8,128)(2,1)S(1)}, bf16[1536,768]{1,0:T(8,128)(2,1)}, u32[]{:S(2)}) copy-start(bf16[1536,768]{1,0:T(8,128)(2,1)} %param.24) | copy-start | bytes 7077892
  7.2 109.7 %all-reduce.13.cloned.1.call-start = ((), (), s32[]{:S(2)}) async-start(), calls=%async_computation.11 | async-start | bytes 3637248 | tf_op jit(solution)/shard_map/psum | solution.py:30
  13.6 107.9 %copy-start.104 = (f32[768]{0:T(1024)}, f32[768]{0:T(1024)S(1)}, u32[]{:S(2)}) copy-start(f32[768]{0:T(1024)S(1)} %get-tuple-element.135) | copy-start | bytes 9220
  13.6 286.2 %copy-start.98 = (f32[768]{0:T(1024)}, f32[768]{0:T(1024)S(1)}, u32[]{:S(2)}) copy-start(f32[768]{0:T(1024)S(1)} %get-tuple-element.137) | copy-start | bytes 9220
  57.2 64.3 %copy-start.126 = (f32[768]{0:T(1024)S(1)}, f32[768]{0:T(1024)}, u32[]{:S(2)}) copy-start(f32[768]{0:T(1024)} %get-tuple-element.97) | copy-start | bytes 9220
  57.2 133.0 %all-reduce.15.cloned.1.call-start = ((), (), s32[]{:S(2)}) async-start(), calls=%async_computation.12 | async-start | bytes 3637248 | tf_op jit(solution)/shard_map/psum | solution.py:30
  133.2 163.0 %all-reduce.17.cloned.1.call-start = ((), (), s32[]{:S(2)}) async-start(), calls=%async_computation.13 | async-start | bytes 3637248 | tf_op jit(solution)/shard_map/psum | solution.py:30
  239.2 491.1 %reduce-scatter.14.cloned.1.call-start = ((), (), s32[]{:S(2)}) async-start(), calls=%async_computation.14 | async-start | bytes 16220160 | tf_op jit(solution)/shard_map/reduce_scatter | solution.py:40
  322.3 240.6 %copy-start.140 = (bf16[1,768,768]{2,1,0:T(8,128)(2,1)S(1)}, bf16[1,768,768]{2,1,0:T(8,128)(2,1)}, u32[]{:S(2)}) copy-start(bf16[1,768,768]{2,1,0:T(8,128)(2,1)} %param.26) | copy-start | bytes 3538948
  562.9 20.0 copy-start.138
  605.2 259.7 %all-gather.3.cloned.1.call-start = ((), (), s32[]{:S(2)}) async-start(), calls=%async_computation.15 | async-start | bytes 16220160 | tf_op jit(solution)/shard_map/all_gather | solution.py:43
  876.9 219.3 %copy-start.110 = (bf16[768,8]{0,1:T(8,128)(2,1)S(1)}, bf16[768,8]{0,1:T(8,128)(2,1)}, u32[]{:S(2)}) copy-start(bf16[768,8]{0,1:T(8,128)(2,1)} %param.25) | copy-start | bytes 36868
  876.9 221.3 %copy-start.75 = (s32[1182,2]{0,1:T(2,128)S(1)}, s32[1182,2]{0,1:T(2,128)}, u32[]{:S(2)}) copy-start(s32[1182,2]{0,1:T(2,128)} %param.17) | copy-start | bytes 28372
  876.9 222.2 %all-to-all-start.1 = ((bf16[16,440,768]{2,1,0:T(8,128)(2,1)}), bf16[16,440,768]{2,1,0:T(8,128)(2,1)}, u32[]{:S(2)}, u32[]{:S(2)}) async-start(bf16[16,440,768]{2,1,0:T(8,128)(2,1)} %copy.243), calls=%async_computation.2 | async-start | bytes 21626880 | tf_op jit(solution)/shard_map/all_to_all | solution.py:44
  882.7 750.0 %reduce-scatter.16.cloned.1.call-start = ((), (), s32[]{:S(2)}) async-start(), calls=%async_computation.16 | async-start | bytes 16220160 | tf_op jit(solution)/shard_map/reduce_scatter | solution.py:40
  1096.2 34.9 %copy-start.112 = (pred[2,1182]{1,0:T(4,128)(4,1)}, pred[2,1182]{1,0:T(4,128)(4,1)S(1)}, u32[]{:S(2)}) copy-start(pred[2,1182]{1,0:T(4,128)(4,1)S(1)} %lt.56) | copy-start | bytes 7096
  1098.3 11.8 copy-start.55
  1098.3 11.8 copy-start.60
  1178.7 279.8 %copy-start.139 = (bf16[1,768,768]{2,1,0:T(8,128)(2,1)S(1)}, bf16[1,768,768]{2,1,0:T(8,128)(2,1)}, u32[]{:S(2)}) copy-start(bf16[1,768,768]{2,1,0:T(8,128)(2,1)} %param.27) | copy-start | bytes 3538948
  1458.5 28.1 copy-start.31
  1507.7 259.8 %all-gather.5.cloned.1.call-start = ((), (), s32[]{:S(2)}) async-start(), calls=%async_computation.17 | async-start | bytes 16220160 | tf_op jit(solution)/shard_map/all_gather | solution.py:43
  1779.9 198.7 %all-to-all-start.3 = ((bf16[16,440,768]{2,1,0:T(8,128)(2,1)}), bf16[16,440,768]{2,1,0:T(8,128)(2,1)}, u32[]{:S(2)}, u32[]{:S(2)}) async-start(bf16[16,440,768]{2,1,0:T(8,128)(2,1)} %copy.247), calls=%async_computation.5 | async-start | bytes 21626880 | tf_op jit(solution)/shard_map/all_to_all | solution.py:44
  1785.7 391.1 %all-reduce.19.cloned.1.call-start = ((), (), s32[]{:S(2)}) async-start(), calls=%async_computation.18 | async-start | bytes 3637248 | tf_op jit(solution)/shard_map/psum | solution.py:30
  1785.9 228.6 %copy-start.68 = (bf16[1182,8]{0,1:T(8,128)(2,1)}, bf16[1182,8]{0,1:T(8,128)(2,1)S(1)}, u32[]{:S(2)}) copy-start(bf16[1182,8]{0,1:T(8,128)(2,1)S(1)} %select_reduce_fusion.1) | copy-start | bytes 56740
  2031.1 13.9 slice-start.2
  2073.6 103.2 %copy-start.67 = (f32[1182]{0:T(1024)S(1)}, f32[1182]{0:T(1024)}, u32[]{:S(2)}) copy-start(f32[1182]{0:T(1024)} %copy-done.66) | copy-start | bytes 14188
  2073.6 103.2 %copy-start.108 = (f32[768]{0:T(1024)S(1)}, f32[768]{0:T(1024)}, u32[]{:S(2)}) copy-start(f32[768]{0:T(1024)} %get-tuple-element.136) | copy-start | bytes 9220
  2079.2 102.2 %copy-start.82 = (f32[1182]{0:T(1024)S(1)}, f32[1182]{0:T(1024)}, u32[]{:S(2)}) copy-start(f32[1182]{0:T(1024)} %copy-done.81) | copy-start | bytes 14188
  2079.2 102.2 %copy-start.95 = (f32[1182]{0:T(1024)S(1)}, f32[1182]{0:T(1024)}, u32[]{:S(2)}) copy-start(f32[1182]{0:T(1024)} %copy-done.94) | copy-start | bytes 14188
  2079.2 177.0 %all-reduce.21.cloned.1.call-start = ((), (), s32[]{:S(2)}) async-start(), calls=%async_computation.19 | async-start | bytes 3637248 | tf_op jit(solution)/shard_map/psum | solution.py:30
  2186.2 8.8 copy-start.137
  2195.0 61.2 %copy-start.65 = (f32[1182]{0:T(1024)S(1)}, f32[1182]{0:T(1024)}, u32[]{:S(2)}) copy-start(f32[1182]{0:T(1024)} %copy-done.64) | copy-start | bytes 14188
  2195.0 61.2 %copy-start.105 = (f32[768]{0:T(1024)S(1)}, f32[768]{0:T(1024)}, u32[]{:S(2)}) copy-start(f32[768]{0:T(1024)} %copy-done.104) | copy-start | bytes 9220
  2199.2 61.8 %copy-start.80 = (f32[1182]{0:T(1024)S(1)}, f32[1182]{0:T(1024)}, u32[]{:S(2)}) copy-start(f32[1182]{0:T(1024)} %copy-done.79) | copy-start | bytes 14188
  2199.2 61.8 %copy-start.92 = (f32[1182]{0:T(1024)S(1)}, f32[1182]{0:T(1024)}, u32[]{:S(2)}) copy-start(f32[1182]{0:T(1024)} %copy-done.91) | copy-start | bytes 14188
  2199.2 184.3 %all-reduce.23.cloned.1.call-start = ((), (), s32[]{:S(2)}) async-start(), calls=%async_computation.20 | async-start | bytes 3637248 | tf_op jit(solution)/shard_map/psum | solution.py:30
  2278.4 13.7 slice-start
  2326.5 116.7 %reduce-scatter.26.cloned.1.call-start = ((), (), s32[]{:S(2)}) async-start(), calls=%async_computation.25 | async-start | bytes 417792
  2329.5 179.3 %reduce-scatter.24.cloned.1.call-start = ((), (), s32[]{:S(2)}) async-start(), calls=%async_computation.24 | async-start | bytes 417792
  2393.0 167.2 %reduce-scatter.22.cloned.1.call-start = ((), (), s32[]{:S(2)}) async-start(), calls=%async_computation.23 | async-start | bytes 417792
  2396.1 352.4 %all-reduce.25.cloned.1.call-start = ((), (), s32[]{:S(2)}) async-start(), calls=%async_computation.26 | async-start | bytes 18874368
  2418.0 410.5 %reduce-scatter.18.cloned.1.call-start = ((), (), s32[]{:S(2)}) async-start(), calls=%async_computation.21 | async-start | bytes 5013504 | tf_op jit(solution)/shard_map/reduce_scatter | solution.py:256
  2427.5 480.3 %reduce-scatter.20.cloned.1.call-start = ((), (), s32[]{:S(2)}) async-start(), calls=%async_computation.22 | async-start | bytes 5013504 | tf_op jit(solution)/shard_map/reduce_scatter | solution.py:257
  2459.2 14.7 copy-start.118
  2459.2 44.9 %copy-start.114 = (f32[1182]{0:T(1024)S(1)}, f32[1182]{0:T(1024)}, u32[]{:S(2)}) copy-start(f32[1182]{0:T(1024)} %get-tuple-element.79) | copy-start | bytes 14188
  2459.2 44.9 %copy-start.86 = (f32[1182]{0:T(1024)S(1)}, f32[1182]{0:T(1024)}, u32[]{:S(2)}) copy-start(f32[1182]{0:T(1024)} %copy-done.85) | copy-start | bytes 14188
  2459.2 44.9 %copy-start.90 = (f32[1182]{0:T(1024)S(1)}, f32[1182]{0:T(1024)}, u32[]{:S(2)}) copy-start(f32[1182]{0:T(1024)} %copy-done.87) | copy-start | bytes 14188
  2459.2 44.9 %copy-start.103 = (f32[768]{0:T(1024)S(1)}, f32[768]{0:T(1024)}, u32[]{:S(2)}) copy-start(f32[768]{0:T(1024)} %copy-done.100) | copy-start | bytes 9220
  (121 other events, 464.6 us)
Sparse Core Ops, SparseCore 0:
  57.3 59.5 all-reduce.12
  133.3 56.8 all-reduce.14
  239.3 56.8 all-reduce.16
  605.3 124.8 reduce-scatter.13
  731.7 133.0 all-gather.2
  1507.8 124.8 reduce-scatter.15
  1634.2 133.1 all-gather.4
  2079.3 97.4 all-reduce.18
  2199.3 56.8 all-reduce.20
  2326.6 56.8 all-reduce.22
  2387.6 55.5 reduce-scatter.25
  2446.9 54.6 reduce-scatter.23
  2505.7 54.5 reduce-scatter.21
  2564.3 184.1 all-reduce.24
  2752.8 75.6 reduce-scatter.17
  2833.2 74.5 reduce-scatter.19
where the time goes:
time: 2920 us; the launch traced here: 2910 us
  waiting for transfers between devices  1450 us (50%)
  blocking collectives  761 us (26%)
  local copies, waits for them, and re-layouts  324 us (11%)
  matrix products  221 us (8%)
  other arithmetic  123 us (4%)
    all_to_all x2, blocking collectives, to_experts(): lax.all_to_all(doubled, 'expert', split_axis=0, concat_axis=0, tiled=True)  520 us
    psum x6, waiting for transfers between devices, tensor_total(): lax.psum(partial_value.astype(jnp.bfloat16), 'tensor').astype(jnp.float32)  346 us
    all_gather x2, waiting for transfers between devices, from_experts(): full_rows = lax.all_gather(share_rows, 'tensor', axis=1, tiled=True)  269 us
    reduce_scatter x2, waiting for transfers between devices, from_experts(): lax.psum_scatter(partial_value.astype(jnp.bfloat16), 'tensor', scatter_di...  250 us
    unnamed x20, waiting for transfers between devices  241 us
    psum x1, blocking collectives, body(): valid_count = lax.psum(local_count, 'expert')  211 us
    all_to_all x2, waiting for transfers between devices, from_experts(): lax.all_to_all(full_rows, 'expert', split_axis=0, concat_axis=0, tiled=True)  193 us
    reduce_scatter x1, waiting for transfers between devices, body(): lax.psum_scatter(grad_mlp_out, 'expert', scatter_dimension=1, tiled=True)  79.4 us
  transfers between devices with their start and end apart: 18, of which 16 were waited for; matrix products, arithmetic and copies ran while one was open for 5% of the time, Pallas kernels for 0%

commit v1 on v0

v1 whole, which is shorter than its diff:
```python
import jax
import jax.numpy as jnp
from jax import lax
from jax.sharding import PartitionSpec as P

HD = 64
SEQ = 197
ROWS = 208
EPS = 1e-06
BF = jnp.bfloat16
F32 = jnp.float32


def mm(a, b, dims):
    return lax.dot_general(a, b, (dims, ((), ())), preferred_element_type=F32)


NN = ((1,), (0,))
NT = ((1,), (1,))
TN = ((0,), (0,))


def swap(value, axis, distance):
    size = lax.axis_size(axis)
    return lax.ppermute(value, axis, [(k, k ^ distance) for k in range(size)])


def normalize(values, gain_row, bias_row):
    center = values - jnp.mean(values, axis=-1, keepdims=True)
    scaled = center * lax.rsqrt(jnp.mean(center * center, axis=-1, keepdims=True) + EPS)
    return scaled * gain_row + bias_row


def norm_backward(values, gain_row, bias_row, grad_normed):
    pull_back = jax.vjp(normalize, values, gain_row, bias_row)[1]
    return pull_back(grad_normed)


def gelu_both(x):
    k = 0.7978845608028654
    a = 0.044715
    th = jnp.tanh(k * (x + a * x * x * x))
    half = 0.5 * (1.0 + th)
    return x * half, half + 0.5 * x * (1.0 - th * th) * k * (1.0 + 3.0 * a * x * x)


def heads_of(rows, images):
    return rows.reshape(images, ROWS, -1, HD)


def attend_forward(normed, qkv, out, images):
    packed = [mm(normed, w, NN).astype(BF) for w in qkv]
    q, k, v = (heads_of(p, images) for p in packed)
    scores = jnp.einsum("bqhe,bkhe->bhqk", q, k, preferred_element_type=F32) * HD ** (-0.5)
    keys = lax.broadcasted_iota(jnp.int32, scores.shape, 3)
    scores = jnp.where(keys < SEQ, scores, -1e30)
    total = jax.nn.logsumexp(scores, axis=-1, keepdims=True)
    probs = jnp.exp(scores - total).astype(BF)
    mixed = jnp.einsum("bhqk,bkhe->bqhe", probs, v, preferred_element_type=F32)
    mixed = mixed.reshape(normed.shape[0], -1).astype(BF)
    return mm(mixed, out, NN), (packed, total, mixed)


def attend_backward(grad_low, out, qkv, kept, images):
    packed, total, mixed = kept
    q, k, v = (heads_of(p, images) for p in packed)
    grad_mixed = heads_of(mm(grad_low, out, NT).astype(BF), images)
    scores = jnp.einsum("bqhe,bkhe->bhqk", q, k, preferred_element_type=F32) * HD ** (-0.5)
    keys = lax.broadcasted_iota(jnp.int32, scores.shape, 3)
    probs = jnp.where(keys < SEQ, jnp.exp(scores - total), 0.0)
    grad_probs = jnp.einsum("bqhe,bkhe->bhqk", grad_mixed, v, preferred_element_type=F32)
    inner = jnp.sum(grad_probs * probs, axis=-1, keepdims=True)
    grad_scores = (probs * (grad_probs - inner)).astype(BF)
    scale = HD ** (-0.5)
    gq = jnp.einsum("bhqk,bkhe->bqhe", grad_scores, k, preferred_element_type=F32) * scale
    gk = jnp.einsum("bhqk,bqhe->bkhe", grad_scores, q, preferred_element_type=F32) * scale
    gv = jnp.einsum("bhqk,bqhe->bkhe", probs.astype(BF), grad_mixed, preferred_element_type=F32)
    grads = [g.reshape(grad_low.shape[0], -1).astype(BF) for g in (gq, gk, gv)]
    grad_normed = sum(mm(g, w, NT) for g, w in zip(grads, qkv))
    return grad_normed, grads


def body(
    tokens,
    teacher,
    valid_flags,
    routes,
    capacity,
    norm_gains,
    norm_biases,
    attn_qkv,
    attn_out,
    mlp_in,
    mlp_out,
    router,
    expert_in,
    expert_out,
):
    owners = lax.axis_size("expert")
    groups = lax.axis_size("tensor")
    place = lax.axis_index("expert")
    group = lax.axis_index("tensor")
    core = place % 2
    local_rows, width = tokens.shape
    experts = router.shape[1]
    image_count = local_rows // SEQ
    images = -(-image_count // groups)
    own_rows = images * ROWS
    all_rows = groups * own_rows
    capacity_most = 4 * (3 * local_rows // (4 * experts))
    part = -(-capacity_most // (2 * groups))
    part = -(-part // 16) * 16
    slots = owners * part
    gains = norm_gains.astype(F32)
    biases = norm_biases.astype(F32)

    def relative(rows, fill, count):
        shape = rows.shape[1:]
        grid = rows.reshape((image_count, SEQ) + shape)
        grid = jnp.pad(
            grid,
            [(0, groups * images - image_count), (0, ROWS - SEQ)] + [(0, 0)] * len(shape),
            constant_values=fill,
        )
        taken = [
            lax.dynamic_slice_in_dim(grid, (group ^ d) * images, images, 0) for d in range(count)
        ]
        return jnp.concatenate(taken, 0).reshape((count * own_rows,) + shape)

    def absolute(rows):
        shape = rows.shape[1:]
        grid = rows.reshape((groups * images, ROWS) + shape)
        taken = [
            lax.dynamic_slice_in_dim(grid, (group ^ d) * images, images, 0) for d in range(groups)
        ]
        grid = jnp.concatenate(taken, 0)[:image_count, :SEQ]
        return grid.reshape((local_rows,) + shape)

    count = jnp.full((8, 128), SEQ * jnp.sum(valid_flags.astype(F32)), F32)
    step = 1
    while step < owners:
        count = count + swap(count, "expert", step)
        step *= 2
    valid_count = count[0, 0]

    order = [None]

    def chained(value):
        if order[0] is not None:
            value, _ = lax.optimization_barrier((value, order[0]))
        return value

    def gather_dense(weight):
        rows = weight.shape[0] // 2
        mine = lax.dynamic_slice_in_dim(weight, core * rows, rows, 0)
        out = [weight]
        for d in range(1, groups):
            first = swap(chained(mine), "tensor", d)
            order[0] = first
            other = swap(first, "expert", 1)
            low = jnp.where(core == 0, first, other)
            high = jnp.where(core == 0, other, first)
            out.append(jnp.concatenate([low, high], 0))
        return out

    def gather_expert(weight):
        out = [weight]
        for d in range(1, groups):
            first = swap(chained(weight), "tensor", d)
            order[0] = first
            out.append(first)
        return out + [swap(w, "expert", 1) for w in out]

    def gather_qkv(weight):
        parts = gather_dense(weight.reshape(3 * width, -1))
        parts = [p.reshape(3, width, -1) for p in parts]
        return [jnp.concatenate([p[s] for p in parts], 1) for s in range(3)]

    qkv_first = gather_qkv(attn_qkv[0])
    out_first = jnp.concatenate(gather_dense(attn_out[0]), 0)
    dense_in = gather_dense(mlp_in)
    dense_out = gather_dense(mlp_out)
    qkv_second = gather_qkv(attn_qkv[1])
    out_second = jnp.concatenate(gather_dense(attn_out[1]), 0)
    whole_in = gather_expert(expert_in[0])
    whole_out = gather_expert(expert_out[0])

    expert_of = jnp.concatenate([routes[:, 0], routes[:, 1]])
    onehot = (expert_of[:, None] == jnp.arange(experts, dtype=jnp.int32)[None, :]).astype(jnp.int32)
    earlier = jnp.cumsum(onehot, axis=0) - onehot
    position = jnp.sum(earlier * onehot, axis=1)
    kept_mask = position < jnp.sum(onehot * capacity[None, :], axis=1)
    quarter = position // part
    row_of = (2 * expert_of + quarter % 2) * part + position % part
    row_of = jnp.where(kept_mask & (quarter // 2 == group), row_of, -1)
    row_of = relative(row_of.reshape(2, local_rows).T, -1, groups)
    routes_rel = relative(routes, 0, groups)
    valid_rows = relative(jnp.repeat(valid_flags.astype(F32), SEQ)[:, None], 0, groups)

    start = relative(tokens, 0, 1).astype(F32)
    normed_first = normalize(start, gains[0], biases[0]).astype(BF)
    branch, saved_first = attend_forward(normed_first, qkv_first, out_first, images)
    after_attn = start + branch
    normed_dense = normalize(after_attn, gains[1], biases[1]).astype(BF)
    dense_pairs = [gelu_both(mm(normed_dense, w, NN)) for w in dense_in]
    dense_act = [a.astype(BF) for a, _ in dense_pairs]
    dense_slope = [b.astype(BF) for _, b in dense_pairs]
    after_dense = after_attn + sum(mm(a, w, NN) for a, w in zip(dense_act, dense_out))
    normed_second = normalize(after_dense, gains[2], biases[2]).astype(BF)
    branch, saved_second = attend_forward(normed_second, qkv_second, out_second, images)
    after_second = after_dense + branch
    normed_expert = normalize(after_second, gains[3], biases[3]).astype(BF)
    normed_all = jnp.concatenate(
        [normed_expert] + [swap(normed_expert, "tensor", d) for d in range(1, groups)], 0
    )

    logits = mm(normed_all, router, NN)
    picker = routes_rel[:, :, None] == jnp.arange(experts, dtype=jnp.int32)[None, None, :]
    chosen = jnp.sum(jnp.where(picker, logits[:, None, :], 0.0), axis=2)
    gate_vals = jax.nn.softmax(chosen, axis=1)

    slot_ids = jnp.arange(slots, dtype=jnp.int32)
    take_first = slot_ids[:, None] == row_of[None, :, 0]
    take_second = slot_ids[:, None] == row_of[None, :, 1]
    take = (take_first | take_second).astype(BF)

    def across(rows):
        return lax.all_to_all(
            rows.reshape(owners, part, width), "expert", split_axis=0, concat_axis=0, tiled=True
        ).reshape(slots, width)

    rows_in = across(mm(take, normed_all, NN).astype(BF))
    pairs = [gelu_both(mm(rows_in, w, NN)) for w in whole_in]
    act = [a.astype(BF) for a, _ in pairs]
    slope = [b.astype(BF) for _, b in pairs]
    merged = across(sum(mm(a, w, NN) for a, w in zip(act, whole_out)).astype(BF))

    weights = jnp.where(take_first, gate_vals[None, :, 0], 0.0) + jnp.where(
        take_second, gate_vals[None, :, 1], 0.0
    )
    weights = weights.astype(BF)
    combined = mm(weights, merged, TN)
    final = after_second + combined[:own_rows]
    for d in range(1, groups):
        sent = combined[d * own_rows : (d + 1) * own_rows].astype(BF)
        final = final + swap(sent, "tensor", d).astype(F32)
    final_low = final.astype(BF)
    final_all = jnp.concatenate(
        [final_low] + [swap(final_low, "tensor", d) for d in range(1, groups)], 0
    )
    activations = absolute(final_all)
    teacher_rel = relative(teacher, 0, groups).astype(F32)
    scale = (local_rows * owners / valid_count) * valid_rows
    grad_final = scale[:own_rows] * (final - teacher_rel[:own_rows])
    grad_all = scale * (final_all.astype(F32) - teacher_rel)
    grad_all = jnp.concatenate([grad_final, grad_all[own_rows:]], 0).astype(BF)

    taken = mm(take, grad_all, NN)
    gate_of_slot = jnp.sum(
        jnp.where(take_first, gate_vals[None, :, 0], 0.0)
        + jnp.where(take_second, gate_vals[None, :, 1], 0.0),
        axis=1,
        keepdims=True,
    )
    grad_slot_gate = jnp.sum(taken * merged.astype(F32), axis=1, keepdims=True)
    grad_out_rows = across((gate_of_slot * taken).astype(BF))
    grad_gates = jnp.stack(
        [
            jnp.sum(jnp.where(take_first, grad_slot_gate, 0.0), axis=0),
            jnp.sum(jnp.where(take_second, grad_slot_gate, 0.0), axis=0),
        ],
        0,
    )
    grad_own = grad_gates[:, :own_rows]
    for d in range(1, groups):
        grad_own = grad_own + swap(
            grad_gates[:, d * own_rows : (d + 1) * own_rows], "tensor", d
        )
    grad_own = grad_own.T
    grad_hidden = [
        (mm(grad_out_rows, w, NT) * s.astype(F32)).astype(BF) for w, s in zip(whole_out, slope)
    ]
    grad_rows = sum(mm(g, w, NT) for g, w in zip(grad_hidden, whole_in)).astype(BF)
    grad_back = across(grad_rows)

    def share_expert(parts):
        kept = []
        for d in range(groups):
            got = swap(parts[groups + d].astype(BF), "expert", 1)
            kept.append(parts[d] + got.astype(F32))
        total = kept[0]
        for d in range(1, groups):
            total = total + swap(kept[d].astype(BF), "tensor", d).astype(F32)
        return total

    grad_expert_out = share_expert([mm(a, grad_out_rows, TN) for a in act])
    grad_expert_in = share_expert([mm(rows_in, g, TN) for g in grad_hidden])

    own_gates = gate_vals[:own_rows]
    grad_chosen = own_gates * (grad_own - jnp.sum(own_gates * grad_own, axis=1, keepdims=True))
    grad_logits = jnp.sum(
        jnp.where(picker[:own_rows], grad_chosen[:, :, None], 0.0), axis=1
    ).astype(BF)
    grad_router = mm(grad_logits, normed_expert, TN)
    returned = mm(take, grad_back, TN)
    grad_normed = returned[:own_rows] + mm(grad_logits, router, NT)
    for d in range(1, groups):
        sent = returned[d * own_rows : (d + 1) * own_rows].astype(BF)
        grad_normed = grad_normed + swap(sent, "tensor", d).astype(F32)
    back, gain_four, bias_four = norm_backward(after_second, gains[3], biases[3], grad_normed)
    grad_second = grad_final + back

    block = width // owners
    feature = jnp.arange(width, dtype=jnp.int32)
    ahead, turned, step = feature // block, 0, 1
    while step < owners:
        turned = turned * 2 + ahead % 2
        ahead = ahead // 2
        step *= 2
    source = (turned ^ place) * block + feature % block
    mover = (feature[:, None] == source[None, :]).astype(BF)

    def moved(rows):
        return mm(rows, mover, NN).astype(BF)

    def share_dense(parts):
        rows = width // 2
        kept = []
        for d in range(groups):
            got = swap(parts[d][rows:].astype(BF), "expert", 1)
            kept.append(parts[d][:rows] + got.astype(F32))
        total = kept[0]
        for d in range(1, groups):
            total = total + swap(kept[d].astype(BF), "tensor", d).astype(F32)
        step = 2
        while step < owners:
            rows //= 2
            got = swap(total[rows:].astype(BF), "expert", step)
            total = total[:rows] + got.astype(F32)
            step *= 2
        return total

    def column_groups(rows):
        span = rows.shape[1] // groups
        return [rows[:, d * span : (d + 1) * span] for d in range(groups)]

    def attention_grads(grad_low, normed, mixed, grads):
        low_moved = moved(grad_low)
        normed_moved = moved(normed)
        out_part = share_dense([mm(low_moved, m, TN) for m in column_groups(mixed)])
        split = [column_groups(g) for g in grads]
        qkv_part = share_dense(
            [
                mm(normed_moved, jnp.concatenate([s[d] for s in split], 1), TN)
                for d in range(groups)
            ]
        )
        span = qkv_part.shape[1] // 3
        qkv_grad = jnp.stack([qkv_part[:, s * span : (s + 1) * span] for s in range(3)])
        return qkv_grad, out_part.T

    grad_low = grad_second.astype(BF)
    grad_part, grads = attend_backward(grad_low, out_second, qkv_second, saved_second, images)
    qkv_two, out_two = attention_grads(grad_low, normed_second, saved_second[2], grads)
    back, gain_three, bias_three = norm_backward(after_dense, gains[2], biases[2], grad_part)
    grad_dense = grad_second + back
    grad_low = grad_dense.astype(BF)
    grad_hid = [
        (mm(grad_low, w, NT) * s.astype(F32)).astype(BF) for w, s in zip(dense_out, dense_slope)
    ]
    grad_part = sum(mm(g, w, NT) for g, w in zip(grad_hid, dense_in))
    low_moved = moved(grad_low)
    normed_moved = moved(normed_dense)
    grad_mlp_out = share_dense([mm(low_moved, a, TN) for a in dense_act]).T
    grad_mlp_in = share_dense([mm(normed_moved, g, TN) for g in grad_hid])
    back, gain_two, bias_two = norm_backward(after_attn, gains[1], biases[1], grad_part)
    grad_attn = grad_dense + back
    grad_low = grad_attn.astype(BF)
    grad_part, grads = attend_backward(grad_low, out_first, qkv_first, saved_first, images)
    back, gain_one, bias_one = norm_backward(start, gains[0], biases[0], grad_part)
    grad_start = (grad_attn + back).astype(BF)
    start_all = jnp.concatenate(
        [grad_start] + [swap(grad_start, "tensor", d) for d in range(1, groups)], 0
    )
    input_grad = absolute(start_all)
    qkv_one, out_one = attention_grads(grad_low, normed_first, saved_first[2], grads)

    small = jnp.concatenate(
        [
            jnp.stack([gain_one, gain_two, gain_three, gain_four]),
            jnp.stack([bias_one, bias_two, bias_three, bias_four]),
            grad_router,
        ],
        0,
    )
    small = lax.psum_scatter(
        lax.psum(small, "tensor"), "expert", scatter_dimension=1, tiled=True
    )
    return (
        activations,
        input_grad,
        small[:4],
        small[4:7],
        small[7],
        jnp.stack([qkv_one, qkv_two]),
        jnp.stack([out_one, out_two]),
        grad_mlp_in,
        grad_mlp_out,
        small[8:].T,
        grad_expert_in[None],
        grad_expert_out[None],
    )


def solution(mesh):
    in_specs = (
        P("expert", None),
        P("expert", None),
        P("expert"),
        P("expert", None),
        P(),
        P(),
        P(),
        P(None, None, None, "tensor"),
        P(None, "tensor", None),
        P(None, "tensor"),
        P("tensor", None),
        P(),
        P("expert", None, "tensor"),
        P("expert", "tensor", None),
    )
    out_specs = (
        P("expert", None),
        P("expert", None),
        P(None, "expert"),
        P(None, "expert"),
        P("expert"),
        P(None, None, "expert", "tensor"),
        P(None, "tensor", "expert"),
        P("expert", "tensor"),
        P("tensor", "expert"),
        P("expert", None),
        P("expert", None, "tensor"),
        P("expert", "tensor", None),
    )
    return jax.shard_map(body, mesh=mesh, in_specs=in_specs, out_specs=out_specs, check_vma=False)
```

time: 2920 us -> 1230 us (0.42)
  waiting for transfers between devices: 1450 us -> 471 us
  blocking collectives: 761 us -> 5.16 us
  local copies, waits for them, and re-layouts: 324 us -> 203 us
  starting transfers between devices: 12.7 us -> 115 us
  matrix products: 221 us -> 315 us
    all_to_all x2 -> x0, blocking collectives: 520 us -> none  [to_experts(): lax.all_to_all(doubled, 'expert', split_axis=0, concat_axis=0, tiled=True)]
    reduce_scatter x4 -> x0, waiting for transfers between devices: 406 us -> none  [the longest x2 250 us: from_experts(): lax.psum_scatter(partial_value.astype(jnp.bfloat16), 'tensor', scatter_di...]
    ppermute x0 -> x70, waiting for transfers between devices: none -> 349 us  [swap(): return lax.ppermute(value, axis, [(k, k ^ distance) for k in range(size)])]
    psum x6 -> x0, waiting for transfers between devices: 346 us -> none  [tensor_total(): lax.psum(partial_value.astype(jnp.bfloat16), 'tensor').astype(jnp.float32)]
    all_gather x2 -> x0, waiting for transfers between devices: 269 us -> none  [from_experts(): full_rows = lax.all_gather(share_rows, 'tensor', axis=1, tiled=True)]
    unnamed x20 -> x2, waiting for transfers between devices: 241 us -> 31.5 us
    psum x1, blocking collectives: 211 us -> 5.16 us  [body(): lax.psum(small, 'tensor')]
    all_to_all x2 -> x4, waiting for transfers between devices: 193 us -> 90.6 us  [across(): lax.all_to_all(rows.reshape(owners, part, width), 'expert', split_axis=0,...]
  transfers between devices with their start and end apart: 18 -> 75, of which waited for: 16 -> 41; matrix products, arithmetic and copies ran while one was open for 5% -> 20% of each run, Pallas kernels for 0% -> 0%
where the time goes in v1:
time: 1230 us; the launch traced here: 1220 us
  waiting for transfers between devices  471 us (38%)
  matrix products  315 us (26%)
  local copies, waits for them, and re-layouts  203 us (17%)
  starting transfers between devices  115 us (9%)
  other arithmetic  94.8 us (8%)
  between operations  18.9 us (2%)
    ppermute x70, waiting for transfers between devices, swap(): return lax.ppermute(value, axis, [(k, k ^ distance) for k in range(size)])  349 us
    dot_general x73, matrix products, mm(): return lax.dot_general(a, b, (dims, ((), ())), preferred_element_type=F32)  274 us
    all_to_all x4, waiting for transfers between devices, across(): lax.all_to_all(rows.reshape(owners, part, width), 'expert', split_axis=0,...  90.6 us
    ppermute x70, starting transfers between devices, swap(): return lax.ppermute(value, axis, [(k, k ^ distance) for k in range(size)])  71.6 us
    reshape x16, local copies, waits for them, and re-layouts, heads_of(): return rows.reshape(images, ROWS, -1, HD)  57.9 us
    all_to_all x4, starting transfers between devices, across(): lax.all_to_all(rows.reshape(owners, part, width), 'expert', split_axis=0,...  42.7 us
    convert_element_type x12, local copies, waits for them, and re-layouts, attend_backward(): grads = [g.reshape(grad_low.shape[0], -1).astype(BF) for g in (gq, gk, gv)]  32.5 us
    unnamed x2, waiting for transfers between devices  31.5 us
  transfers between devices with their start and end apart: 75, of which 41 were waited for; matrix products, arithmetic and copies ran while one was open for 20% of the time, Pallas kernels for 0%

profile of v1, /device:TPU:0, one launch (start us, length us, event | category | flops | bytes accessed | tf_op | source)
XLA Modules:
  0.0 1222.4 jit_solution(13422210858680898634)
XLA Ops:
  19.2 17.4 %collective-permute-done = bf16[1152,384]{1,0:T(8,128)(2,1)} collective-permute-done((bf16[1152,384]{1,0:T(8,128)(2,1)}, bf16[1152,384]{1,0:T(8,128)(2,1)}, u32[]{:S(2)}, u32[]{:S(2)}) %collective-permute-start) | collective-permute-done | bytes 884768 | tf_op jit(solution)/shard_map/ppermute | solution.py:25
  57.2 14.1 %collective-permute-done.4 = bf16[384,1536]{1,0:T(8,128)(2,1)} collective-permute-done((bf16[384,1536]{1,0:T(8,128)(2,1)}, bf16[384,1536]{1,0:T(8,128)(2,1)}, u32[]{:S(2)}, u32[]{:S(2)}) %collective-permute-start.4) | collective-permute-done | bytes 1179680 | tf_op jit(solution)/shard_map/ppermute | solution.py:25
  84.1 13.6 %collective-permute-done.6 = bf16[768,768]{1,0:T(8,128)(2,1)S(1)} collective-permute-done((bf16[768,768]{1,0:T(8,128)(2,1)}, bf16[768,768]{1,0:T(8,128)(2,1)S(1)}, u32[]{:S(2)}, u32[]{:S(2)}) %collective-permute-start.6) | collective-permute-done | bytes 1179680 | tf_op jit(solution)/shard_map/ppermute | solution.py:25
  104.7 12.8 %collective-permute-done.8 = bf16[1152,384]{1,0:T(8,128)(2,1)S(1)} collective-permute-done((bf16[1152,384]{1,0:T(8,128)(2,1)S(1)}, bf16[1152,384]{1,0:T(8,128)(2,1)S(1)}, u32[]{:S(2)}, u32[]{:S(2)}) %collective-permute-start.8) | collective-permute-done | bytes 884768 | tf_op jit(solution)/shard_map/ppermute | solution.py:25
  246.1 22.0 %collective-permute-done.12 = bf16[624,768]{1,0:T(8,128)(2,1)} collective-permute-done((bf16[624,768]{1,0:T(8,128)(2,1)S(1)}, bf16[624,768]{1,0:T(8,128)(2,1)}, u32[]{:S(2)}, u32[]{:S(2)}) %collective-permute-start.12) | collective-permute-done | bytes 958496 | tf_op jit(solution)/shard_map/ppermute | solution.py:25
  268.1 7.3 fusion.84
  275.4 6.0 all-to-all-start
  283.0 27.0 %collective-permute-done.13 = bf16[768,768]{1,0:T(8,128)(2,1)} collective-permute-done((bf16[768,768]{1,0:T(8,128)(2,1)}, bf16[768,768]{1,0:T(8,128)(2,1)}, u32[]{:S(2)}, u32[]{:S(2)}) %collective-permute-start.13) | collective-permute-done | bytes 1179680 | tf_op jit(solution)/shard_map/ppermute | solution.py:25
  312.0 25.7 %collective-permute-done.14 = bf16[768,768]{1,0:T(8,128)(2,1)} collective-permute-done((bf16[768,768]{1,0:T(8,128)(2,1)}, bf16[768,768]{1,0:T(8,128)(2,1)}, u32[]{:S(2)}, u32[]{:S(2)}) %collective-permute-start.14) | collective-permute-done | bytes 1179680 | tf_op jit(solution)/shard_map/ppermute | solution.py:25
  350.3 5.6 fusion.289
  360.5 6.4 fusion.307
  367.0 7.2 fusion.286
  374.2 7.3 add_convert_fusion.1
  381.5 9.9 all-to-all-start.1
  398.4 45.5 %all-to-all-done.1 = bf16[16,112,768]{2,1,0:T(8,128)(2,1)} async-done(((bf16[16,112,768]{2,1,0:T(8,128)(2,1)}), bf16[16,112,768]{2,1,0:T(8,128)(2,1)}, u32[]{:S(2)}, u32[]{:S(2)}) %all-to-all-start.1) | async-done | bytes 2752544 | tf_op jit(solution)/shard_map/all_to_all | solution.py:228
  443.9 6.6 fusion.35
  458.9 7.9 collective-permute-start.23
  482.8 21.5 %collective-permute-done.20 = bf16[624,768]{1,0:T(8,128)(2,1)} collective-permute-done((bf16[624,768]{1,0:T(8,128)(2,1)S(1)}, bf16[624,768]{1,0:T(8,128)(2,1)}, u32[]{:S(2)}, u32[]{:S(2)}) %collective-permute-start.20) | collective-permute-done | bytes 958496 | tf_op jit(solution)/shard_map/ppermute | solution.py:25
  506.5 7.4 multiply_reduce_fusion.2
  513.9 6.2 select_reduce_fusion.1
  522.0 13.0 %all-to-all-start.2 = ((bf16[16,112,768]{2,1,0:T(8,128)(2,1)}), bf16[16,112,768]{2,1,0:T(8,128)(2,1)}, u32[]{:S(2)}, u32[]{:S(2)}) async-start(bf16[16,112,768]{2,1,0:T(8,128)(2,1)} %bitcast.269), calls=%async_computation.2 | async-start | bytes 5505024 | tf_op jit(solution)/shard_map/all_to_all | solution.py:228
  550.9 36.7 %all-to-all-done.2 = bf16[16,112,768]{2,1,0:T(8,128)(2,1)} async-done(((bf16[16,112,768]{2,1,0:T(8,128)(2,1)}), bf16[16,112,768]{2,1,0:T(8,128)(2,1)}, u32[]{:S(2)}, u32[]{:S(2)}) %all-to-all-start.2) | async-done | bytes 2752544 | tf_op jit(solution)/shard_map/all_to_all | solution.py:228
  587.6 7.3 multiply_convert_fusion.5
  597.3 7.3 multiply_convert_fusion.2
  604.7 7.7 multiply_convert_fusion.4
  612.4 7.3 multiply_convert_fusion.3
  628.0 5.7 add_convert_fusion
  633.7 13.9 %all-to-all-start.3 = ((bf16[16,112,768]{2,1,0:T(8,128)(2,1)}), bf16[16,112,768]{2,1,0:T(8,128)(2,1)}, u32[]{:S(2)}, u32[]{:S(2)}) async-start(bf16[16,112,768]{2,1,0:T(8,128)(2,1)} %bitcast.270), calls=%async_computation.3 | async-start | bytes 5505024 | tf_op jit(solution)/shard_map/all_to_all | solution.py:228
  648.0 6.4 convolution_convert_fusion
  659.4 7.4 convolution_convert_fusion.1
  666.8 5.9 fusion.287
  678.4 6.0 add_convert_fusion.2
  691.7 8.4 all-to-all-done.3
  700.1 6.6 fusion.29
  717.1 21.8 %collective-permute-done.66 = bf16[768,768]{1,0:T(8,128)(2,1)} collective-permute-done((bf16[768,768]{1,0:T(8,128)(2,1)}, bf16[768,768]{1,0:T(8,128)(2,1)}, u32[]{:S(2)}, u32[]{:S(2)}) %collective-permute-start.66) | collective-permute-done | bytes 1179680 | tf_op jit(solution)/shard_map/ppermute | solution.py:25
  742.0 16.8 %collective-permute-done.26 = bf16[624,768]{1,0:T(8,128)(2,1)S(1)} collective-permute-done((bf16[624,768]{1,0:T(8,128)(2,1)S(1)}, bf16[624,768]{1,0:T(8,128)(2,1)S(1)}, u32[]{:S(2)}, u32[]{:S(2)}) %collective-permute-start.26) | collective-permute-done | bytes 958496 | tf_op jit(solution)/shard_map/ppermute | solution.py:25
  772.8 6.6 multiply_reduce_fusion.1
  875.4 7.0 multiply_reduce_fusion
  972.6 31.4 %reduce-scatter.4.cloned.1.call-done = f32[48,16]{1,0:T(8,128)} async-done(((f32[768,16]{1,0:T(8,128)}), f32[48,16]{1,0:T(8,128)}) %reduce-scatter.4.cloned.1.call-update) | async-done | bytes 3088
  1057.7 19.6 %collective-permute-done.27 = bf16[624,768]{1,0:T(8,128)(2,1)S(1)} collective-permute-done((bf16[624,768]{1,0:T(8,128)(2,1)S(1)}, bf16[624,768]{1,0:T(8,128)(2,1)S(1)}, u32[]{:S(2)}, u32[]{:S(2)}) %collective-permute-start.27) | collective-permute-done | bytes 958496 | tf_op jit(solution)/shard_map/ppermute | solution.py:25
  1089.7 15.2 %collective-permute-done.30 = bf16[384,1152]{1,0:T(8,128)(2,1)S(1)} collective-permute-done((bf16[384,1152]{1,0:T(8,128)(2,1)S(1)}, bf16[384,1152]{1,0:T(8,128)(2,1)S(1)}, u32[]{:S(2)}, u32[]{:S(2)}) %collective-permute-start.30) | collective-permute-done | bytes 884768 | tf_op jit(solution)/shard_map/ppermute | solution.py:25
  1108.7 15.2 %collective-permute-done.36 = bf16[384,1152]{1,0:T(8,128)(2,1)S(1)} collective-permute-done((bf16[384,1152]{1,0:T(8,128)(2,1)S(1)}, bf16[384,1152]{1,0:T(8,128)(2,1)S(1)}, u32[]{:S(2)}, u32[]{:S(2)}) %collective-permute-start.36) | collective-permute-done | bytes 884768 | tf_op jit(solution)/shard_map/ppermute | solution.py:25
  1126.6 8.7 collective-permute-done.31
  1136.6 9.2 collective-permute-done.37
  1152.3 21.8 %collective-permute-done.54 = bf16[384,1536]{1,0:T(8,128)(2,1)S(1)} collective-permute-done((bf16[384,1536]{1,0:T(8,128)(2,1)S(1)}, bf16[384,1536]{1,0:T(8,128)(2,1)S(1)}, u32[]{:S(2)}, u32[]{:S(2)}) %collective-permute-start.54) | collective-permute-done | bytes 1179680 | tf_op jit(solution)/shard_map/ppermute | solution.py:25
  1179.0 8.0 collective-permute-done.33
  1191.8 7.7 collective-permute-done.62
  1200.1 6.3 collective-permute-done.56
  (879 shorter events, 591.2 us)
Async XLA Ops:
  13.7 22.9 %collective-permute-start = (bf16[1152,384]{1,0:T(8,128)(2,1)}, bf16[1152,384]{1,0:T(8,128)(2,1)}, u32[]{:S(2)}, u32[]{:S(2)}) collective-permute-start(bf16[1152,384]{1,0:T(8,128)(2,1)} %constant_dynamic-slice_fusion.7), channel_id=1, source_target_pairs={{0,1},{1,0},{2,3},{3,2},{4,5},{5,4},{6,7},{7,6},{8,9},{9,8},{10,11... | collective-permute-start | bytes 2654216 | tf_op jit(solution)/shard_map/ppermute | solution.py:25
  44.8 26.5 %collective-permute-start.4 = (bf16[384,1536]{1,0:T(8,128)(2,1)}, bf16[384,1536]{1,0:T(8,128)(2,1)}, u32[]{:S(2)}, u32[]{:S(2)}) collective-permute-start(bf16[384,1536]{1,0:T(8,128)(2,1)} %constant_dynamic-slice_fusion.6), channel_id=1, source_target_pairs={{0,1},{1,0},{2,3},{3,2},{4,5},{5,4},{6,7},{7,6},{8,9},{9,8},{10,11... | collective-permute-start | bytes 3538952 | tf_op jit(solution)/shard_map/ppermute | solution.py:25
  71.3 26.3 %collective-permute-start.6 = (bf16[768,768]{1,0:T(8,128)(2,1)}, bf16[768,768]{1,0:T(8,128)(2,1)S(1)}, u32[]{:S(2)}, u32[]{:S(2)}) collective-permute-start(bf16[768,768]{1,0:T(8,128)(2,1)} %constant_dynamic-slice_fusion.5), channel_id=1, source_target_pairs={{0,1},{1,0},{2,3},{3,2},{4,5},{5,4},{6,7},{7,6},{8,9},{9,8},{10,11... | collective-permute-start | bytes 3538952 | tf_op jit(solution)/shard_map/ppermute | solution.py:25
  74.1 44.5 %collective-permute-start.5 = (bf16[384,1536]{1,0:T(8,128)(2,1)}, bf16[384,1536]{1,0:T(8,128)(2,1)}, u32[]{:S(2)}, u32[]{:S(2)}) collective-permute-start(bf16[384,1536]{1,0:T(8,128)(2,1)} %collective-permute-done.4), channel_id=1, source_target_pairs={{0,2},{2,0},{4,6},{6,4},{8,10},{10,8},{12,14},{14,12},{16,18},{18,... | collective-permute-start | bytes 3538952 | tf_op jit(solution)/shard_map/ppermute | solution.py:25
  100.8 23.4 %collective-permute-start.7 = (bf16[768,768]{1,0:T(8,128)(2,1)S(1)}, bf16[768,768]{1,0:T(8,128)(2,1)S(1)}, u32[]{:S(2)}, u32[]{:S(2)}) collective-permute-start(bf16[768,768]{1,0:T(8,128)(2,1)S(1)} %collective-permute-done.6), channel_id=1, source_target_pairs={{0,2},{2,0},{4,6},{6,4},{8,10},{10,8},{12,14},{14,12},{16,18},{18,... | collective-permute-start | bytes 3538952 | tf_op jit(solution)/shard_map/ppermute | solution.py:25
  104.2 22.8 %collective-permute-start.1 = (bf16[1152,384]{1,0:T(8,128)(2,1)}, bf16[1152,384]{1,0:T(8,128)(2,1)S(1)}, u32[]{:S(2)}, u32[]{:S(2)}) collective-permute-start(bf16[1152,384]{1,0:T(8,128)(2,1)} %collective-permute-done), channel_id=1, source_target_pairs={{0,2},{2,0},{4,6},{6,4},{8,10},{10,8},{12,14},{14,12},{16,18},{18,... | collective-permute-start | bytes 2654216 | tf_op jit(solution)/shard_map/ppermute | solution.py:25
  104.2 21.7 %collective-permute-start.3 = (bf16[192,768]{1,0:T(8,128)(2,1)S(1)}, bf16[192,768]{1,0:T(8,128)(2,1)S(1)}, u32[]{:S(2)}, u32[]{:S(2)}) collective-permute-start(bf16[192,768]{1,0:T(8,128)(2,1)S(1)} %copy-done.112), channel_id=1, source_target_pairs={{0,2},{2,0},{4,6},{6,4},{8,10},{10,8},{12,14},{14,12},{16,18},{18,... | collective-permute-start | bytes 884744 | tf_op jit(solution)/shard_map/ppermute | solution.py:25
  244.4 23.7 %collective-permute-start.12 = (bf16[624,768]{1,0:T(8,128)(2,1)S(1)}, bf16[624,768]{1,0:T(8,128)(2,1)}, u32[]{:S(2)}, u32[]{:S(2)}) collective-permute-start(bf16[624,768]{1,0:T(8,128)(2,1)S(1)} %add_convert_fusion.5), channel_id=1, source_target_pairs={{0,1},{1,0},{2,3},{3,2},{4,5},{5,4},{6,7},{7,6},{8,9},{9,8},{10,11... | collective-permute-start | bytes 2875400 | tf_op jit(solution)/shard_map/ppermute | solution.py:25
  275.4 62.4 %all-to-all-start = ((bf16[16,112,768]{2,1,0:T(8,128)(2,1)}), bf16[16,112,768]{2,1,0:T(8,128)(2,1)}, u32[]{:S(2)}, u32[]{:S(2)}) async-start(bf16[16,112,768]{2,1,0:T(8,128)(2,1)} %bitcast.276), calls=%async_computation | async-start | bytes 5505024 | tf_op jit(solution)/shard_map/all_to_all | solution.py:228
  281.4 28.6 %collective-permute-start.13 = (bf16[768,768]{1,0:T(8,128)(2,1)}, bf16[768,768]{1,0:T(8,128)(2,1)}, u32[]{:S(2)}, u32[]{:S(2)}) collective-permute-start(bf16[768,768]{1,0:T(8,128)(2,1)} %bitcast.287), channel_id=1, source_target_pairs={{0,1},{1,0},{2,3},{3,2},{4,5},{5,4},{6,7},{7,6},{8,9},{9,8},{10,11... | collective-permute-start | bytes 3538952 | tf_op jit(solution)/shard_map/ppermute | solution.py:25
  310.0 27.7 %collective-permute-start.14 = (bf16[768,768]{1,0:T(8,128)(2,1)}, bf16[768,768]{1,0:T(8,128)(2,1)}, u32[]{:S(2)}, u32[]{:S(2)}) collective-permute-start(bf16[768,768]{1,0:T(8,128)(2,1)} %bitcast.285), channel_id=1, source_target_pairs={{0,1},{1,0},{2,3},{3,2},{4,5},{5,4},{6,7},{7,6},{8,9},{9,8},{10,11... | collective-permute-start | bytes 3538952 | tf_op jit(solution)/shard_map/ppermute | solution.py:25
  311.5 49.0 %collective-permute-start.15 = (bf16[768,768]{1,0:T(8,128)(2,1)}, bf16[768,768]{1,0:T(8,128)(2,1)}, u32[]{:S(2)}, u32[]{:S(2)}) collective-permute-start(bf16[768,768]{1,0:T(8,128)(2,1)} %bitcast.288), channel_id=1, source_target_pairs={{0,2},{2,0},{4,6},{6,4},{8,10},{10,8},{12,14},{14,12},{16,18},{18,... | collective-permute-start | bytes 3538952 | tf_op jit(solution)/shard_map/ppermute | solution.py:25
  311.5 55.5 %collective-permute-start.16 = (bf16[768,768]{1,0:T(8,128)(2,1)}, bf16[768,768]{1,0:T(8,128)(2,1)}, u32[]{:S(2)}, u32[]{:S(2)}) collective-permute-start(bf16[768,768]{1,0:T(8,128)(2,1)} %bitcast.286), channel_id=1, source_target_pairs={{0,2},{2,0},{4,6},{6,4},{8,10},{10,8},{12,14},{14,12},{16,18},{18,... | collective-permute-start | bytes 3538952 | tf_op jit(solution)/shard_map/ppermute | solution.py:25
  312.0 43.8 %collective-permute-start.17 = (bf16[768,768]{1,0:T(8,128)(2,1)}, bf16[768,768]{1,0:T(8,128)(2,1)}, u32[]{:S(2)}, u32[]{:S(2)}) collective-permute-start(bf16[768,768]{1,0:T(8,128)(2,1)} %collective-permute-done.13), channel_id=1, source_target_pairs={{0,2},{2,0},{4,6},{6,4},{8,10},{10,8},{12,14},{14,12},{16,18},{18,... | collective-permute-start | bytes 3538952 | tf_op jit(solution)/shard_map/ppermute | solution.py:25
  337.8 36.4 %collective-permute-start.18 = (bf16[768,768]{1,0:T(8,128)(2,1)}, bf16[768,768]{1,0:T(8,128)(2,1)}, u32[]{:S(2)}, u32[]{:S(2)}) collective-permute-start(bf16[768,768]{1,0:T(8,128)(2,1)} %collective-permute-done.14), channel_id=1, source_target_pairs={{0,2},{2,0},{4,6},{6,4},{8,10},{10,8},{12,14},{14,12},{16,18},{18,... | collective-permute-start | bytes 3538952 | tf_op jit(solution)/shard_map/ppermute | solution.py:25
  381.5 62.4 %all-to-all-start.1 = ((bf16[16,112,768]{2,1,0:T(8,128)(2,1)}), bf16[16,112,768]{2,1,0:T(8,128)(2,1)}, u32[]{:S(2)}, u32[]{:S(2)}) async-start(bf16[16,112,768]{2,1,0:T(8,128)(2,1)} %bitcast.275), calls=%async_computation.1 | async-start | bytes 5505024 | tf_op jit(solution)/shard_map/all_to_all | solution.py:228
  392.7 60.4 %collective-permute-start.21 = (f32[8,128]{1,0:T(8,128)S(1)}, f32[8,128]{1,0:T(8,128)S(1)}, u32[]{:S(2)}, u32[]{:S(2)}) collective-permute-start(f32[8,128]{1,0:T(8,128)S(1)} %broadcast_in_dim.158), channel_id=1, source_target_pairs={{0,2},{2,0},{4,6},{6,4},{8,10},{10,8},{12,14},{14,12},{16,18},{18,... | collective-permute-start | bytes 12296 | tf_op jit(solution)/shard_map/ppermute | solution.py:25
  451.6 24.1 %collective-permute-start.19 = (bf16[624,768]{1,0:T(8,128)(2,1)}, bf16[624,768]{1,0:T(8,128)(2,1)S(1)}, u32[]{:S(2)}, u32[]{:S(2)}) collective-permute-start(bf16[624,768]{1,0:T(8,128)(2,1)} %slice.887), channel_id=1, source_target_pairs={{0,1},{1,0},{2,3},{3,2},{4,5},{5,4},{6,7},{7,6},{8,9},{9,8},{10,11... | collective-permute-start | bytes 2875400 | tf_op jit(solution)/shard_map/ppermute | solution.py:25
  481.1 23.2 %collective-permute-start.20 = (bf16[624,768]{1,0:T(8,128)(2,1)S(1)}, bf16[624,768]{1,0:T(8,128)(2,1)}, u32[]{:S(2)}, u32[]{:S(2)}) collective-permute-start(bf16[624,768]{1,0:T(8,128)(2,1)S(1)} %convert_element_type.527), channel_id=1, source_target_pairs={{0,1},{1,0},{2,3},{3,2},{4,5},{5,4},{6,7},{7,6},{8,9},{9,8},{10,11... | collective-permute-start | bytes 2875400 | tf_op jit(solution)/shard_map/ppermute | solution.py:25
  522.0 65.6 %all-to-all-start.2 = ((bf16[16,112,768]{2,1,0:T(8,128)(2,1)}), bf16[16,112,768]{2,1,0:T(8,128)(2,1)}, u32[]{:S(2)}, u32[]{:S(2)}) async-start(bf16[16,112,768]{2,1,0:T(8,128)(2,1)} %bitcast.269), calls=%async_computation.2 | async-start | bytes 5505024 | tf_op jit(solution)/shard_map/all_to_all | solution.py:228
  633.7 66.5 %all-to-all-start.3 = ((bf16[16,112,768]{2,1,0:T(8,128)(2,1)}), bf16[16,112,768]{2,1,0:T(8,128)(2,1)}, u32[]{:S(2)}, u32[]{:S(2)}) async-start(bf16[16,112,768]{2,1,0:T(8,128)(2,1)} %bitcast.270), calls=%async_computation.3 | async-start | bytes 5505024 | tf_op jit(solution)/shard_map/all_to_all | solution.py:228
  647.6 356.5 %reduce-scatter.4.cloned.1.call-start = ((), (), s32[]{:S(2)}) async-start(), calls=%async_computation.5 | async-start | bytes 417792
  654.4 24.0 %collective-permute-start.68 = (bf16[768,768]{1,0:T(8,128)(2,1)S(1)}, bf16[768,768]{1,0:T(8,128)(2,1)S(1)}, u32[]{:S(2)}, u32[]{:S(2)}) collective-permute-start(bf16[768,768]{1,0:T(8,128)(2,1)S(1)} %convolution_convert_fusion), channel_id=1, source_target_pairs={{0,2},{2,0},{4,6},{6,4},{8,10},{10,8},{12,14},{14,12},{16,18},{18,... | collective-permute-start | bytes 3538952 | tf_op jit(solution)/shard_map/ppermute | solution.py:25
  659.2 26.8 %collective-permute-start.65 = (bf16[768,768]{1,0:T(8,128)(2,1)S(1)}, bf16[768,768]{1,0:T(8,128)(2,1)S(1)}, u32[]{:S(2)}, u32[]{:S(2)}) collective-permute-start(bf16[768,768]{1,0:T(8,128)(2,1)S(1)} %convolution_convert_fusion.2), channel_id=1, source_target_pairs={{0,2},{2,0},{4,6},{6,4},{8,10},{10,8},{12,14},{14,12},{16,18},{18,... | collective-permute-start | bytes 3538952 | tf_op jit(solution)/shard_map/ppermute | solution.py:25
  677.9 34.7 %collective-permute-start.67 = (bf16[768,768]{1,0:T(8,128)(2,1)}, bf16[768,768]{1,0:T(8,128)(2,1)}, u32[]{:S(2)}, u32[]{:S(2)}) collective-permute-start(bf16[768,768]{1,0:T(8,128)(2,1)} %convolution_convert_fusion.1), channel_id=1, source_target_pairs={{0,2},{2,0},{4,6},{6,4},{8,10},{10,8},{12,14},{14,12},{16,18},{18,... | collective-permute-start | bytes 3538952 | tf_op jit(solution)/shard_map/ppermute | solution.py:25
  678.3 38.8 %collective-permute-start.64 = (bf16[768,768]{1,0:T(8,128)(2,1)}, bf16[768,768]{1,0:T(8,128)(2,1)S(1)}, u32[]{:S(2)}, u32[]{:S(2)}) collective-permute-start(bf16[768,768]{1,0:T(8,128)(2,1)} %convolution_convert_fusion.3), channel_id=1, source_target_pairs={{0,2},{2,0},{4,6},{6,4},{8,10},{10,8},{12,14},{14,12},{16,18},{18,... | collective-permute-start | bytes 3538952 | tf_op jit(solution)/shard_map/ppermute | solution.py:25
  684.5 29.2 %collective-permute-start.69 = (bf16[768,768]{1,0:T(8,128)(2,1)}, bf16[768,768]{1,0:T(8,128)(2,1)}, u32[]{:S(2)}, u32[]{:S(2)}) collective-permute-start(bf16[768,768]{1,0:T(8,128)(2,1)} %add_convert_fusion.2), channel_id=1, source_target_pairs={{0,1},{1,0},{2,3},{3,2},{4,5},{5,4},{6,7},{7,6},{8,9},{9,8},{10,11... | collective-permute-start | bytes 3538952 | tf_op jit(solution)/shard_map/ppermute | solution.py:25
  691.2 47.7 %collective-permute-start.66 = (bf16[768,768]{1,0:T(8,128)(2,1)}, bf16[768,768]{1,0:T(8,128)(2,1)}, u32[]{:S(2)}, u32[]{:S(2)}) collective-permute-start(bf16[768,768]{1,0:T(8,128)(2,1)} %add_convert_fusion.3), channel_id=1, source_target_pairs={{0,1},{1,0},{2,3},{3,2},{4,5},{5,4},{6,7},{7,6},{8,9},{9,8},{10,11... | collective-permute-start | bytes 3538952 | tf_op jit(solution)/shard_map/ppermute | solution.py:25
  706.9 51.9 %collective-permute-start.26 = (bf16[624,768]{1,0:T(8,128)(2,1)S(1)}, bf16[624,768]{1,0:T(8,128)(2,1)S(1)}, u32[]{:S(2)}, u32[]{:S(2)}) collective-permute-start(bf16[624,768]{1,0:T(8,128)(2,1)S(1)} %slice.886), channel_id=1, source_target_pairs={{0,1},{1,0},{2,3},{3,2},{4,5},{5,4},{6,7},{7,6},{8,9},{9,8},{10,11... | collective-permute-start | bytes 2875400 | tf_op jit(solution)/shard_map/ppermute | solution.py:25
  919.6 162.7 %collective-permute-start.59 = (bf16[384,1536]{1,0:T(8,128)(2,1)}, bf16[384,1536]{1,0:T(8,128)(2,1)}, u32[]{:S(2)}, u32[]{:S(2)}) collective-permute-start(bf16[384,1536]{1,0:T(8,128)(2,1)} %slice.882), channel_id=1, source_target_pairs={{0,2},{2,0},{4,6},{6,4},{8,10},{10,8},{12,14},{14,12},{16,18},{18,... | collective-permute-start | bytes 3538952 | tf_op jit(solution)/shard_map/ppermute | solution.py:25
  927.2 83.5 %collective-permute-start.41 = (bf16[384,384]{1,0:T(8,128)(2,1)}, bf16[384,384]{1,0:T(8,128)(2,1)}, u32[]{:S(2)}, u32[]{:S(2)}) collective-permute-start(bf16[384,384]{1,0:T(8,128)(2,1)} %slice.900), channel_id=1, source_target_pairs={{0,2},{2,0},{4,6},{6,4},{8,10},{10,8},{12,14},{14,12},{16,18},{18,... | collective-permute-start | bytes 884744 | tf_op jit(solution)/shard_map/ppermute | solution.py:25
  929.5 87.7 %collective-permute-start.40 = (bf16[384,384]{1,0:T(8,128)(2,1)}, bf16[384,384]{1,0:T(8,128)(2,1)}, u32[]{:S(2)}, u32[]{:S(2)}) collective-permute-start(bf16[384,384]{1,0:T(8,128)(2,1)} %slice.901), channel_id=1, source_target_pairs={{0,2},{2,0},{4,6},{6,4},{8,10},{10,8},{12,14},{14,12},{16,18},{18,... | collective-permute-start | bytes 884744 | tf_op jit(solution)/shard_map/ppermute | solution.py:25
  931.3 82.4 %collective-permute-start.47 = (bf16[384,384]{1,0:T(8,128)(2,1)}, bf16[384,384]{1,0:T(8,128)(2,1)}, u32[]{:S(2)}, u32[]{:S(2)}) collective-permute-start(bf16[384,384]{1,0:T(8,128)(2,1)} %slice.898), channel_id=1, source_target_pairs={{0,2},{2,0},{4,6},{6,4},{8,10},{10,8},{12,14},{14,12},{16,18},{18,... | collective-permute-start | bytes 884744 | tf_op jit(solution)/shard_map/ppermute | solution.py:25
  933.7 88.6 %collective-permute-start.46 = (bf16[384,384]{1,0:T(8,128)(2,1)}, bf16[384,384]{1,0:T(8,128)(2,1)}, u32[]{:S(2)}, u32[]{:S(2)}) collective-permute-start(bf16[384,384]{1,0:T(8,128)(2,1)} %slice.899), channel_id=1, source_target_pairs={{0,2},{2,0},{4,6},{6,4},{8,10},{10,8},{12,14},{14,12},{16,18},{18,... | collective-permute-start | bytes 884744 | tf_op jit(solution)/shard_map/ppermute | solution.py:25
  1017.2 130.1 %collective-permute-start.58 = (bf16[384,1536]{1,0:T(8,128)(2,1)}, bf16[384,1536]{1,0:T(8,128)(2,1)}, u32[]{:S(2)}, u32[]{:S(2)}) collective-permute-start(bf16[384,1536]{1,0:T(8,128)(2,1)} %slice.883), channel_id=1, source_target_pairs={{0,2},{2,0},{4,6},{6,4},{8,10},{10,8},{12,14},{14,12},{16,18},{18,... | collective-permute-start | bytes 3538952 | tf_op jit(solution)/shard_map/ppermute | solution.py:25
  1021.1 65.2 %collective-permute-start.53 = (bf16[384,1536]{1,0:T(8,128)(2,1)}, bf16[384,1536]{1,0:T(8,128)(2,1)}, u32[]{:S(2)}, u32[]{:S(2)}) collective-permute-start(bf16[384,1536]{1,0:T(8,128)(2,1)} %slice.884), channel_id=1, source_target_pairs={{0,2},{2,0},{4,6},{6,4},{8,10},{10,8},{12,14},{14,12},{16,18},{18,... | collective-permute-start | bytes 3538952 | tf_op jit(solution)/shard_map/ppermute | solution.py:25
  1022.2 31.4 %collective-permute-start.29 = (bf16[384,1152]{1,0:T(8,128)(2,1)S(1)}, bf16[384,1152]{1,0:T(8,128)(2,1)S(1)}, u32[]{:S(2)}, u32[]{:S(2)}) collective-permute-start(bf16[384,1152]{1,0:T(8,128)(2,1)S(1)} %copy-done.86), channel_id=1, source_target_pairs={{0,2},{2,0},{4,6},{6,4},{8,10},{10,8},{12,14},{14,12},{16,18},{18,... | collective-permute-start | bytes 2654216 | tf_op jit(solution)/shard_map/ppermute | solution.py:25
  1053.7 23.6 %collective-permute-start.27 = (bf16[624,768]{1,0:T(8,128)(2,1)S(1)}, bf16[624,768]{1,0:T(8,128)(2,1)S(1)}, u32[]{:S(2)}, u32[]{:S(2)}) collective-permute-start(bf16[624,768]{1,0:T(8,128)(2,1)S(1)} %add_convert_fusion.4), channel_id=1, source_target_pairs={{0,1},{1,0},{2,3},{3,2},{4,5},{5,4},{6,7},{7,6},{8,9},{9,8},{10,11... | collective-permute-start | bytes 2875400 | tf_op jit(solution)/shard_map/ppermute | solution.py:25
  1056.3 33.3 %collective-permute-start.28 = (bf16[384,1152]{1,0:T(8,128)(2,1)}, bf16[384,1152]{1,0:T(8,128)(2,1)}, u32[]{:S(2)}, u32[]{:S(2)}) collective-permute-start(bf16[384,1152]{1,0:T(8,128)(2,1)} %slice.891), channel_id=1, source_target_pairs={{0,2},{2,0},{4,6},{6,4},{8,10},{10,8},{12,14},{14,12},{16,18},{18,... | collective-permute-start | bytes 2654216 | tf_op jit(solution)/shard_map/ppermute | solution.py:25
  1077.3 30.7 %collective-permute-start.34 = (bf16[384,1152]{1,0:T(8,128)(2,1)}, bf16[384,1152]{1,0:T(8,128)(2,1)}, u32[]{:S(2)}, u32[]{:S(2)}) collective-permute-start(bf16[384,1152]{1,0:T(8,128)(2,1)} %slice.889), channel_id=1, source_target_pairs={{0,2},{2,0},{4,6},{6,4},{8,10},{10,8},{12,14},{14,12},{16,18},{18,... | collective-permute-start | bytes 2654216 | tf_op jit(solution)/shard_map/ppermute | solution.py:25
  1082.4 22.5 %collective-permute-start.30 = (bf16[384,1152]{1,0:T(8,128)(2,1)S(1)}, bf16[384,1152]{1,0:T(8,128)(2,1)S(1)}, u32[]{:S(2)}, u32[]{:S(2)}) collective-permute-start(bf16[384,1152]{1,0:T(8,128)(2,1)S(1)} %copy-done.84), channel_id=1, source_target_pairs={{0,1},{1,0},{2,3},{3,2},{4,5},{5,4},{6,7},{7,6},{8,9},{9,8},{10,11... | collective-permute-start | bytes 2654216 | tf_op jit(solution)/shard_map/ppermute | solution.py:25
  1086.3 37.6 %collective-permute-start.36 = (bf16[384,1152]{1,0:T(8,128)(2,1)S(1)}, bf16[384,1152]{1,0:T(8,128)(2,1)S(1)}, u32[]{:S(2)}, u32[]{:S(2)}) collective-permute-start(bf16[384,1152]{1,0:T(8,128)(2,1)S(1)} %copy-done.83), channel_id=1, source_target_pairs={{0,1},{1,0},{2,3},{3,2},{4,5},{5,4},{6,7},{7,6},{8,9},{9,8},{10,11... | collective-permute-start | bytes 2654216 | tf_op jit(solution)/shard_map/ppermute | solution.py:25
  1089.6 62.7 %collective-permute-start.52 = (bf16[384,1536]{1,0:T(8,128)(2,1)S(1)}, bf16[384,1536]{1,0:T(8,128)(2,1)S(1)}, u32[]{:S(2)}, u32[]{:S(2)}) collective-permute-start(bf16[384,1536]{1,0:T(8,128)(2,1)S(1)} %copy-done.72), channel_id=1, source_target_pairs={{0,2},{2,0},{4,6},{6,4},{8,10},{10,8},{12,14},{14,12},{16,18},{18,... | collective-permute-start | bytes 3538952 | tf_op jit(solution)/shard_map/ppermute | solution.py:25
  1104.9 44.2 %collective-permute-start.60 = (bf16[384,1536]{1,0:T(8,128)(2,1)S(1)}, bf16[384,1536]{1,0:T(8,128)(2,1)S(1)}, u32[]{:S(2)}, u32[]{:S(2)}) collective-permute-start(bf16[384,1536]{1,0:T(8,128)(2,1)S(1)} %fusion.87), channel_id=1, source_target_pairs={{0,1},{1,0},{2,3},{3,2},{4,5},{5,4},{6,7},{7,6},{8,9},{9,8},{10,11... | collective-permute-start | bytes 3538952 | tf_op jit(solution)/shard_map/ppermute | solution.py:25
  1108.0 66.0 %collective-permute-start.54 = (bf16[384,1536]{1,0:T(8,128)(2,1)S(1)}, bf16[384,1536]{1,0:T(8,128)(2,1)S(1)}, u32[]{:S(2)}, u32[]{:S(2)}) collective-permute-start(bf16[384,1536]{1,0:T(8,128)(2,1)S(1)} %fusion.89), channel_id=1, source_target_pairs={{0,1},{1,0},{2,3},{3,2},{4,5},{5,4},{6,7},{7,6},{8,9},{9,8},{10,11... | collective-permute-start | bytes 3538952 | tf_op jit(solution)/shard_map/ppermute | solution.py:25
  1145.8 30.1 %collective-permute-start.32 = (bf16[96,1152]{1,0:T(8,128)(2,1)S(1)}, bf16[96,1152]{1,0:T(8,128)(2,1)S(1)}, u32[]{:S(2)}, u32[]{:S(2)}) collective-permute-start(bf16[96,1152]{1,0:T(8,128)(2,1)S(1)} %slice.903), channel_id=1, source_target_pairs={{0,8},{2,10},{4,12},{6,14},{8,0},{10,2},{12,4},{14,6},{16,24},{18,... | collective-permute-start | bytes 663560 | tf_op jit(solution)/shard_map/ppermute | solution.py:25
  1147.3 30.3 %collective-permute-start.38 = (bf16[96,1152]{1,0:T(8,128)(2,1)S(1)}, bf16[96,1152]{1,0:T(8,128)(2,1)S(1)}, u32[]{:S(2)}, u32[]{:S(2)}) collective-permute-start(bf16[96,1152]{1,0:T(8,128)(2,1)S(1)} %slice.902), channel_id=1, source_target_pairs={{0,8},{2,10},{4,12},{6,14},{8,0},{10,2},{12,4},{14,6},{16,24},{18,... | collective-permute-start | bytes 663560 | tf_op jit(solution)/shard_map/ppermute | solution.py:25
  1151.0 38.3 %collective-permute-start.61 = (bf16[192,1536]{1,0:T(8,128)(2,1)S(1)}, bf16[192,1536]{1,0:T(8,128)(2,1)S(1)}, u32[]{:S(2)}, u32[]{:S(2)}) collective-permute-start(bf16[192,1536]{1,0:T(8,128)(2,1)S(1)} %slice.892), channel_id=1, source_target_pairs={{0,4},{2,6},{4,0},{6,2},{8,12},{10,14},{12,8},{14,10},{16,20},{18,... | collective-permute-start | bytes 1769480 | tf_op jit(solution)/shard_map/ppermute | solution.py:25
  (236 other events, 2542.7 us)
Sparse Core Ops, SparseCore 0:
  947.2 56.7 reduce-scatter.3

commit v2 on v1

v2 whole, which is shorter than its diff:
```python
import functools

import jax
import jax.numpy as jnp
from jax import lax
from jax.experimental import pallas as pl
from jax.experimental.pallas import tpu as pltpu
from jax.sharding import PartitionSpec as P

HD = 64
SEQ = 197
ROWS = 208
EPS = 1e-06
COST = 0.2
BF = jnp.bfloat16
F32 = jnp.float32


def mm(a, b, dims):
    return lax.dot_general(a, b, (dims, ((), ())), preferred_element_type=F32)


NN = ((1,), (0,))
NT = ((1,), (1,))
TN = ((0,), (0,))


def swap(value, axis, distance):
    size = lax.axis_size(axis)
    return lax.ppermute(value, axis, [(k, k ^ distance) for k in range(size)])


def gelu_both(x):
    k = 0.7978845608028654
    a = 0.044715 * k
    square = x * x
    half = 0.5 * jnp.tanh(x * (a * square + k)) + 0.5
    act = x * half
    return act, half + act * (1.0 - half) * (6.0 * a * square + 2.0 * k)


def row_stats(values):
    center = values - jnp.mean(values, axis=-1, keepdims=True)
    scale = lax.rsqrt(jnp.mean(center * center, axis=-1, keepdims=True) + EPS)
    return center * scale, scale


def norm_pull(grad, hat, scale, gain):
    inner = grad * gain
    first = jnp.mean(inner, axis=-1, keepdims=True)
    second = jnp.mean(inner * hat, axis=-1, keepdims=True)
    return scale * (inner - first - hat * second)


def attend_copies(layer, place, refs, targets, sems):
    qkv_in, out_in, parts = refs[0], refs[1], refs[2:]
    own_qkv, own_out, far_qkv, far_out = targets
    pairs = [(qkv_in.at[layer], own_qkv), (out_in.at[layer], own_out)]
    blocks, span = far_out.shape[1], far_out.shape[2]
    rows, few = far_qkv.shape[2] // 4, span // 4
    for k, part in enumerate(parts):
        d = k // 4
        quarter = (place % 4) ^ (k % 4)
        at = pl.multiple_of(quarter * rows, 16)
        for s in range(3):
            pairs.append((part.at[pl.ds(s * rows, rows)], far_qkv.at[d, s, pl.ds(at, rows)]))
        at = pl.multiple_of(quarter * few, 16)
        for j in range(blocks):
            source = part.at[pl.ds(3 * rows + j * few, few)]
            pairs.append((source, far_out.at[d, j, pl.ds(at, few)]))
    return [pltpu.make_async_copy(x, y, sems.at[n]) for n, (x, y) in enumerate(pairs)]


def dense_copies(place, refs, targets, sems):
    first_in, second_in, parts = refs[0], refs[1], refs[2:]
    own_first, own_second, far_first, far_second = targets
    pairs = [(first_in, own_first), (second_in, own_second)]
    width, span = own_first.shape
    rows, few = width // 4, span // 4
    for k, part in enumerate(parts):
        d = k // 4
        quarter = (place % 4) ^ (k % 4)
        at = pl.multiple_of(quarter * rows, 16)
        pairs.append((part.at[pl.ds(0, rows)], far_first.at[d, pl.ds(at, rows)]))
        for j in range(few // rows):
            at = pl.multiple_of(quarter * few + j * rows, 16)
            source = part.at[pl.ds(rows, rows), pl.ds(j * width, width)]
            pairs.append((source, far_second.at[d, pl.ds(at, rows)]))
    return [pltpu.make_async_copy(x, y, sems.at[n]) for n, (x, y) in enumerate(pairs)]


def attend_scratch(width, groups):
    span = width // groups
    return (
        (3, width, span), (span, width), (groups - 1, 3, width, span),
        (groups - 1, groups, span, span),
    ), 2 + 4 * (groups - 1) * (3 + groups)


def dense_scratch(width, hidden, groups):
    span = hidden // groups
    return (
        (width, span), (span, width), (groups - 1, width, span), (groups - 1, span, width),
    ), 2 + 4 * (groups - 1) * (1 + span // width)


def run_at_start(copies):
    @pl.when(pl.program_id(0) == 0)
    def _():
        for copy in copies:
            copy.start()


def wait_at_start(copies):
    @pl.when(pl.program_id(0) == 0)
    def _():
        for copy in copies:
            copy.wait()


def pair_masks():
    left = lax.broadcasted_iota(jnp.int32, (ROWS, 2 * HD), 1) < HD
    seen = lax.broadcasted_iota(jnp.int32, (2 * ROWS, ROWS), 1) < SEQ
    return left, seen


def stack_pair(rows, left):
    none = jnp.zeros_like(rows)
    return jnp.concatenate([jnp.where(left, rows, none), jnp.where(left, none, rows)], 0)


def attend_kernel(layer, groups, follow, place_ref, x_ref, gain_ref, bias_ref, *refs):
    next_norm, refs = refs[: 2 * follow], refs[2 * follow :]
    many = 4 * groups - 2
    new_ref, normed_ref, packed_ref, mixed_ref, total_ref = refs[many : many + 5]
    targets, sems = refs[-5:-1], refs[-1]
    next_refs = refs[many + 5 : -5]
    own_qkv, own_out, far_qkv, far_out = targets
    copies = attend_copies(layer, place_ref[0], refs[:many], targets, sems)
    run_at_start(copies)
    values = x_ref[...]
    hat, _ = row_stats(values)
    normed = (hat * gain_ref[...] + bias_ref[...]).astype(BF)
    normed_ref[...] = normed
    wait_at_start(copies)
    span = own_qkv.shape[-1]
    for s in range(3):
        packed_ref[s, :, :span] = mm(normed, own_qkv[s], NN).astype(BF)
        for d in range(1, groups):
            part = mm(normed, far_qkv[d - 1, s], NN).astype(BF)
            packed_ref[s, :, d * span : (d + 1) * span] = part
    left, seen = pair_masks()
    lane = lax.broadcasted_iota(jnp.int32, (ROWS, 128), 1)
    totals = jnp.zeros((ROWS, 128), F32)
    for pair in range(packed_ref.shape[-1] // (2 * HD)):
        cols = slice(pair * 2 * HD, (pair + 1) * 2 * HD)
        query = stack_pair(packed_ref[0, :, cols] * BF(HD**-0.5), left)
        scores = jnp.where(seen, mm(query, packed_ref[1, :, cols], NT), -1e30)
        most = jnp.max(scores, axis=-1, keepdims=True)
        probs = jnp.exp(scores - most)
        total = jnp.sum(probs, axis=-1, keepdims=True)
        mixed = mm(probs.astype(BF), packed_ref[2, :, cols], NN) / total
        mixed_ref[:, cols] = jnp.where(left, mixed[:ROWS], mixed[ROWS:]).astype(BF)
        logs = most + jnp.log(total)
        totals = jnp.where(lane == 2 * pair, logs[:ROWS], totals)
        totals = jnp.where(lane == 2 * pair + 1, logs[ROWS:], totals)
    total_ref[...] = totals
    values = values + mm(mixed_ref[:, :span], own_out[...], NN)
    for d in range(1, groups):
        mixed = mixed_ref[:, d * span : (d + 1) * span]
        parts = [mm(mixed, far_out[d - 1, j], NN) for j in range(groups)]
        values = values + jnp.concatenate(parts, 1)
    new_ref[...] = values
    for next_ref in next_refs:
        hat, _ = row_stats(values)
        next_ref[...] = (hat * next_norm[0][...] + next_norm[1][...]).astype(BF)


def attend_back_kernel(
    layer, groups, place_ref, grad_ref, x_ref, packed_ref, total_ref, gain_ref, *refs
):
    many = 4 * groups - 2
    targets, sems = refs[-5:-1], refs[-1]
    moved_ref, gain_out, bias_out = refs[many : many + 3]
    new_refs = refs[many + 3 : -5]
    own_qkv, own_out, far_qkv, far_out = targets
    copies = attend_copies(layer, place_ref[0], refs[:many], targets, sems)
    run_at_start(copies)
    grad = grad_ref[...]
    low = grad.astype(BF)
    wait_at_start(copies)
    span = own_qkv.shape[-1]
    grad_mixed = [mm(low, own_out[...], NT).astype(BF)]
    for d in range(1, groups):
        parts = [
            mm(low[:, j * span : (j + 1) * span], far_out[d - 1, j], NT) for j in range(groups)
        ]
        grad_mixed.append(sum(parts).astype(BF))
    grad_mixed = jnp.concatenate(grad_mixed, 1)
    left, seen = pair_masks()
    for pair in range(packed_ref.shape[-1] // (2 * HD)):
        cols = slice(pair * 2 * HD, (pair + 1) * 2 * HD)
        query = stack_pair(packed_ref[0, :, cols] * BF(HD**-0.5), left)
        key = packed_ref[1, :, cols]
        outer = stack_pair(grad_mixed[:, cols], left)
        total = jnp.concatenate(
            [total_ref[:, 2 * pair : 2 * pair + 1], total_ref[:, 2 * pair + 1 : 2 * pair + 2]], 0
        )
        probs = jnp.where(seen, jnp.exp(mm(query, key, NT) - total), 0.0)
        grad_probs = mm(outer, packed_ref[2, :, cols], NT)
        inner = jnp.sum(grad_probs * probs, axis=-1, keepdims=True)
        grad_scores = (probs * (grad_probs - inner)).astype(BF)
        grad_query = mm(grad_scores, key, NN) * HD**-0.5
        moved_ref[0, :, cols] = jnp.where(left, grad_query[:ROWS], grad_query[ROWS:]).astype(BF)
        moved_ref[1, :, cols] = mm(grad_scores, query, TN).astype(BF)
        moved_ref[2, :, cols] = mm(probs.astype(BF), outer, TN).astype(BF)
    back = jnp.zeros_like(grad)
    for s in range(3):
        back = back + mm(moved_ref[s, :, :span], own_qkv[s], NT)
        for d in range(1, groups):
            back = back + mm(moved_ref[s, :, d * span : (d + 1) * span], far_qkv[d - 1, s], NT)
    finish_back(grad, back, x_ref, gain_ref, new_refs, gain_out, bias_out)


def finish_back(grad, back, x_ref, gain_ref, new_refs, gain_out, bias_out):
    hat, scale = row_stats(x_ref[...])
    grad = grad + norm_pull(back, hat, scale, gain_ref[...])
    for new_ref in new_refs:
        new_ref[...] = grad.astype(new_ref.dtype)

    @pl.when(pl.program_id(0) == 0)
    def _():
        gain_out[...] = jnp.zeros_like(gain_out)
        bias_out[...] = jnp.zeros_like(bias_out)

    gain_out[...] += jnp.sum(back * hat, axis=0, keepdims=True)
    bias_out[...] += jnp.sum(back, axis=0, keepdims=True)


def dense_kernel(groups, place_ref, x_ref, gain_ref, bias_ref, *refs):
    many = 4 * groups - 2
    new_ref, normed_ref, act_ref, slope_ref = refs[many : many + 4]
    targets, sems = refs[many + 4 : -1], refs[-1]
    copies = dense_copies(place_ref[0], refs[:many], targets, sems)
    firsts = [targets[0]] + [targets[2].at[d] for d in range(groups - 1)]
    seconds = [targets[1]] + [targets[3].at[d] for d in range(groups - 1)]
    run_at_start(copies)
    values = x_ref[...]
    hat, _ = row_stats(values)
    normed = (hat * gain_ref[...] + bias_ref[...]).astype(BF)
    normed_ref[...] = normed
    wait_at_start(copies)
    span = targets[0].shape[-1]
    chunk = span // 2
    for d in range(groups):
        for part in range(2):
            inner = slice(part * chunk, (part + 1) * chunk)
            cols = slice(d * span + part * chunk, d * span + (part + 1) * chunk)
            act, slope = gelu_both(mm(normed, firsts[d][:, inner], NN))
            act = act.astype(BF)
            act_ref[:, cols] = act
            slope_ref[:, cols] = slope.astype(BF)
            values = values + mm(act, seconds[d][inner], NN)
    new_ref[...] = values


def dense_back_kernel(groups, place_ref, grad_ref, x_ref, slope_ref, gain_ref, *refs):
    many = 4 * groups - 2
    moved_ref, gain_out, bias_out = refs[many : many + 3]
    new_refs = refs[many + 3 : -5]
    targets, sems = refs[-5:-1], refs[-1]
    copies = dense_copies(place_ref[0], refs[:many], targets, sems)
    firsts = [targets[0]] + [targets[2].at[d] for d in range(groups - 1)]
    seconds = [targets[1]] + [targets[3].at[d] for d in range(groups - 1)]
    run_at_start(copies)
    grad = grad_ref[...]
    low = grad.astype(BF)
    wait_at_start(copies)
    span = targets[0].shape[-1]
    chunk = span // 2
    back = jnp.zeros_like(grad)
    for d in range(groups):
        for part in range(2):
            inner = slice(part * chunk, (part + 1) * chunk)
            cols = slice(d * span + part * chunk, d * span + (part + 1) * chunk)
            hidden = mm(low, seconds[d][inner], NT) * slope_ref[:, cols].astype(F32)
            hidden = hidden.astype(BF)
            moved_ref[:, cols] = hidden
            back = back + mm(hidden, firsts[d][:, inner], NT)
    finish_back(grad, back, x_ref, gain_ref, new_refs, gain_out, bias_out)


def image_block(*shape):
    lead = len(shape) - 2
    return pl.BlockSpec(shape, lambda i: (0,) * lead + (i, 0))


def fixed_block(*shape):
    return pl.BlockSpec(shape, lambda i: (0,) * len(shape))


RAW = pl.BlockSpec(memory_space=pl.ANY)


def dense_call(kernel, place, rows, singles, flat, outs, scratch, flops):
    buffers, copies = scratch
    specs = [pl.BlockSpec(memory_space=pltpu.SMEM)]
    specs += [image_block(*r.shape[:-2], ROWS, r.shape[-1]) for r in rows]
    specs += [fixed_block(*r.shape) for r in singles]
    specs += [RAW] * len(flat)
    out_specs = [
        image_block(*o.shape[:-2], ROWS, o.shape[-1]) if o.shape[-2] > 1 else fixed_block(*o.shape)
        for o in outs
    ]
    moved = sum(o.size * o.dtype.itemsize for o in list(outs) + list(rows) + flat)
    return pl.pallas_call(
        kernel,
        grid=(rows[0].shape[-2] // ROWS,),
        in_specs=specs,
        out_specs=out_specs,
        out_shape=outs,
        scratch_shapes=[pltpu.VMEM(b, BF) for b in buffers]
        + [pltpu.SemaphoreType.DMA((copies,))],
        cost_estimate=cost_of(flops, moved),
    )(place, *rows, *singles, *flat)


def cost_of(flops, moved):
    return pl.CostEstimate(
        flops=int(COST * flops), bytes_accessed=int(COST * moved), transcendentals=0
    )


def shape(*dims, kind=BF):
    return jax.ShapeDtypeStruct(dims, kind)


def attend_forward(layer, groups, place, values, gain, bias, weights, follow=()):
    rows, width = values.shape
    outs = (
        shape(rows, width, kind=F32),
        shape(rows, width),
        shape(3, rows, width),
        shape(rows, width),
        shape(rows, 128, kind=F32),
    ) + (shape(rows, width),) * bool(follow)
    return dense_call(
        functools.partial(attend_kernel, layer, groups, bool(follow)),
        place, (values,), (gain, bias) + follow, weights, outs, attend_scratch(width, groups),
        rows * width * (8 * width + 4 * ROWS),
    )


def attend_backward(
    layer, groups, place, grad, values, gain, packed, total, weights, kinds
):
    rows, width = values.shape
    outs = (
        shape(3, rows, width),
        shape(1, width, kind=F32),
        shape(1, width, kind=F32),
    ) + tuple(shape(rows, width, kind=k) for k in kinds)
    return dense_call(
        functools.partial(attend_back_kernel, layer, groups),
        place, (grad, values, packed, total), (gain,), weights, outs,
        attend_scratch(width, groups), rows * width * (8 * width + 10 * ROWS),
    )


def dense_forward(groups, place, values, gain, bias, weights):
    rows, width = values.shape
    hidden = groups * weights[0].shape[-1]
    outs = (
        shape(rows, width, kind=F32),
        shape(rows, width),
        shape(rows, hidden),
        shape(rows, hidden),
    )
    return dense_call(
        functools.partial(dense_kernel, groups),
        place, (values,), (gain, bias), weights, outs, dense_scratch(width, hidden, groups),
        4 * rows * width * hidden,
    )


def dense_backward(groups, place, grad, values, gain, slope, weights):
    rows, width = values.shape
    hidden = groups * weights[0].shape[-1]
    outs = (
        shape(rows, hidden),
        shape(1, width, kind=F32),
        shape(1, width, kind=F32),
        shape(rows, width, kind=F32),
        shape(rows, width),
    )
    return dense_call(
        functools.partial(dense_back_kernel, groups),
        place, (grad, values, slope), (gain,), weights, outs,
        dense_scratch(width, hidden, groups), 4 * rows * width * hidden,
    )


def expert_kernel(rows_ref, *refs):
    weights, (out_ref, act_ref, slope_ref) = refs[:-3], refs[-3:]
    rows = rows_ref[...]
    width = rows.shape[1]
    span = weights[0].shape[1]
    total = jnp.zeros(rows.shape, F32)
    for j, weight in enumerate(weights):
        cols = slice(j * span, (j + 1) * span)
        act, slope = gelu_both(mm(rows, weight[:width], NN))
        act = act.astype(BF)
        act_ref[:, cols] = act
        slope_ref[:, cols] = slope.astype(BF)
        parts = [mm(act, weight[k : k + span], NN) for k in range(width, 2 * width, span)]
        total = total + (jnp.concatenate(parts, 1) if len(parts) > 1 else parts[0])
    out_ref[...] = total.astype(BF)


def expert_back_kernel(grad_ref, slope_ref, *refs):
    weights, (out_ref, hidden_ref) = refs[:-2], refs[-2:]
    grad = grad_ref[...]
    width = grad.shape[1]
    span = weights[0].shape[1]
    total = jnp.zeros(grad.shape, F32)
    for j, weight in enumerate(weights):
        cols = slice(j * span, (j + 1) * span)
        parts = [
            mm(grad[:, k : k + span], weight[width + k : width + k + span], NT)
            for k in range(0, width, span)
        ]
        hidden = (sum(parts) * slope_ref[:, cols].astype(F32)).astype(BF)
        hidden_ref[:, cols] = hidden
        total = total + mm(hidden, weight[:width], NT)
    out_ref[...] = total.astype(BF)


def expert_call(kernel, rows, weights, outs):
    count = rows[0].shape[0]
    tile = 256 if count % 256 == 0 else 128
    hold = [
        pl.BlockSpec(w.shape, lambda i: (0, 0), pipeline_mode=pl.Buffered(1)) for w in weights
    ]
    moved = sum(o.size * o.dtype.itemsize for o in list(outs) + list(rows) + list(weights))
    return pl.pallas_call(
        kernel,
        grid=(count // tile,),
        in_specs=[image_spec(tile, r) for r in rows] + hold,
        out_specs=[image_spec(tile, o) for o in outs],
        out_shape=outs,
        cost_estimate=cost_of(2 * count * sum(w.size for w in weights), moved),
    )(*rows, *weights)


def image_spec(tile, like):
    return pl.BlockSpec((tile, like.shape[1]), lambda i: (i, 0))


def expert_forward(rows, weights):
    count, width = rows.shape
    hidden = len(weights) * weights[0].shape[1]
    outs = (shape(count, width), shape(count, hidden), shape(count, hidden))
    return expert_call(expert_kernel, (rows,), weights, outs)


def expert_backward(grad, slope, weights):
    outs = (shape(*grad.shape), shape(*slope.shape))
    return expert_call(expert_back_kernel, (grad, slope), weights, outs)


def weight_kernel(groups, lines, mover_ref, *refs):
    stats, refs = refs[:lines], refs[lines:]
    count = (len(refs) - 2) // 2
    lefts, rights, (keep_ref, send_ref) = refs[:count], refs[count:-2], refs[-2:]
    half = keep_ref.shape[0]
    turned = [mm(mover_ref[...], left[...], NT).astype(BF) for left in lefts]
    at = 0
    columns = keep_ref.shape[1] // groups
    for left, right in zip(turned, rights):
        for s in range(right.shape[0] if len(right.shape) == 3 else 1):
            source = right.at[s] if len(right.shape) == 3 else right
            span = source.shape[1] // groups
            tile = min(source.shape[1], 768)
            for k in range(0, source.shape[1], tile):
                part = mm(left, source[:, k : k + tile], NN).astype(BF)
                for j in range(k, k + tile, min(span, tile)):
                    low = (j // span) * columns + at + j % span
                    high = low + min(span, tile)
                    piece = part[:, j - k : j - k + min(span, tile)]
                    keep_ref[:, low:high] = piece[:half]
                    send_ref[:, low:high] = piece[half:]
            at += span
    if lines:
        rows = [stat[...] for stat in stats]
        room = columns - at
        rows.append(jnp.zeros((room - sum(r.shape[0] for r in rows), half * 2), F32))
        piece = mm(mover_ref[...], jnp.concatenate(rows, 0).astype(BF), NT).astype(BF)
        for d in range(groups):
            keep_ref[:, d * columns + at : (d + 1) * columns] = piece[:half]
            send_ref[:, d * columns + at : (d + 1) * columns] = piece[half:]


def weight_grads(groups, mover, pairs, stats=()):
    width = mover.shape[0]
    columns = sum(r.size // r.shape[-2] for _, r in pairs)
    columns += groups * -(-sum(r.shape[0] for r in stats) // 128) * 128
    out = shape(width // 2, columns)
    rows = pairs[0][0].shape[0]
    operands = [mover, *stats] + [p[0] for p in pairs] + [p[1] for p in pairs]
    return pl.pallas_call(
        functools.partial(weight_kernel, groups, len(stats)),
        in_specs=[pl.BlockSpec(memory_space=pltpu.VMEM)] * len(operands),
        out_specs=[pl.BlockSpec(memory_space=pltpu.VMEM)] * 2,
        out_shape=(out, out),
        cost_estimate=cost_of(
            2 * width * columns * rows, sum(2 * o.size for o in operands) + 4 * out.size
        ),
    )(*operands)


def dispatch_kernel(part, far, back, extra_ref, lines_ref, gates_ref, rows_ref, *refs):
    seats, got, refs = refs[:far], refs[far : 2 * far], refs[2 * far :]
    out_ref = refs[back]
    tile = out_ref.shape[0]
    base = pl.program_id(0) * tile
    ids = base + lax.broadcasted_iota(jnp.int32, (tile, lines_ref.shape[1]), 0)
    first, second = ids == lines_ref[:1], ids == lines_ref[1:]
    total = mm((first | second).astype(F32).astype(BF), rows_ref[...], NN)
    if back:
        gates = jnp.where(first, gates_ref[:1], 0.0) + jnp.where(second, gates_ref[1:], 0.0)
        refs[2][...] = jnp.sum(total * refs[0][...].astype(F32), axis=1, keepdims=True)
        total = total * jnp.sum(gates, axis=1, keepdims=True)
    else:
        line = base + lax.broadcasted_iota(jnp.int32, (tile, 1), 0)
        total = total + jnp.where(line % part == part - 1, extra_ref[0], 0.0)
    for seat, x in zip(seats, got):
        ids = base + lax.broadcasted_iota(jnp.int32, (tile, seat.shape[1]), 0)
        total = total + mm((ids == seat[...]).astype(F32).astype(BF), x[...], NN)
    out_ref[...] = total.astype(BF)


def dispatch_call(part, slots, extra, lines, gates, rows, seats, got, merged=None):
    tile = 256 if slots % 256 == 0 else 128
    width = rows.shape[1]
    back = merged is not None
    held = [lines, gates, rows, *seats, *got]
    block = pl.BlockSpec((tile, width), lambda i: (i, 0))
    outs = (shape(slots, width),)
    specs = (block,)
    if back:
        outs += (shape(slots, 1, kind=F32),)
        specs += (pl.BlockSpec((tile, 1), lambda i: (i, 0)),)
    inputs = held + [merged] * back
    return pl.pallas_call(
        functools.partial(dispatch_kernel, part, len(got), back),
        grid=(slots // tile,),
        in_specs=[pl.BlockSpec(memory_space=pltpu.SMEM)]
        + [fixed_block(*x.shape) for x in held]
        + [block] * back,
        out_specs=specs,
        out_shape=outs,
        cost_estimate=cost_of(2 * slots * rows.size, 2 * (slots * width + rows.size)),
    )(extra, *inputs)


def picks_of(cols_ref, gates_ref, count):
    ids = lax.broadcasted_iota(jnp.int32, (cols_ref.shape[0], count), 1)
    first, second = ids == cols_ref[:, :1], ids == cols_ref[:, 1:]
    if gates_ref is None:
        return (first | second).astype(F32).astype(BF)
    picks = jnp.where(first, gates_ref[:, :1], 0.0) + jnp.where(second, gates_ref[:, 1:], 0.0)
    return picks.astype(BF)


def combine_kernel(far, cols_ref, gates_ref, x_ref, teacher_ref, scale_ref, *refs):
    others, rows_ref, got = refs[:far], refs[far], refs[far + 1 : 2 * far + 1]
    final_ref, grad_ref, low_ref = refs[2 * far + 1 :]
    total = x_ref[...]
    for cols, rows in zip((cols_ref,) + others, (rows_ref,) + got):
        total = total + mm(picks_of(cols, gates_ref, rows.shape[0]), rows[...], NN)
    final_ref[...] = total.astype(BF)
    grad = scale_ref[...] * (total - teacher_ref[...].astype(F32))
    grad_ref[...] = grad
    low_ref[...] = grad.astype(BF)


def combine_back_kernel(far, cols_ref, x_ref, grad_ref, logits_ref, *refs):
    others, rows_ref, got = refs[:far], refs[far], refs[far + 1 : 2 * far + 1]
    router_ref, gain_ref, gain_out, bias_out, *new_refs = refs[2 * far + 1 :]
    total = mm(logits_ref[...], router_ref[...], NT)
    for cols, rows in zip((cols_ref,) + others, (rows_ref,) + got):
        total = total + mm(picks_of(cols, None, rows.shape[0]), rows[...], NN)
    finish_back(grad_ref[...], total, x_ref, gain_ref, new_refs, gain_out, bias_out)


def combine_call(kernel, tiled, held, outs):
    moved = sum(x.size * x.dtype.itemsize for x in list(tiled) + list(held) + list(outs))
    return pl.pallas_call(
        kernel,
        grid=(tiled[0].shape[0] // ROWS,),
        in_specs=[image_block(ROWS, x.shape[1]) for x in tiled]
        + [fixed_block(*x.shape) for x in held],
        out_specs=[
            image_block(ROWS, o.shape[1]) if o.shape[0] > 1 else fixed_block(*o.shape) for o in outs
        ],
        out_shape=outs,
        cost_estimate=cost_of(2 * tiled[0].shape[0] * held[0].size, moved),
    )(*tiled, *held)


def outer_kernel(left_ref, right_ref, *refs):
    part = mm(left_ref[...], right_ref[...], TN)
    for got in refs[:-1]:
        part = part + got[...].astype(F32)
    refs[-1][...] = part.astype(refs[-1].dtype)


def expert_grads(left, right, width, span, odd, got=None, cut_left=True):
    rows = left.shape[0]
    wide = left.shape[1] if cut_left else right.shape[1]
    count = wide // (2 * span)
    high, low = (span, width) if cut_left else (width, span)
    cut = pl.BlockSpec((rows, span), lambda j: (0, 2 * j + odd))
    whole = pl.BlockSpec((rows, width), lambda j: (0, 0))
    block = pl.BlockSpec((high, low), lambda j: (j, 0))
    more = () if got is None else (got,)
    out = shape(count * high, low)
    return pl.pallas_call(
        outer_kernel,
        grid=(count,),
        in_specs=([cut, whole] if cut_left else [whole, cut]) + [block] * len(more),
        out_specs=block,
        out_shape=out,
        cost_estimate=cost_of(2 * out.size * rows, 2 * (left.size + right.size + 2 * out.size)),
    )(left, right, *more)


def pinned_all(values, *others):
    return lax.optimization_barrier(tuple(values) + others)[: len(values)]


def pinned(value, *others):
    return lax.optimization_barrier((value,) + others)[0]


def body(
    tokens,
    teacher,
    valid_flags,
    routes,
    capacity,
    norm_gains,
    norm_biases,
    attn_qkv,
    attn_out,
    mlp_in,
    mlp_out,
    router,
    expert_in,
    expert_out,
):
    owners = lax.axis_size("expert")
    groups = lax.axis_size("tensor")
    place = lax.axis_index("expert")
    group = lax.axis_index("tensor")
    local_rows, width = tokens.shape
    experts = router.shape[1]
    image_count = local_rows // SEQ
    images = -(-image_count // groups)
    own_rows = images * ROWS
    all_rows = groups * own_rows
    capacity_most = 4 * (3 * local_rows // (4 * experts))
    used = -(-capacity_most // (2 * groups))
    part = -(-(used + 1) // 16) * 16
    slots = owners * part
    gains = norm_gains.astype(F32)
    biases = norm_biases.astype(F32)

    def relative(rows, fill, count):
        shape = rows.shape[1:]
        grid = rows.reshape((image_count, SEQ) + shape)
        grid = jnp.pad(
            grid,
            [(0, groups * images - image_count), (0, ROWS - SEQ)] + [(0, 0)] * len(shape),
            constant_values=fill,
        )
        taken = [
            lax.dynamic_slice_in_dim(grid, (group ^ d) * images, images, 0) for d in range(count)
        ]
        return jnp.concatenate(taken, 0).reshape((count * own_rows,) + shape)

    def absolute(rows):
        shape = rows.shape[1:]
        grid = rows.reshape((groups * images, ROWS) + shape)
        taken = [
            lax.dynamic_slice_in_dim(grid, (group ^ d) * images, images, 0) for d in range(groups)
        ]
        grid = jnp.concatenate(taken, 0)[:image_count, :SEQ]
        return grid.reshape((local_rows,) + shape)

    place_ref = jnp.full((1,), place, jnp.int32)
    gain_rows = [gains[j : j + 1] for j in range(4)]
    bias_rows = [biases[j : j + 1] for j in range(4)]

    quarter = place % 4

    def attend_piece(layer):
        span = attn_out.shape[1]
        rows, few = width // 4, span // 4
        qkv_part = lax.dynamic_slice(
            attn_qkv, (layer, 0, quarter * rows, 0), (1, 3, rows, span)
        ).reshape(3 * rows, span)
        out_part = lax.dynamic_slice(attn_out, (layer, quarter * few, 0), (1, few, width))[0]
        parts = [out_part[:, j * span : (j + 1) * span] for j in range(groups)]
        return jnp.concatenate([qkv_part] + parts, 0)

    def dense_piece(first, second):
        rows, few = width // 4, second.shape[0] // 4
        second = lax.dynamic_slice_in_dim(second, quarter * few, few, 0)
        parts = [second[j * rows : (j + 1) * rows] for j in range(few // rows)]
        first = lax.dynamic_slice_in_dim(first, quarter * rows, rows, 0)
        return jnp.concatenate([first, jnp.concatenate(parts, 1)], 0)

    def over_tensor(value):
        return [swap(value, "tensor", d) for d in range(1, groups)]

    def both_cores(value):
        return [value, swap(value, "expert", 1)]

    last = [None]

    def after(*values):
        if last[0] is not None:
            values = pinned_all(values, last[0])
        return values if len(values) > 1 else values[0]

    def mark(value):
        last[0] = value
        return value

    def spread(parts):
        return [swap(part, "expert", 2) for part in parts], [swap(part, "expert", 1) for part in parts]

    def fourth(parts):
        return [swap(part, "expert", 1) for part in parts]

    def joined(first, second, third, last):
        return [x for four in zip(first, third, second, last) for x in four]

    piece_first = mark(attend_piece(0))
    first_x = over_tensor(piece_first)
    tokens = after(tokens)
    start = relative(tokens, 0, 1).astype(F32)
    first_x = list(pinned_all(first_x, start))
    first_y, first_c = spread(first_x)
    mark(first_x[0])
    piece_dense = mark(dense_piece(*after(mlp_in, mlp_out)))
    dense_x = over_tensor(piece_dense)
    first_y = list(pinned_all(first_y, piece_dense))
    first_l = fourth(first_y)
    mark(first_y[0])
    piece_second = mark(after(attend_piece(1)))
    second_x = over_tensor(piece_second)
    weights_first = [attn_qkv, attn_out] + joined(first_x, first_y, first_c, first_l)

    room = 2 * used
    kind = jnp.int32
    routes = pinned(routes, first_x[0])
    expert_of = jnp.concatenate([routes[:, 0], routes[:, 1]])
    owner = jnp.tile(jnp.arange(local_rows, dtype=kind) // (SEQ * images), 2)
    of_expert = (expert_of[:, None] == jnp.arange(experts, dtype=kind)).astype(kind)
    of_owner = (owner[:, None] == jnp.arange(groups, dtype=kind)).astype(kind)
    both = (
        (expert_of * groups + owner)[:, None] == jnp.arange(experts * groups, dtype=kind)
    ).astype(kind)
    earlier = (jnp.cumsum(both, axis=0) - both).reshape(-1, experts, groups)
    ahead = jnp.sum(earlier * of_expert[:, :, None], axis=1)
    rank = jnp.sum(ahead * of_owner, axis=1)
    kept_mask = jnp.sum(ahead, axis=1) < jnp.sum(of_expert * capacity[None, :], axis=1)
    held = jnp.sum(both * kept_mask[:, None].astype(kind), axis=0).reshape(experts, groups)
    inside = jnp.minimum(held, room)
    beyond = held - inside
    free = room - inside

    def before(counts):
        return jnp.cumsum(counts, axis=1) - counts

    def of_pair(table):
        return jnp.sum(of_expert[:, :, None] * table[None], axis=1)

    late = jnp.sum(of_pair(before(beyond)) * of_owner, axis=1) + rank - room
    free_from = of_pair(before(free))
    hit = (late[:, None] >= free_from) & (late[:, None] < free_from + of_pair(free))
    hit = hit.astype(kind)
    fits = rank < room
    at = jnp.where(fits, rank, jnp.sum(hit * (of_pair(inside) + late[:, None] - free_from), axis=1))
    home = jnp.where(fits, owner, jnp.sum(hit * jnp.arange(groups, dtype=kind), axis=1))
    row_of = (2 * expert_of + at // used) * part + at % used

    def own_pairs(values):
        return relative(values.reshape(2, local_rows).T, -1, 1)

    local_row = own_pairs(jnp.where(kept_mask & (owner == group) & (home == group), row_of, -1))
    most = min(experts, 2 * SEQ * images // capacity_most)
    rest = min(2 * SEQ * images - most * capacity_most, capacity_most) - room
    most = most * (capacity_most - room) + max(rest, 0)
    most = -(-most // 16) * 16
    few = min(64, most)
    masks = []
    for d in range(1, groups):
        masks.append(kept_mask & (owner == group) & (home == group ^ d))
        masks.append(kept_mask & (owner == group ^ d) & (home == group))
    masks = jnp.stack(masks, 1).astype(kind)
    ranks = jnp.cumsum(masks, axis=0) - masks
    ranks = jnp.where(masks > 0, ranks, -1)
    guest_out, guest_in = [], []
    for d in range(1, groups):
        guest_out.append(own_pairs(ranks[:, 2 * d - 2]))
        named = ranks[:, 2 * d - 1][None, :] == jnp.arange(most, dtype=kind)[:, None]
        guest_in.append(jnp.sum(jnp.where(named, row_of[None, :] + 1, 0), axis=1) - 1)
    distances = [1 << k for k in range(owners.bit_length() - 1)]

    def wider(value, step, *others):
        got = swap(value, "expert", step)
        return jnp.maximum(value, pinned(got, *others) if others else got)

    crowd = wider(jnp.full((8, 128), jnp.max(beyond.sum(0)), kind), 1)
    routes_own = relative(routes, 0, 1)
    valid_rows = relative(jnp.repeat(valid_flags.astype(F32), SEQ)[:, None], 0, 1)

    dense_x = list(pinned_all(dense_x, piece_second, local_row, crowd, *first_c, *first_l))
    dense_y, dense_c = spread(dense_x)
    start = pinned(start, *dense_x)
    after_attn, normed_first, packed_first, mixed_first, total_first = attend_forward(
        0, groups, place_ref, start, gain_rows[0], bias_rows[0], weights_first
    )
    crowd = wider(crowd, 4, after_attn)
    second_x = pinned_all(second_x, after_attn)
    dense_y = pinned_all(dense_y, *second_x)
    dense_l = fourth(dense_y)
    second_y, second_c = spread(second_x)
    weights_dense = [mlp_in, mlp_out] + joined(dense_x, dense_y, dense_c, dense_l)
    after_dense, normed_dense, dense_act, dense_slope = dense_forward(
        groups, place_ref, pinned(after_attn, crowd, *second_x), gain_rows[1], bias_rows[1], weights_dense
    )
    second_y = pinned_all(second_y, after_dense)
    weights_second = [attn_qkv, attn_out] + joined(second_x, second_y, second_c, fourth(second_y))
    crowd = wider(crowd, 8, after_dense)
    second = attend_forward(
        1, groups, place_ref, pinned(after_dense, crowd), gain_rows[2], bias_rows[2],
        weights_second, (gain_rows[3], bias_rows[3]),
    )
    after_second, normed_second, packed_second, mixed_second, total_second, normed_expert = second
    for step in [2] + distances[4:]:
        crowd = wider(crowd, step, after_second)
    logits = mm(normed_expert, router, NN)
    picker = routes_own[:, :, None] == jnp.arange(experts, dtype=kind)[None, None, :]
    chosen = jnp.sum(jnp.where(picker, logits[:, None, :], 0.0), axis=2)
    gate_vals = jax.nn.softmax(chosen, axis=1)
    gate_lines = gate_vals.T
    local_lines = local_row.T
    slot_ids = jnp.arange(slots, dtype=kind)

    def guests(count):
        ids = jnp.arange(count, dtype=kind)[:, None]
        return [(ids == g[None, :, 0], ids == g[None, :, 1]) for g in guest_out]

    def chosen_rows(count, rows):
        return [mm((a | b).astype(BF), rows, NN) for a, b in guests(count)]

    def returned_rows(count, rows):
        return [
            mm((g[:count, None] == slot_ids[None, :]).astype(BF), rows, NN).astype(BF)
            for g in guest_in
        ]

    def seats(count):
        return [g[None, :count] for g in guest_in]

    def over(rows):
        return [swap(x, "tensor", d + 1) for d, x in enumerate(rows)]

    def sized(branch, *operands):
        if few == most:
            return branch(few)(*operands)
        return lax.cond(crowd[0, 0] <= few, branch(few), branch(most), *operands)

    def grown(rows):
        return jnp.pad(rows, ((0, most - rows.shape[0]), (0, 0)))

    def across(rows):
        return lax.all_to_all(
            rows.reshape(owners, part, width), "expert", split_axis=0, concat_axis=0, tiled=True
        ).reshape(slots, width)

    images_valid = jnp.sum(valid_flags.astype(F32)).reshape(1)
    blank = jnp.zeros((2, own_rows), F32)

    def dispatch(count):
        def branch(rows):
            got = over([x.astype(BF) for x in chosen_rows(count, rows)])
            return dispatch_call(
                part, slots, images_valid, local_lines, blank, rows, seats(count), got
            )[0]

        return branch

    sent_rows = sized(dispatch, normed_expert)
    span = expert_in.shape[2]
    blocks = [expert_out[0, :, k : k + span] for k in range(0, width, span)]
    expert_own = pinned(jnp.concatenate([expert_in[0]] + blocks, 0), sent_rows)
    expert_parts = [x for w in [expert_own] + over_tensor(expert_own) for x in both_cores(w)]
    rows_in = across(sent_rows)
    valid_count = SEQ * jnp.sum(rows_in[part - 1 :: part, :1].astype(F32))
    teacher_rel = relative(teacher, 0, 1)
    scale = (local_rows * owners / valid_count) * valid_rows
    rows_in = pinned(rows_in, teacher_rel, scale)
    expert_rows, act, slope = expert_forward(rows_in, expert_parts)
    merged = across(expert_rows)

    outs = (shape(own_rows, width), shape(own_rows, width, kind=F32), shape(own_rows, width))

    def combine(count):
        def branch(rows):
            got = over(returned_rows(count, rows))
            results = combine_call(
                functools.partial(combine_kernel, groups - 1),
                (local_row, gate_vals, after_second, teacher_rel, scale, *guest_out),
                (rows, *got),
                outs,
            )
            return tuple(results) + tuple(grown(x) for x in got)

        return branch

    final_low, grad_final, grad_low, *lodged = sized(combine, merged)

    def dispatch_back(count):
        def branch(rows, merged, *lodged):
            sent, parts = [], []
            for (a, b), x, taken in zip(guests(count), lodged, chosen_rows(count, rows)):
                gates = jnp.sum(
                    jnp.where(a, gate_lines[:1], 0.0) + jnp.where(b, gate_lines[1:], 0.0),
                    axis=1,
                    keepdims=True,
                )
                sent.append((gates * taken).astype(BF))
                inner = jnp.sum(taken * x[:count].astype(F32), axis=1, keepdims=True)
                parts.append(grown(inner))
            results = dispatch_call(
                part, slots, images_valid, local_lines, gate_lines, rows, seats(count),
                over(sent), merged,
            )
            return tuple(results) + tuple(parts)

        return branch

    sent_back, grad_slot_gate, *grad_guest_gate = sized(
        dispatch_back, grad_low, merged, *lodged
    )
    final_far = over_tensor(pinned(final_low, sent_back))
    grad_out_rows = across(sent_back)
    grad_rows, grad_hidden = expert_backward(
        pinned(grad_out_rows, *final_far), slope, expert_parts
    )
    activations = absolute(jnp.concatenate([final_low] + list(pinned_all(final_far, grad_rows)), 0))
    grad_back = across(grad_rows)

    def start_groups(total):
        span = total.shape[1] // groups
        sent = [total[:, d * span : (d + 1) * span].astype(BF) for d in range(1, groups)]
        return total[:, :span], sent

    def start_rows(total):
        rows = total.shape[0] // 2
        return total[:rows], [total[rows:].astype(BF)]

    def cross(sent):
        return [swap(x, "tensor", d + 1) for d, x in enumerate(sent)]

    def along(sent, distance):
        return [swap(x, "expert", distance) for x in sent]

    def finish(keep, got, *after):
        total = keep.astype(F32)
        for x in got:
            total = total + (pinned(x, *after) if after else x).astype(F32)
        return total

    act, rows_in, grad_slot_gate = pinned_all((act, rows_in, grad_slot_gate), grad_rows)
    grad_own = []
    for choice in range(2):
        taken = slot_ids[:, None] == local_row[None, :, choice]
        total = jnp.sum(jnp.where(taken, grad_slot_gate, 0.0), axis=0)
        for pair, values in zip(guests(most), grad_guest_gate):
            total = total + jnp.sum(jnp.where(pair[choice], values, 0.0), axis=0)
        grad_own.append(total)
    grad_own = jnp.stack(grad_own, 1)
    span = expert_in.shape[2]
    sent = mark(expert_grads(act, grad_out_rows, width, span, 1))
    got_eo = along([sent], 1)[0]
    sent = mark(expert_grads(after(rows_in), grad_hidden, width, span, 1, None, False))
    got_ei = along([sent], 1)[0]

    def shares_of(total, rows):
        return total[:rows], [total[d * rows : (d + 1) * rows] for d in range(1, groups)]

    keep_eo, sent_eo = shares_of(
        mark(expert_grads(act, grad_out_rows, width, span, 0, after(got_eo))), span
    )
    got_eo = cross(sent_eo)
    keep_ei, sent_ei = shares_of(
        mark(expert_grads(rows_in, grad_hidden, width, span, 0, after(got_ei), False)), width
    )

    own_gates = gate_vals
    grad_chosen = own_gates * (grad_own - jnp.sum(own_gates * grad_own, axis=1, keepdims=True))
    grad_logits = jnp.sum(
        jnp.where(picker, grad_chosen[:, :, None], 0.0), axis=1
    ).astype(BF)
    grad_router = mm(grad_logits, normed_expert, TN)
    grad_back = pinned(grad_back, *sent_ei, *got_eo, grad_router)
    grad_expert_out = finish(keep_eo, got_eo)

    outs = (shape(1, width, kind=F32),) * 2 + (
        shape(own_rows, width, kind=F32), shape(own_rows, width),
    )

    def combine_back(count):
        def branch(rows):
            results = combine_call(
                functools.partial(combine_back_kernel, groups - 1),
                (local_row, after_second, grad_final, grad_logits, *guest_out),
                (rows, *over(returned_rows(count, rows)), router, gain_rows[3]),
                outs,
            )
            return tuple(results)

        return branch

    gain_four, bias_four, grad_second, low_second = sized(combine_back, grad_back)
    got_ei = cross([pinned(p, grad_second) for p in sent_ei])

    block = width // owners
    feature = jnp.arange(width, dtype=jnp.int32)

    def mover_of(distances):
        ahead, turned = feature // block, 0
        for distance in reversed(distances):
            turned = turned + distance * (ahead % 2)
            ahead = ahead // 2
        source = (turned ^ place) * block + feature % block
        return (source[:, None] == feature[None, :]).astype(BF)

    mover = mover_of(distances)
    turned_order = [1, 4, 2] + distances[3:]
    mover_turned = mover_of(turned_order)

    mark(grad_second)
    def arrive(keep, got):
        return finish(keep, [after(x) for x in got])

    grads_second, gain_three, bias_three, grad_dense, low_dense = attend_backward(
        1, groups, place_ref, grad_second, after_dense, gain_rows[2], packed_second,
        total_second, weights_second, (F32, BF),
    )
    mark(grad_dense)
    got_ei = [after(x) for x in got_ei]
    keep_a, send_a = weight_grads(
        groups,
        mover,
        [(pinned(normed_second, *got_ei), grads_second), (low_second, mixed_second)],
    )
    mark(send_a)
    got_a = along([send_a], 1)
    low_dense = after(low_dense)
    keep_b, send_b = weight_grads(groups, mover, [(low_dense, dense_act)])
    mark(send_b)
    got_b = along([send_b], 1)
    keep_a, sent_a = start_groups(arrive(keep_a, got_a).astype(BF))
    mark(sent_a[0])
    got_a = cross(sent_a)
    grad_expert_in = finish(keep_ei, got_ei)
    grad_hidden, gain_two, bias_two, grad_attn, low_first = dense_backward(
        groups, place_ref, after(grad_dense), after_attn, gain_rows[1], dense_slope, weights_dense,
    )
    mark(grad_attn)
    keep_b, sent_b = start_rows(arrive(keep_b, got_b).astype(BF))
    mark(sent_b[0])
    got_b = along(sent_b, 2)

    got_a = [after(x) for x in got_a]
    stats = [gain_two, gain_three, gain_four, bias_two, bias_three, bias_four]
    keep_c, send_c = weight_grads(
        groups,
        mover_turned,
        [
            (pinned(normed_dense, *got_a), grad_hidden),
            (low_first, mixed_first),
        ],
        stats + [grad_router],
    )
    mark(send_c)
    got_c = along([send_c], 1)
    keep_a, sent_a = start_rows(arrive(keep_a, got_a).astype(BF))
    mark(sent_a[0])
    got_a = along(sent_a, 2)
    keep_c, sent_c = start_rows(arrive(keep_c, got_c).astype(BF))
    mark(sent_c[0])
    got_c = along(sent_c, 4)
    grads_first, gain_one, bias_one, grad_start = attend_backward(
        0, groups, place_ref, after(grad_attn), start, gain_rows[0], packed_first, total_first,
        weights_first, (BF,),
    )
    mark(grad_start)
    start_far = over_tensor(grad_start)
    got_b = [after(x) for x in got_b]
    keep_d, send_d = weight_grads(
        groups,
        mover,
        [(pinned(normed_first, *got_b), grads_first)],
        [gain_one, bias_one],
    )
    mark(send_d)
    got_d = along([send_d], 1)
    keep_b, sent_b = start_groups(arrive(keep_b, got_b).astype(BF))
    mark(sent_b[0])
    got_b = cross(sent_b)
    keep_a, sent_a = start_rows(arrive(keep_a, got_a))
    mark(sent_a[0])
    got_a = along(sent_a, 4)
    total_c = mark(arrive(keep_c, got_c).astype(BF))
    total_d = arrive(keep_d, got_d).astype(BF)
    span = total_d.shape[1] // groups
    cut = attn_out.shape[1]
    far_d = [
        jnp.concatenate([total_d[:, d * span : d * span + cut] for d in range(groups)], 1),
        jnp.concatenate([total_d[:, d * span + cut : (d + 1) * span] for d in range(groups)], 1),
    ]
    keep_d, sent_d = start_groups(far_d[0])
    keep_e, sent_e = start_rows(far_d[1])
    mark(sent_e[0])
    got_d = cross(sent_d)
    got_e = along(sent_e, 2)
    keep_c, sent_c = start_rows(after(total_c))
    mark(sent_c[0])
    got_c = along(sent_c, 2)
    start_far = [after(x) for x in start_far]
    input_grad = mark(absolute(jnp.concatenate([grad_start] + start_far, 0)))
    keep_a, sent_a = start_rows(arrive(keep_a, got_a))
    mark(sent_a[0])
    got_a = along(sent_a, 8)
    keep_b, sent_b = start_rows(arrive(keep_b, got_b))
    mark(sent_b[0])
    got_b = along(sent_b, 4)
    keep_d, sent_d = start_rows(arrive(keep_d, got_d))
    mark(sent_d[0])
    got_d = along(sent_d, 2)
    keep_e, sent_e = start_groups(arrive(keep_e, got_e))
    mark(sent_e[0])
    got_e = cross(sent_e)
    keep_c, sent_c = start_groups(arrive(keep_c, got_c))
    mark(sent_c[0])
    got_c = cross(sent_c)
    total_a = mark(arrive(keep_a, got_a))
    keep_b, sent_b = start_rows(arrive(keep_b, got_b))
    mark(sent_b[0])
    got_b = along(sent_b, 8)
    total_d = arrive(keep_d, got_d)
    total_e = arrive(keep_e, got_e)
    keep_d, sent_d = start_rows(jnp.concatenate([total_d, total_e], 1))
    mark(sent_d[0])
    got_d = along(sent_d, 4)
    keep_c, sent_c = start_rows(arrive(keep_c, got_c))
    mark(sent_c[0])
    got_c = along(sent_c, 8)
    total_b = mark(arrive(keep_b, got_b))
    keep_d, sent_d = start_rows(arrive(keep_d, got_d))
    mark(sent_d[0])
    got_d = along(sent_d, 8)
    total_c = mark(arrive(keep_c, got_c))
    total_d = arrive(keep_d, got_d)
    joint = jnp.concatenate([total_a, total_b, total_c, total_d], 1)
    step = 16
    while step < owners:
        keep, sent = start_rows(joint)
        joint = finish(keep, along(sent, step))
        step *= 2
    spans = [attn_out.shape[1], mlp_in.shape[1], -(-(6 + experts) // 128) * 128]
    widths = [4 * spans[0], spans[1], spans[1], spans[0], spans[2], 3 * spans[0], 128]
    taken, at = [], 0
    for span in widths:
        taken.append(joint[:, at : at + span])
        at += span
    two, grad_mlp_out, grad_mlp_in = taken[0], taken[1].T, taken[2]
    one = jnp.concatenate([taken[5], taken[3]], 1)
    lines, last_lines = taken[4], taken[6]
    joint_small = jnp.concatenate(
        [last_lines[:, :1], lines[:, :3], last_lines[:, 1:2], lines[:, 3 : 6 + experts]], 1
    )

    def split_attention(total):
        span = total.shape[1] // 4
        return jnp.stack([total[:, s * span : (s + 1) * span] for s in range(3)]), total[:, -span:].T

    qkv_one, out_one = split_attention(one)
    qkv_two, out_two = split_attention(two)
    small = joint_small.T
    return (
        activations,
        input_grad,
        small[:4],
        small[4:7],
        small[7],
        jnp.stack([qkv_one, qkv_two]),
        jnp.stack([out_one, out_two]),
        grad_mlp_in,
        grad_mlp_out,
        small[8:].T,
        grad_expert_in[None],
        grad_expert_out[None],
    )


def solution(mesh):
    in_specs = (
        P("expert", None),
        P("expert", None),
        P("expert"),
        P("expert", None),
        P(),
        P(),
        P(),
        P(None, None, None, "tensor"),
        P(None, "tensor", None),
        P(None, "tensor"),
        P("tensor", None),
        P(),
        P("expert", None, "tensor"),
        P("expert", "tensor", None),
    )
    out_specs = (
        P("expert", None),
        P("expert", None),
        P(None, "expert"),
        P(None, "expert"),
        P("expert"),
        P(None, None, "expert", "tensor"),
        P(None, "tensor", "expert"),
        P("expert", "tensor"),
        P("tensor", "expert"),
        P("expert", None),
        P("expert", None, "tensor"),
        P("expert", "tensor", None),
    )
    return jax.shard_map(body, mesh=mesh, in_specs=in_specs, out_specs=out_specs, check_vma=False)
```

time: 1230 us -> 766 us (0.62)
  matrix products: 315 us -> 7.87 us
  Pallas kernels: 0 us -> 273 us
  waiting for transfers between devices: 471 us -> 255 us
  local copies, waits for them, and re-layouts: 203 us -> 63.5 us
  other arithmetic: 94.8 us -> 63.2 us
  starting transfers between devices: 115 us -> 93.9 us
  between operations: 18.9 us -> 3.44 us
    pallas_call x0 -> x20, Pallas kernels: none -> 273 us  [the longest x6 116 us: dense_call(): pl.pallas_call(kernel, grid=(rows[0].shape[-2] // ROWS,), in_specs=specs,...]
    dot_general x73 -> x6, matrix products: 274 us -> 7.87 us  [mm(): return lax.dot_general(a, b, (dims, ((), ())), preferred_element_type=F32)]
    ppermute x70 -> x51, waiting for transfers between devices: 349 us -> 175 us  [swap(): return lax.ppermute(value, axis, [(k, k ^ distance) for k in range(size)])]
    reshape x24 -> x2, local copies, waits for them, and re-layouts: 57.9 us -> 0.17 us  [the longest x1 0.09 us: body(): earlier = (jnp.cumsum(both, axis=0) - both).reshape(-1, experts, groups)]
    convert_element_type x16 -> x0, local copies, waits for them, and re-layouts: 43.3 us -> none  [the longest x12 32.5 us: attend_backward(): grads = [g.reshape(grad_low.shape[0], -1).astype(BF) for g in (gq, gk, gv)]]
    dot_general x12 -> x0, matrix products: 41.8 us -> none  [the longest x2 13.6 us: attend_backward(): jnp.einsum('bqhe,bkhe->bhqk', grad_mixed, v, preferred_element_type=F32)]
    unnamed x2 -> x0, waiting for transfers between devices: 31.5 us -> none
    slice x52 -> x41, local copies, waits for them, and re-layouts: 43.6 us -> 17.9 us  [the longest x11 5.19 us: start_rows(): return (total[:rows], [total[rows:].astype(BF)])]
  transfers between devices with their start and end apart: 75 -> 55, of which waited for: 41 -> 24; matrix products, arithmetic and copies ran while one was open for 20% -> 14% of each run, Pallas kernels for 0% -> 22%
where the time goes in v2:
time: 766 us; the launch traced here: 760 us
  Pallas kernels  273 us (36%)
  waiting for transfers between devices  255 us (33%)
  starting transfers between devices  93.9 us (12%)
  local copies, waits for them, and re-layouts  63.5 us (8%)
  other arithmetic  63.2 us (8%)
  matrix products  7.87 us (1%)
    ppermute x51, waiting for transfers between devices, swap(): return lax.ppermute(value, axis, [(k, k ^ distance) for k in range(size)])  175 us
    pallas_call x6, Pallas kernels, dense_call(): pl.pallas_call(kernel, grid=(rows[0].shape[-2] // ROWS,), in_specs=specs,...  116 us
    all_to_all x4, waiting for transfers between devices, across(): lax.all_to_all(rows.reshape(owners, part, width), 'expert', split_axis=0,...  79.3 us
    ppermute x51, starting transfers between devices, swap(): return lax.ppermute(value, axis, [(k, k ^ distance) for k in range(size)])  55.3 us
    pallas_call x2, Pallas kernels, expert_call(): pl.pallas_call(kernel, grid=(count // tile,), in_specs=[image_spec(tile,...  54.2 us
    pallas_call x4, Pallas kernels, weight_grads(): pl.pallas_call(functools.partial(weight_kernel, groups, len(stats)), in_s...  41.8 us
    all_to_all x4, starting transfers between devices, across(): lax.all_to_all(rows.reshape(owners, part, width), 'expert', split_axis=0,...  38.6 us
    pallas_call x4, Pallas kernels, expert_grads(): pl.pallas_call(outer_kernel, grid=(count,), in_specs=([cut, whole] if cut...  34.2 us
  transfers between devices with their start and end apart: 55, of which 24 were waited for; matrix products, arithmetic and copies ran while one was open for 14% of the time, Pallas kernels for 22%

profile of v2, /device:TPU:0, one launch (start us, length us, event | category | flops | bytes accessed | tf_op | source)
XLA Modules:
  0.0 760.3 jit_solution(7790569186528753068)
XLA Ops:
  16.0 5.1 collective-permute-done.8.refs_2_
  24.2 4.6 reduce-window.14
  41.9 20.5 %collective-permute-done.11.refs_2_ = bf16[384,1536]{1,0:T(8,128)(2,1)S(1)} collective-permute-done((bf16[384,1536]{1,0:T(8,128)(2,1)}, bf16[384,1536]{1,0:T(8,128)(2,1)S(1)}, u32[]{:S(2)}, u32[]{:S(2)}) %collective-permute-start.11) | collective-permute-done | bytes 1179680 | tf_op jit(solution)/shard_map/ppermute | solution.py:30
  65.4 13.4 %shard_map.229 = (f32[624,768]{1,0:T(8,128)}, bf16[624,768]{1,0:T(8,128)(2,1)}, bf16[3,624,768]{2,1,0:T(8,128)(2,1)}, bf16[624,768]{1,0:T(8,128)(2,1)}, f32[624,128]{1,0:T(8,128)}) custom-call(s32[1]{0:T(128)} %bitcast.7.place_ref, f32[624,768]{1,0:T(8,128)} %bitcast_convert_fusion.x_ref, f32[1,768]{1,0:T(1,128)} %get-tuple-element.813.gain_ref, ...), custom_call_target="tpu_custom_call" | custom-call | flops 668624512 | bytes 3204710 | tf_op jit(solution)/shard_map/pallas_call | solution.py:316
  78.8 10.8 %collective-permute-done.18.refs_4_ = bf16[384,1536]{1,0:T(8,128)(2,1)S(1)} collective-permute-done((bf16[384,1536]{1,0:T(8,128)(2,1)S(1)}, bf16[384,1536]{1,0:T(8,128)(2,1)S(1)}, u32[]{:S(2)}, u32[]{:S(2)}) %collective-permute-start.18) | collective-permute-done | bytes 1179680 | tf_op jit(solution)/shard_map/ppermute | solution.py:30
  98.8 15.5 %shard_map.230 = (f32[624,768]{1,0:T(8,128)}, bf16[624,768]{1,0:T(8,128)(2,1)}, bf16[624,3072]{1,0:T(8,128)(2,1)}, bf16[624,3072]{1,0:T(8,128)(2,1)}) custom-call(s32[1]{0:T(128)} %bitcast.7.place_ref, f32[624,768]{1,0:T(8,128)} %get-tuple-element.345.x_ref, f32[1,768]{1,0:T(1,128)} %get-tuple-element.814.gain_ref, f32[1,768]{1,0:T(1,128)} %get-tuple-element.799.bias_ref, ...), custom_call_target="tpu_custom_call" | custom-call | flops 1177760512 | bytes 4379443 | tf_op jit(solution)/shard_map/pallas_call | solution.py:316
  122.4 23.7 %shard_map.231 = (f32[624,768]{1,0:T(8,128)}, bf16[624,768]{1,0:T(8,128)(2,1)}, bf16[3,624,768]{2,1,0:T(8,128)(2,1)}, bf16[624,768]{1,0:T(8,128)(2,1)}, f32[624,128]{1,0:T(8,128)}, /*index=5*/bf16[624,768]{1,0:T(8,128)(2,1)}) custom-call(s32[1]{0:T(128)} %bitcast.7.place_ref, f32[624,768]{1,0:T(8,128)} %get-tuple-element.349.x_ref, ...), custom_call_target="tpu_custom_call" | custom-call | flops 668624512 | bytes 3396403 | tf_op jit(solution)/shard_map/pallas_call | solution.py:316
  147.3 12.7 %conditional.4 = (bf16[1792,768]{1,0:T(8,128)(2,1)S(1)}) conditional(s32[]{:T(128)} %bitcast.12, (s32[528]{0:T(1024)S(1)}, s32[624,2]{0,1:T(2,128)S(1)}, bf16[624,768]{1,0:T(8,128)(2,1)}, f32[1]{0:T(128)}, s32[2,624]{1,0:T(2,128)S(1)}) %tuple.264, (s32[528]{0:T(1024)S(1)}, s32[624,2]{0,1:T(2,128)S(1)}, bf16[624,768]{1,0:T(8,128)(2,1)}, ...), branch_computations={%region_22.23_spmd, %region_23.24_spmd} | conditional | flops 850976384 | bytes 9024003 | solution.py:886
  154.2 5.8 branch_1_fun.4
  161.6 5.0 all-to-all-start
  171.4 52.3 %collective-permute-done.25.refs_2_ = bf16[1536,768]{1,0:T(8,128)(2,1)} collective-permute-done((bf16[1536,768]{1,0:T(8,128)(2,1)}, bf16[1536,768]{1,0:T(8,128)(2,1)}, u32[]{:S(2)}, u32[]{:S(2)}) %collective-permute-start.25) | collective-permute-done | bytes 2359328 | tf_op jit(solution)/shard_map/ppermute | solution.py:30
  223.7 3.2 reshape.655
  230.9 28.1 %shard_map.232 = (bf16[1792,768]{1,0:T(8,128)(2,1)}, bf16[1792,3072]{1,0:T(8,128)(2,1)}, bf16[1792,3072]{1,0:T(8,128)(2,1)}) custom-call(bf16[1792,768]{1,0:T(8,128)(2,1)} %bitcast.130, bf16[1536,768]{1,0:T(8,128)(2,1)} %pad_maximum_fusion.refs_0_, bf16[1536,768]{1,0:T(8,128)(2,1)} %collective-permute-done.24.refs_1_, ...), custom_call_target="tpu_custom_call" | custom-call | flops 3382286848 | bytes 7392460 | tf_op jit(solution)/shard_map/pallas_call | solution.py:445
  259.0 6.0 all-to-all-start.1
  266.9 50.6 %all-to-all-done.1 = bf16[16,112,768]{2,1,0:T(8,128)(2,1)S(1)} async-done(((bf16[16,112,768]{2,1,0:T(8,128)(2,1)}), bf16[16,112,768]{2,1,0:T(8,128)(2,1)S(1)}, u32[]{:S(2)}, u32[]{:S(2)}) %all-to-all-start.1) | async-done | bytes 2752544 | tf_op jit(solution)/shard_map/all_to_all | solution.py:892
  317.5 13.9 %conditional.5 = (bf16[624,768]{1,0:T(8,128)(2,1)}, f32[624,768]{1,0:T(8,128)}, bf16[624,768]{1,0:T(8,128)(2,1)}, bf16[528,768]{1,0:T(8,128)(2,1)}) conditional(s32[]{:T(128)} %bitcast.12, (s32[528]{0:T(1024)S(1)}, s32[1792]{0:T(1024)S(1)}, bf16[1792,768]{1,0:T(8,128)(2,1)S(1)}, s32[624,2]{0,1:T(2,128)S(1)}, f32[624,2]{0,1:T(2,128)S(1)}, ...), branch_computations={%region_28.29_spmd, %region_29.30_spmd} | conditional | flops 1798191488 | bytes 8909896 | solution.py:886
  324.9 6.5 branch_1_fun.5
  331.4 14.9 %conditional.6 = (bf16[1792,768]{1,0:T(8,128)(2,1)}, f32[1792,1]{1,0:T(8,128)}, f32[528,1]{0,1:T(1,128)S(1)}) conditional(s32[]{:T(128)} %bitcast.12, (s32[528]{0:T(1024)S(1)}, s32[624,2]{0,1:T(2,128)S(1)}, f32[2,624]{1,0:T(2,128)S(1)}, bf16[624,768]{1,0:T(8,128)(2,1)}, f32[1]{0:T(128)}, /*index=5*/s32[2,624]{1,0:T(2,128)S(1)}, ...), branch_computations={%region_30.33_spmd, %region_33.36_spmd} | conditional | flops 854574208 | bytes 6616499 | solution.py:886
  338.7 7.6 %branch_1_fun.6 = (bf16[1792,768]{1,0:T(8,128)(2,1)}, f32[1792,1]{1,0:T(8,128)}) custom-call(f32[1]{0:T(128)} %get-tuple-element.175.extra_ref, s32[2,624]{1,0:T(2,128)S(1)} %get-tuple-element.176.lines_ref, f32[2,624]{1,0:T(2,128)S(1)} %get-tuple-element.177.gates_ref, bf16[624,768]{1,0:T(8,128)(2,1)} %get-tuple-element.178.rows_ref, ...), custom_call_target="tpu_custom_call" | custom-call | flops 343513504 | bytes 742195 | tf_op jit(solution)/shard_map/cond/branch_1_fun/pallas_call | solution.py:554
  346.3 13.4 %all-to-all-start.2 = ((bf16[16,112,768]{2,1,0:T(8,128)(2,1)}), bf16[16,112,768]{2,1,0:T(8,128)(2,1)S(1)}, u32[]{:S(2)}, u32[]{:S(2)}) async-start(bf16[16,112,768]{2,1,0:T(8,128)(2,1)} %bitcast.140), calls=%async_computation.2 | async-start | bytes 5505024 | tf_op jit(solution)/shard_map/all_to_all | solution.py:892
  361.1 22.5 %collective-permute-done.27 = bf16[624,768]{1,0:T(8,128)(2,1)} collective-permute-done((bf16[624,768]{1,0:T(8,128)(2,1)}, bf16[624,768]{1,0:T(8,128)(2,1)}, u32[]{:S(2)}, u32[]{:S(2)}) %collective-permute-start.27) | collective-permute-done | bytes 958496 | tf_op jit(solution)/shard_map/ppermute | solution.py:30
  383.6 28.7 %all-to-all-done.2 = bf16[16,112,768]{2,1,0:T(8,128)(2,1)S(1)} async-done(((bf16[16,112,768]{2,1,0:T(8,128)(2,1)}), bf16[16,112,768]{2,1,0:T(8,128)(2,1)S(1)}, u32[]{:S(2)}, u32[]{:S(2)}) %all-to-all-start.2) | async-done | bytes 2752544 | tf_op jit(solution)/shard_map/all_to_all | solution.py:892
  413.8 26.2 %shard_map.233 = (bf16[1792,768]{1,0:T(8,128)(2,1)}, bf16[1792,3072]{1,0:T(8,128)(2,1)}) custom-call(bf16[1792,768]{1,0:T(8,128)(2,1)} %bitcast.126, bf16[1792,3072]{1,0:T(8,128)(2,1)} %get-tuple-element.363.slope_ref, bf16[1536,768]{1,0:T(8,128)(2,1)} %pad_maximum_fusion.refs_0_, bf16[1536,768]{1,0:T(8,128)(2,1)} %collective-permute-done.24.refs_1_, ...), custom_call_target="tpu_custom_call" | custom-call | flops 3382286848 | bytes 7392460 | tf_op jit(solution)/shard_map/pallas_call | solution.py:445
  440.0 14.3 %all-to-all-start.3 = ((bf16[16,112,768]{2,1,0:T(8,128)(2,1)}), bf16[16,112,768]{2,1,0:T(8,128)(2,1)S(1)}, u32[]{:S(2)}, u32[]{:S(2)}) async-start(bf16[16,112,768]{2,1,0:T(8,128)(2,1)} %bitcast.138), calls=%async_computation.3 | async-start | bytes 5505024 | tf_op jit(solution)/shard_map/all_to_all | solution.py:892
  454.3 8.4 %shard_map.234 = bf16[1536,768]{1,0:T(8,128)(2,1)} custom-call(bf16[1792,3072]{1,0:T(8,128)(2,1)} %get-tuple-element.370.left_ref, bf16[1792,768]{1,0:T(8,128)(2,1)} %bitcast.127), custom_call_target="tpu_custom_call" | custom-call | flops 845571712 | bytes 3696230 | tf_op jit(solution)/shard_map/pallas_call | solution.py:628
  463.1 8.3 %shard_map.235 = bf16[1536,768]{1,0:T(8,128)(2,1)} custom-call(bf16[1792,768]{1,0:T(8,128)(2,1)} %bitcast.131, bf16[1792,3072]{1,0:T(8,128)(2,1)} %get-tuple-element.369.right_ref), custom_call_target="tpu_custom_call" | custom-call | flops 845571712 | bytes 3696230 | tf_op jit(solution)/shard_map/pallas_call | solution.py:628
  471.6 8.7 %shard_map.236 = bf16[1536,768]{1,0:T(8,128)(2,1)} custom-call(bf16[1792,3072]{1,0:T(8,128)(2,1)} %get-tuple-element.370.left_ref, bf16[1792,768]{1,0:T(8,128)(2,1)} %bitcast.128, bf16[1536,768]{1,0:T(8,128)(2,1)} %collective-permute-done.29.refs_0_), custom_call_target="tpu_custom_call" | custom-call | flops 845571712 | bytes 3696230 | tf_op jit(solution)/shard_map/pallas_call | solution.py:628
  489.3 8.7 %shard_map.237 = bf16[1536,768]{1,0:T(8,128)(2,1)} custom-call(bf16[1792,768]{1,0:T(8,128)(2,1)} %bitcast.132, bf16[1792,3072]{1,0:T(8,128)(2,1)} %get-tuple-element.369.right_ref, bf16[1536,768]{1,0:T(8,128)(2,1)} %collective-permute-done.28.refs_0_), custom_call_target="tpu_custom_call" | custom-call | flops 845571712 | bytes 3696230 | tf_op jit(solution)/shard_map/pallas_call | solution.py:628
  500.4 11.0 %collective-permute-done.30 = bf16[768,768]{1,0:T(8,128)(2,1)} collective-permute-done((bf16[768,768]{1,0:T(8,128)(2,1)}, bf16[768,768]{1,0:T(8,128)(2,1)}, u32[]{:S(2)}, u32[]{:S(2)}) %collective-permute-start.30) | collective-permute-done | bytes 1179680 | tf_op jit(solution)/shard_map/ppermute | solution.py:30
  511.3 13.0 %conditional.7 = ((f32[1,768]{1,0:T(1,128)S(1)}, f32[1,768]{1,0:T(1,128)}, f32[624,768]{1,0:T(8,128)}, bf16[624,768]{1,0:T(8,128)(2,1)})) conditional(s32[]{:T(128)} %bitcast.12, (s32[528]{0:T(1024)S(1)}, s32[1792]{0:T(1024)S(1)}, bf16[1792,768]{1,0:T(8,128)(2,1)S(1)}, s32[624,2]{0,1:T(2,128)S(1)}, f32[624,768]{1,0:T(8,128)}, ...), branch_computations={%region_42.43_spmd, %region_43.44_spmd} | conditional | flops 1798191488 | bytes 8944240 | solution.py:886
  517.6 6.8 branch_1_fun.7
  527.0 23.3 %shard_map.238 = (bf16[3,624,768]{2,1,0:T(8,128)(2,1)}, f32[1,768]{1,0:T(1,128)}, f32[1,768]{1,0:T(1,128)}, f32[624,768]{1,0:T(8,128)}, bf16[624,768]{1,0:T(8,128)(2,1)}) custom-call(s32[1]{0:T(128)} %bitcast.7.place_ref, f32[624,768]{1,0:T(8,128)} %get-tuple-element.378.grad_ref, f32[624,768]{1,0:T(8,128)} %get-tuple-element.349.x_ref, ...), custom_call_target="tpu_custom_call" | custom-call | flops 788240768 | bytes 3972710 | tf_op jit(solution)/shard_map/pallas_call | solution.py:316
  551.9 10.9 %shard_map.239 = (bf16[384,3072]{1,0:T(8,128)(2,1)}, bf16[384,3072]{1,0:T(8,128)(2,1)}) custom-call(bf16[768,768]{1,0:T(8,128)(2,1)} %fusion.38.mover_ref, bf16[624,768]{1,0:T(8,128)(2,1)} %get-tuple-element.385.refs_0_, bf16[624,768]{1,0:T(8,128)(2,1)S(1)} %copy-done.31, bf16[3,624,768]{2,1,0:T(8,128)(2,1)} %get-tuple-element.387.refs_2_, ...), custom_call_target="tpu_custom_call" | custom-call | flops 588880256 | bytes 2329804 | tf_op jit(solution)/shard_map/pallas_call | solution.py:510
  562.8 9.7 %shard_map.240 = (bf16[384,3072]{1,0:T(8,128)(2,1)}, bf16[384,3072]{1,0:T(8,128)(2,1)}) custom-call(bf16[768,768]{1,0:T(8,128)(2,1)} %fusion.38.mover_ref, bf16[624,768]{1,0:T(8,128)(2,1)} %get-tuple-element.392.refs_0_, bf16[624,3072]{1,0:T(8,128)(2,1)} %get-tuple-element.393.refs_1_), custom_call_target="tpu_custom_call" | custom-call | flops 588880256 | bytes 2138112 | tf_op jit(solution)/shard_map/pallas_call | solution.py:510
  580.1 17.5 %shard_map.241 = (bf16[624,3072]{1,0:T(8,128)(2,1)}, f32[1,768]{1,0:T(1,128)}, f32[1,768]{1,0:T(1,128)}, f32[624,768]{1,0:T(8,128)}, bf16[624,768]{1,0:T(8,128)(2,1)}) custom-call(s32[1]{0:T(128)} %bitcast.7.place_ref, f32[624,768]{1,0:T(8,128)} %get-tuple-element.396.grad_ref, f32[624,768]{1,0:T(8,128)} %get-tuple-element.345.x_ref, ...), custom_call_target="tpu_custom_call" | custom-call | flops 1177760512 | bytes 4764057 | tf_op jit(solution)/shard_map/pallas_call | solution.py:316
  602.7 3.5 collective-permute-done.33
  606.2 12.8 %shard_map.242 = (bf16[384,4096]{1,0:T(8,128)(2,1)}, bf16[384,4096]{1,0:T(8,128)(2,1)}) custom-call(bf16[768,768]{1,0:T(8,128)(2,1)} %fusion.39.mover_ref, f32[1,768]{1,0:T(1,128)} %get-tuple-element.399.refs_0_, f32[1,768]{1,0:T(1,128)} %get-tuple-element.400.refs_1_, f32[1,768]{1,0:T(1,128)S(1)} %get-tuple-element.401.refs_2_, ...), custom_call_target="tpu_custom_call" | custom-call | flops 785173696 | bytes 2840371 | tf_op jit(solution)/shard_map/pallas_call | solution.py:510
  621.9 3.4 reshape.663
  635.6 6.9 collective-permute-start.37
  645.2 22.8 %shard_map.243 = (bf16[3,624,768]{2,1,0:T(8,128)(2,1)}, f32[1,768]{1,0:T(1,128)}, f32[1,768]{1,0:T(1,128)}, bf16[624,768]{1,0:T(8,128)(2,1)}) custom-call(s32[1]{0:T(128)} %bitcast.7.place_ref, f32[624,768]{1,0:T(8,128)} %get-tuple-element.417.grad_ref, f32[624,768]{1,0:T(8,128)} %bitcast_convert_fusion.x_ref, ...), custom_call_target="tpu_custom_call" | custom-call | flops 788240768 | bytes 3589324 | tf_op jit(solution)/shard_map/pallas_call | solution.py:316
  668.1 8.5 %shard_map.244 = (bf16[384,2560]{1,0:T(8,128)(2,1)}, bf16[384,2560]{1,0:T(8,128)(2,1)}) custom-call(bf16[768,768]{1,0:T(8,128)(2,1)} %fusion.38.mover_ref, f32[1,768]{1,0:T(1,128)} %get-tuple-element.422.refs_0_, f32[1,768]{1,0:T(1,128)} %get-tuple-element.423.refs_1_, bf16[624,768]{1,0:T(8,128)(2,1)} %get-tuple-element.425.refs_2_, ...), custom_call_target="tpu_custom_call" | custom-call | flops 490733568 | bytes 1789747 | tf_op jit(solution)/shard_map/pallas_call | solution.py:510
  692.1 8.7 %collective-permute-done.36 = bf16[624,768]{1,0:T(8,128)(2,1)S(1)} collective-permute-done((bf16[624,768]{1,0:T(8,128)(2,1)}, bf16[624,768]{1,0:T(8,128)(2,1)S(1)}, u32[]{:S(2)}, u32[]{:S(2)}) %collective-permute-start.36) | collective-permute-done | bytes 958496 | tf_op jit(solution)/shard_map/ppermute | solution.py:30
  702.5 3.2 reshape.667
  708.5 4.6 collective-permute-done.42
  716.5 5.5 collective-permute-done.41
  729.7 5.9 collective-permute-done.49
  736.7 5.0 collective-permute-done.52
  745.6 9.0 %collective-permute-done.54 = bf16[48,2048]{1,0:T(8,128)(2,1)S(1)} collective-permute-done((bf16[48,2048]{1,0:T(8,128)(2,1)S(1)}, bf16[48,2048]{1,0:T(8,128)(2,1)S(1)}, u32[]{:S(2)}, u32[]{:S(2)}) %collective-permute-start.54) | collective-permute-done | bytes 196640 | tf_op jit(solution)/shard_map/ppermute | solution.py:30
  (411 shorter events, 179.6 us)
Async XLA Ops:
  4.6 16.5 %collective-permute-start.8 = (bf16[768,384]{1,0:T(8,128)(2,1)}, bf16[768,384]{1,0:T(8,128)(2,1)S(1)}, u32[]{:S(2)}, u32[]{:S(2)}) collective-permute-start(bf16[768,384]{1,0:T(8,128)(2,1)} %pad_maximum_fusion.6), channel_id=1, source_target_pairs={{0,1},{1,0},{2,3},{3,2},{4,5},{5,4},{6,7},{7,6},{8,9},{9,8},{10,11... | collective-permute-start | bytes 1769480 | tf_op jit(solution)/shard_map/ppermute | solution.py:30
  21.1 14.5 %collective-permute-start.12 = (bf16[768,384]{1,0:T(8,128)(2,1)S(1)}, bf16[768,384]{1,0:T(8,128)(2,1)S(1)}, u32[]{:S(2)}, u32[]{:S(2)}) collective-permute-start(bf16[768,384]{1,0:T(8,128)(2,1)S(1)} %collective-permute-done.8.refs_2_), channel_id=1, source_target_pairs={{0,4},{2,6},{4,0},{6,2},{8,12},{10,14},{12,8},{14,10},{16,20},{18,... | collective-permute-start | bytes 1769480 | tf_op jit(solution)/shard_map/ppermute | solution.py:30
  22.8 18.3 %collective-permute-start.13 = (bf16[768,384]{1,0:T(8,128)(2,1)S(1)}, bf16[768,384]{1,0:T(8,128)(2,1)S(1)}, u32[]{:S(2)}, u32[]{:S(2)}) collective-permute-start(bf16[768,384]{1,0:T(8,128)(2,1)S(1)} %collective-permute-done.8.refs_2_), channel_id=1, source_target_pairs={{0,2},{2,0},{4,6},{6,4},{8,10},{10,8},{12,14},{14,12},{16,18},{18,... | collective-permute-start | bytes 1769480 | tf_op jit(solution)/shard_map/ppermute | solution.py:30
  33.5 29.0 %collective-permute-start.11 = (bf16[384,1536]{1,0:T(8,128)(2,1)}, bf16[384,1536]{1,0:T(8,128)(2,1)S(1)}, u32[]{:S(2)}, u32[]{:S(2)}) collective-permute-start(bf16[384,1536]{1,0:T(8,128)(2,1)} %maximum_maximum_fusion), channel_id=1, source_target_pairs={{0,1},{1,0},{2,3},{3,2},{4,5},{5,4},{6,7},{7,6},{8,9},{9,8},{10,11... | collective-permute-start | bytes 3538952 | tf_op jit(solution)/shard_map/ppermute | solution.py:30
  39.7 39.2 %collective-permute-start.16 = (bf16[768,384]{1,0:T(8,128)(2,1)}, bf16[768,384]{1,0:T(8,128)(2,1)}, u32[]{:S(2)}, u32[]{:S(2)}) collective-permute-start(bf16[768,384]{1,0:T(8,128)(2,1)} %pad_maximum_fusion.7), channel_id=1, source_target_pairs={{0,1},{1,0},{2,3},{3,2},{4,5},{5,4},{6,7},{7,6},{8,9},{9,8},{10,11... | collective-permute-start | bytes 1769480 | tf_op jit(solution)/shard_map/ppermute | solution.py:30
  62.4 27.2 %collective-permute-start.18 = (bf16[384,1536]{1,0:T(8,128)(2,1)S(1)}, bf16[384,1536]{1,0:T(8,128)(2,1)S(1)}, u32[]{:S(2)}, u32[]{:S(2)}) collective-permute-start(bf16[384,1536]{1,0:T(8,128)(2,1)S(1)} %collective-permute-done.11.refs_2_), channel_id=1, source_target_pairs={{0,4},{2,6},{4,0},{6,2},{8,12},{10,14},{12,8},{14,10},{16,20},{18,... | collective-permute-start | bytes 3538952 | tf_op jit(solution)/shard_map/ppermute | solution.py:30
  65.4 32.0 %collective-permute-start.17 = (bf16[384,1536]{1,0:T(8,128)(2,1)S(1)}, bf16[384,1536]{1,0:T(8,128)(2,1)S(1)}, u32[]{:S(2)}, u32[]{:S(2)}) collective-permute-start(bf16[384,1536]{1,0:T(8,128)(2,1)S(1)} %collective-permute-done.11.refs_2_), channel_id=1, source_target_pairs={{0,2},{2,0},{4,6},{6,4},{8,10},{10,8},{12,14},{14,12},{16,18},{18,... | collective-permute-start | bytes 3538952 | tf_op jit(solution)/shard_map/ppermute | solution.py:30
  89.7 7.7 %collective-permute-start.19 = (bf16[384,1536]{1,0:T(8,128)(2,1)S(1)}, bf16[384,1536]{1,0:T(8,128)(2,1)S(1)}, u32[]{:S(2)}, u32[]{:S(2)}) collective-permute-start(bf16[384,1536]{1,0:T(8,128)(2,1)S(1)} %collective-permute-done.18.refs_4_), channel_id=1, source_target_pairs={{0,2},{2,0},{4,6},{6,4},{8,10},{10,8},{12,14},{14,12},{16,18},{18,... | collective-permute-start | bytes 3538952 | tf_op jit(solution)/shard_map/ppermute | solution.py:30
  90.5 23.8 %collective-permute-start.22 = (bf16[768,384]{1,0:T(8,128)(2,1)}, bf16[768,384]{1,0:T(8,128)(2,1)}, u32[]{:S(2)}, u32[]{:S(2)}) collective-permute-start(bf16[768,384]{1,0:T(8,128)(2,1)} %collective-permute-done.16.refs_4_.refs_2_), channel_id=1, source_target_pairs={{0,4},{2,6},{4,0},{6,2},{8,12},{10,14},{12,8},{14,10},{16,20},{18,... | collective-permute-start | bytes 1769480 | tf_op jit(solution)/shard_map/ppermute | solution.py:30
  95.4 26.2 %collective-permute-start.21 = (bf16[768,384]{1,0:T(8,128)(2,1)}, bf16[768,384]{1,0:T(8,128)(2,1)}, u32[]{:S(2)}, u32[]{:S(2)}) collective-permute-start(bf16[768,384]{1,0:T(8,128)(2,1)} %collective-permute-done.16.refs_4_.refs_2_), channel_id=1, source_target_pairs={{0,2},{2,0},{4,6},{6,4},{8,10},{10,8},{12,14},{14,12},{16,18},{18,... | collective-permute-start | bytes 1769480 | tf_op jit(solution)/shard_map/ppermute | solution.py:30
  114.3 7.3 collective-permute-start.23
  119.8 26.3 %collective-permute-start.20 = (s32[8,128]{1,0:T(8,128)S(1)}, s32[8,128]{1,0:T(8,128)S(1)}, u32[]{:S(2)}, u32[]{:S(2)}) collective-permute-start(s32[8,128]{1,0:T(8,128)S(1)} %max.16), channel_id=1, source_target_pairs={{0,4},{2,6},{4,0},{6,2},{8,12},{10,14},{12,8},{14,10},{16,20},{18,... | collective-permute-start | bytes 12296 | tf_op jit(solution)/shard_map/ppermute | solution.py:30
  161.6 67.6 %all-to-all-start = ((bf16[16,112,768]{2,1,0:T(8,128)(2,1)}), bf16[16,112,768]{2,1,0:T(8,128)(2,1)S(1)}, u32[]{:S(2)}, u32[]{:S(2)}) async-start(bf16[16,112,768]{2,1,0:T(8,128)(2,1)} %bitcast.133), calls=%async_computation | async-start | bytes 5505024 | tf_op jit(solution)/shard_map/all_to_all | solution.py:892
  169.8 53.9 %collective-permute-start.25 = (bf16[1536,768]{1,0:T(8,128)(2,1)}, bf16[1536,768]{1,0:T(8,128)(2,1)}, u32[]{:S(2)}, u32[]{:S(2)}) collective-permute-start(bf16[1536,768]{1,0:T(8,128)(2,1)} %pad_maximum_fusion.refs_0_), channel_id=1, source_target_pairs={{0,1},{1,0},{2,3},{3,2},{4,5},{5,4},{6,7},{7,6},{8,9},{9,8},{10,11... | collective-permute-start | bytes 7077896 | tf_op jit(solution)/shard_map/ppermute | solution.py:30
  171.3 59.6 %collective-permute-start.24 = (bf16[1536,768]{1,0:T(8,128)(2,1)}, bf16[1536,768]{1,0:T(8,128)(2,1)}, u32[]{:S(2)}, u32[]{:S(2)}) collective-permute-start(bf16[1536,768]{1,0:T(8,128)(2,1)} %pad_maximum_fusion.refs_0_), channel_id=1, source_target_pairs={{0,2},{2,0},{4,6},{6,4},{8,10},{10,8},{12,14},{14,12},{16,18},{18,... | collective-permute-start | bytes 7077896 | tf_op jit(solution)/shard_map/ppermute | solution.py:30
  223.7 7.2 collective-permute-start.26
  259.0 58.5 %all-to-all-start.1 = ((bf16[16,112,768]{2,1,0:T(8,128)(2,1)}), bf16[16,112,768]{2,1,0:T(8,128)(2,1)S(1)}, u32[]{:S(2)}, u32[]{:S(2)}) async-start(bf16[16,112,768]{2,1,0:T(8,128)(2,1)} %bitcast.139), calls=%async_computation.1 | async-start | bytes 5505024 | tf_op jit(solution)/shard_map/all_to_all | solution.py:892
  318.4 5.5 collective-permute-start.3
  346.3 65.9 %all-to-all-start.2 = ((bf16[16,112,768]{2,1,0:T(8,128)(2,1)}), bf16[16,112,768]{2,1,0:T(8,128)(2,1)S(1)}, u32[]{:S(2)}, u32[]{:S(2)}) async-start(bf16[16,112,768]{2,1,0:T(8,128)(2,1)} %bitcast.140), calls=%async_computation.2 | async-start | bytes 5505024 | tf_op jit(solution)/shard_map/all_to_all | solution.py:892
  359.7 23.9 %collective-permute-start.27 = (bf16[624,768]{1,0:T(8,128)(2,1)}, bf16[624,768]{1,0:T(8,128)(2,1)}, u32[]{:S(2)}, u32[]{:S(2)}) collective-permute-start(bf16[624,768]{1,0:T(8,128)(2,1)} %get-tuple-element.361), channel_id=1, source_target_pairs={{0,1},{1,0},{2,3},{3,2},{4,5},{5,4},{6,7},{7,6},{8,9},{9,8},{10,11... | collective-permute-start | bytes 2875400 | tf_op jit(solution)/shard_map/ppermute | solution.py:30
  440.0 71.3 %all-to-all-start.3 = ((bf16[16,112,768]{2,1,0:T(8,128)(2,1)}), bf16[16,112,768]{2,1,0:T(8,128)(2,1)S(1)}, u32[]{:S(2)}, u32[]{:S(2)}) async-start(bf16[16,112,768]{2,1,0:T(8,128)(2,1)} %bitcast.138), calls=%async_computation.3 | async-start | bytes 5505024 | tf_op jit(solution)/shard_map/all_to_all | solution.py:892
  462.6 8.9 %collective-permute-start.29 = (bf16[1536,768]{1,0:T(8,128)(2,1)}, bf16[1536,768]{1,0:T(8,128)(2,1)}, u32[]{:S(2)}, u32[]{:S(2)}) collective-permute-start(bf16[1536,768]{1,0:T(8,128)(2,1)} %shard_map.234), channel_id=1, source_target_pairs={{0,2},{2,0},{4,6},{6,4},{8,10},{10,8},{12,14},{14,12},{16,18},{18,... | collective-permute-start | bytes 7077896 | tf_op jit(solution)/shard_map/ppermute | solution.py:30
  471.5 17.8 %collective-permute-start.28 = (bf16[1536,768]{1,0:T(8,128)(2,1)}, bf16[1536,768]{1,0:T(8,128)(2,1)}, u32[]{:S(2)}, u32[]{:S(2)}) collective-permute-start(bf16[1536,768]{1,0:T(8,128)(2,1)} %shard_map.235), channel_id=1, source_target_pairs={{0,2},{2,0},{4,6},{6,4},{8,10},{10,8},{12,14},{14,12},{16,18},{18,... | collective-permute-start | bytes 7077896 | tf_op jit(solution)/shard_map/ppermute | solution.py:30
  482.7 28.7 %collective-permute-start.30 = (bf16[768,768]{1,0:T(8,128)(2,1)}, bf16[768,768]{1,0:T(8,128)(2,1)}, u32[]{:S(2)}, u32[]{:S(2)}) collective-permute-start(bf16[768,768]{1,0:T(8,128)(2,1)} %slice.462), channel_id=1, source_target_pairs={{0,1},{1,0},{2,3},{3,2},{4,5},{5,4},{6,7},{7,6},{8,9},{9,8},{10,11... | collective-permute-start | bytes 3538952 | tf_op jit(solution)/shard_map/ppermute | solution.py:30
  524.4 27.5 %collective-permute-start.31 = (bf16[768,768]{1,0:T(8,128)(2,1)}, bf16[768,768]{1,0:T(8,128)(2,1)S(1)}, u32[]{:S(2)}, u32[]{:S(2)}) collective-permute-start(bf16[768,768]{1,0:T(8,128)(2,1)} %slice.461), channel_id=1, source_target_pairs={{0,1},{1,0},{2,3},{3,2},{4,5},{5,4},{6,7},{7,6},{8,9},{9,8},{10,11... | collective-permute-start | bytes 3538952 | tf_op jit(solution)/shard_map/ppermute | solution.py:30
  562.8 10.2 %collective-permute-start.32 = (bf16[384,3072]{1,0:T(8,128)(2,1)}, bf16[384,3072]{1,0:T(8,128)(2,1)}, u32[]{:S(2)}, u32[]{:S(2)}) collective-permute-start(bf16[384,3072]{1,0:T(8,128)(2,1)} %get-tuple-element.390), channel_id=1, source_target_pairs={{0,2},{2,0},{4,6},{6,4},{8,10},{10,8},{12,14},{14,12},{16,18},{18,... | collective-permute-start | bytes 7077896 | tf_op jit(solution)/shard_map/ppermute | solution.py:30
  572.5 25.1 %collective-permute-start.34 = (bf16[384,3072]{1,0:T(8,128)(2,1)}, bf16[384,3072]{1,0:T(8,128)(2,1)}, u32[]{:S(2)}, u32[]{:S(2)}) collective-permute-start(bf16[384,3072]{1,0:T(8,128)(2,1)} %get-tuple-element.394), channel_id=1, source_target_pairs={{0,2},{2,0},{4,6},{6,4},{8,10},{10,8},{12,14},{14,12},{16,18},{18,... | collective-permute-start | bytes 7077896 | tf_op jit(solution)/shard_map/ppermute | solution.py:30
  578.1 28.1 %collective-permute-start.33 = (bf16[384,1536]{1,0:T(8,128)(2,1)}, bf16[384,1536]{1,0:T(8,128)(2,1)S(1)}, u32[]{:S(2)}, u32[]{:S(2)}) collective-permute-start(bf16[384,1536]{1,0:T(8,128)(2,1)} %slice.467), channel_id=1, source_target_pairs={{0,1},{1,0},{2,3},{3,2},{4,5},{5,4},{6,7},{7,6},{8,9},{9,8},{10,11... | collective-permute-start | bytes 3538952 | tf_op jit(solution)/shard_map/ppermute | solution.py:30
  619.0 11.9 %collective-permute-start.35 = (bf16[384,4096]{1,0:T(8,128)(2,1)}, bf16[384,4096]{1,0:T(8,128)(2,1)}, u32[]{:S(2)}, u32[]{:S(2)}) collective-permute-start(bf16[384,4096]{1,0:T(8,128)(2,1)} %get-tuple-element.414), channel_id=1, source_target_pairs={{0,2},{2,0},{4,6},{6,4},{8,10},{10,8},{12,14},{14,12},{16,18},{18,... | collective-permute-start | bytes 9437192 | tf_op jit(solution)/shard_map/ppermute | solution.py:30
  628.4 39.7 %collective-permute-start.39 = (bf16[192,3072]{1,0:T(8,128)(2,1)}, bf16[192,3072]{1,0:T(8,128)(2,1)}, u32[]{:S(2)}, u32[]{:S(2)}) collective-permute-start(bf16[192,3072]{1,0:T(8,128)(2,1)} %slice.468), channel_id=1, source_target_pairs={{0,4},{2,6},{4,0},{6,2},{8,12},{10,14},{12,8},{14,10},{16,20},{18,... | collective-permute-start | bytes 3538952 | tf_op jit(solution)/shard_map/ppermute | solution.py:30
  635.6 49.2 %collective-permute-start.37 = (bf16[192,4096]{1,0:T(8,128)(2,1)}, bf16[192,4096]{1,0:T(8,128)(2,1)}, u32[]{:S(2)}, u32[]{:S(2)}) collective-permute-start(bf16[192,4096]{1,0:T(8,128)(2,1)} %slice.471), channel_id=1, source_target_pairs={{0,8},{2,10},{4,12},{6,14},{8,0},{10,2},{12,4},{14,6},{16,24},{18,... | collective-permute-start | bytes 4718600 | tf_op jit(solution)/shard_map/ppermute | solution.py:30
  644.2 37.3 %collective-permute-start.38 = (bf16[192,1536]{1,0:T(8,128)(2,1)}, bf16[192,1536]{1,0:T(8,128)(2,1)}, u32[]{:S(2)}, u32[]{:S(2)}) collective-permute-start(bf16[192,1536]{1,0:T(8,128)(2,1)} %slice.470), channel_id=1, source_target_pairs={{0,4},{2,6},{4,0},{6,2},{8,12},{10,14},{12,8},{14,10},{16,20},{18,... | collective-permute-start | bytes 1769480 | tf_op jit(solution)/shard_map/ppermute | solution.py:30
  676.5 10.3 %collective-permute-start.40 = (bf16[384,2560]{1,0:T(8,128)(2,1)}, bf16[384,2560]{1,0:T(8,128)(2,1)S(1)}, u32[]{:S(2)}, u32[]{:S(2)}) collective-permute-start(bf16[384,2560]{1,0:T(8,128)(2,1)} %get-tuple-element.427), channel_id=1, source_target_pairs={{0,2},{2,0},{4,6},{6,4},{8,10},{10,8},{12,14},{14,12},{16,18},{18,... | collective-permute-start | bytes 5898248 | tf_op jit(solution)/shard_map/ppermute | solution.py:30
  676.6 24.2 %collective-permute-start.36 = (bf16[624,768]{1,0:T(8,128)(2,1)}, bf16[624,768]{1,0:T(8,128)(2,1)S(1)}, u32[]{:S(2)}, u32[]{:S(2)}) collective-permute-start(bf16[624,768]{1,0:T(8,128)(2,1)} %get-tuple-element.420), channel_id=1, source_target_pairs={{0,1},{1,0},{2,3},{3,2},{4,5},{5,4},{6,7},{7,6},{8,9},{9,8},{10,11... | collective-permute-start | bytes 2875400 | tf_op jit(solution)/shard_map/ppermute | solution.py:30
  680.6 32.6 %collective-permute-start.42 = (bf16[192,1536]{1,0:T(8,128)(2,1)}, bf16[192,1536]{1,0:T(8,128)(2,1)}, u32[]{:S(2)}, u32[]{:S(2)}) collective-permute-start(bf16[192,1536]{1,0:T(8,128)(2,1)} %slice.475), channel_id=1, source_target_pairs={{0,1},{1,0},{2,3},{3,2},{4,5},{5,4},{6,7},{7,6},{8,9},{9,8},{10,11... | collective-permute-start | bytes 1769480 | tf_op jit(solution)/shard_map/ppermute | solution.py:30
  683.6 22.2 %collective-permute-start.43 = (bf16[96,1536]{1,0:T(8,128)(2,1)}, bf16[96,1536]{1,0:T(8,128)(2,1)}, u32[]{:S(2)}, u32[]{:S(2)}) collective-permute-start(bf16[96,1536]{1,0:T(8,128)(2,1)} %slice.605), channel_id=1, source_target_pairs={{0,8},{2,10},{4,12},{6,14},{8,0},{10,2},{12,4},{14,6},{16,24},{18,... | collective-permute-start | bytes 884744 | tf_op jit(solution)/shard_map/ppermute | solution.py:30
  689.1 34.1 %collective-permute-start.48 = (bf16[192,1792]{1,0:T(8,128)(2,1)}, bf16[192,1792]{1,0:T(8,128)(2,1)}, u32[]{:S(2)}, u32[]{:S(2)}) collective-permute-start(bf16[192,1792]{1,0:T(8,128)(2,1)} %fusion.40), channel_id=1, source_target_pairs={{0,4},{2,6},{4,0},{6,2},{8,12},{10,14},{12,8},{14,10},{16,20},{18,... | collective-permute-start | bytes 2064392 | tf_op jit(solution)/shard_map/ppermute | solution.py:30
  690.8 34.8 %collective-permute-start.47 = (bf16[96,4096]{1,0:T(8,128)(2,1)}, bf16[96,4096]{1,0:T(8,128)(2,1)}, u32[]{:S(2)}, u32[]{:S(2)}) collective-permute-start(bf16[96,4096]{1,0:T(8,128)(2,1)} %slice.397), channel_id=1, source_target_pairs={{0,4},{2,6},{4,0},{6,2},{8,12},{10,14},{12,8},{14,10},{16,20},{18,... | collective-permute-start | bytes 2359304 | tf_op jit(solution)/shard_map/ppermute | solution.py:30
  707.1 21.0 %collective-permute-start.46 = (bf16[48,1536]{1,0:T(8,128)(2,1)S(1)}, bf16[48,1536]{1,0:T(8,128)(2,1)S(1)}, u32[]{:S(2)}, u32[]{:S(2)}) collective-permute-start(bf16[48,1536]{1,0:T(8,128)(2,1)S(1)} %slice.609), channel_id=1, source_target_pairs={{0,16},{2,18},{4,20},{6,22},{8,24},{10,26},{12,28},{14,30},{16,0},... | collective-permute-start | bytes 442376 | tf_op jit(solution)/shard_map/ppermute | solution.py:30
  713.1 8.8 %collective-permute-start.41 = (bf16[384,384]{1,0:T(8,128)(2,1)}, bf16[384,384]{1,0:T(8,128)(2,1)S(1)}, u32[]{:S(2)}, u32[]{:S(2)}) collective-permute-start(bf16[384,384]{1,0:T(8,128)(2,1)} %slice.482), channel_id=1, source_target_pairs={{0,1},{1,0},{2,3},{3,2},{4,5},{5,4},{6,7},{7,6},{8,9},{9,8},{10,11... | collective-permute-start | bytes 884744 | tf_op jit(solution)/shard_map/ppermute | solution.py:30
  715.5 12.6 %collective-permute-start.45 = (bf16[96,1536]{1,0:T(8,128)(2,1)S(1)}, bf16[96,1536]{1,0:T(8,128)(2,1)S(1)}, u32[]{:S(2)}, u32[]{:S(2)}) collective-permute-start(bf16[96,1536]{1,0:T(8,128)(2,1)S(1)} %slice.604), channel_id=1, source_target_pairs={{0,8},{2,10},{4,12},{6,14},{8,0},{10,2},{12,4},{14,6},{16,24},{18,... | collective-permute-start | bytes 884744 | tf_op jit(solution)/shard_map/ppermute | solution.py:30
  722.1 7.5 collective-permute-start.44
  724.5 11.1 %collective-permute-start.49 = (bf16[192,896]{1,0:T(8,128)(2,1)S(1)}, bf16[192,896]{1,0:T(8,128)(2,1)S(1)}, u32[]{:S(2)}, u32[]{:S(2)}) collective-permute-start(bf16[192,896]{1,0:T(8,128)(2,1)S(1)} %slice.603), channel_id=1, source_target_pairs={{0,1},{1,0},{2,3},{3,2},{4,5},{5,4},{6,7},{7,6},{8,9},{9,8},{10,11... | collective-permute-start | bytes 1032200 | tf_op jit(solution)/shard_map/ppermute | solution.py:30
  727.0 14.7 %collective-permute-start.52 = (bf16[96,2048]{1,0:T(8,128)(2,1)S(1)}, bf16[96,2048]{1,0:T(8,128)(2,1)S(1)}, u32[]{:S(2)}, u32[]{:S(2)}) collective-permute-start(bf16[96,2048]{1,0:T(8,128)(2,1)S(1)} %slice.602), channel_id=1, source_target_pairs={{0,1},{1,0},{2,3},{3,2},{4,5},{5,4},{6,7},{7,6},{8,9},{9,8},{10,11... | collective-permute-start | bytes 1179656 | tf_op jit(solution)/shard_map/ppermute | solution.py:30
  728.2 15.0 %collective-permute-start.51 = (bf16[48,1536]{1,0:T(8,128)(2,1)S(1)}, bf16[48,1536]{1,0:T(8,128)(2,1)S(1)}, u32[]{:S(2)}, u32[]{:S(2)}) collective-permute-start(bf16[48,1536]{1,0:T(8,128)(2,1)S(1)} %slice.607), channel_id=1, source_target_pairs={{0,16},{2,18},{4,20},{6,22},{8,24},{10,26},{12,28},{14,30},{16,0},... | collective-permute-start | bytes 442376 | tf_op jit(solution)/shard_map/ppermute | solution.py:30
  735.7 8.2 %collective-permute-start.50 = (bf16[96,1280]{1,0:T(8,128)(2,1)S(1)}, bf16[96,1280]{1,0:T(8,128)(2,1)S(1)}, u32[]{:S(2)}, u32[]{:S(2)}) collective-permute-start(bf16[96,1280]{1,0:T(8,128)(2,1)S(1)} %fusion.43), channel_id=1, source_target_pairs={{0,8},{2,10},{4,12},{6,14},{8,0},{10,2},{12,4},{14,6},{16,24},{18,... | collective-permute-start | bytes 737288 | tf_op jit(solution)/shard_map/ppermute | solution.py:30
  741.7 12.9 %collective-permute-start.54 = (bf16[48,2048]{1,0:T(8,128)(2,1)S(1)}, bf16[48,2048]{1,0:T(8,128)(2,1)S(1)}, u32[]{:S(2)}, u32[]{:S(2)}) collective-permute-start(bf16[48,2048]{1,0:T(8,128)(2,1)S(1)} %slice.606), channel_id=1, source_target_pairs={{0,16},{2,18},{4,20},{6,22},{8,24},{10,26},{12,28},{14,30},{16,0},... | collective-permute-start | bytes 589832 | tf_op jit(solution)/shard_map/ppermute | solution.py:30
  744.0 12.8 %collective-permute-start.53 = (bf16[48,1280]{1,0:T(8,128)(2,1)S(1)}, bf16[48,1280]{1,0:T(8,128)(2,1)S(1)}, u32[]{:S(2)}, u32[]{:S(2)}) collective-permute-start(bf16[48,1280]{1,0:T(8,128)(2,1)S(1)} %slice.610), channel_id=1, source_target_pairs={{0,16},{2,18},{4,20},{6,22},{8,24},{10,26},{12,28},{14,30},{16,0},... | collective-permute-start | bytes 368648 | tf_op jit(solution)/shard_map/ppermute | solution.py:30
  (62 other events, 480.0 us)

commit v3 on v2

--- a/solution.py
+++ b/solution.py
@@ -75,17 +75,13 @@
     first_in, second_in, parts = refs[0], refs[1], refs[2:]
     own_first, own_second, far_first, far_second = targets
     pairs = [(first_in, own_first), (second_in, own_second)]
-    width, span = own_first.shape
-    rows, few = width // 4, span // 4
-    for k, part in enumerate(parts):
-        d = k // 4
-        quarter = (place % 4) ^ (k % 4)
-        at = pl.multiple_of(quarter * rows, 16)
-        pairs.append((part.at[pl.ds(0, rows)], far_first.at[d, pl.ds(at, rows)]))
-        for j in range(few // rows):
-            at = pl.multiple_of(quarter * few + j * rows, 16)
-            source = part.at[pl.ds(rows, rows), pl.ds(j * width, width)]
-            pairs.append((source, far_second.at[d, pl.ds(at, rows)]))
+    quarters = (place % 4, place % 2 + place // 4 % 2 * 2)
+    count = len(parts) // 2
+    for k in range(count):
+        for side, target in enumerate((far_first, far_second)):
+            rows = target.shape[1] // 4
+            at = pl.multiple_of((quarters[side] ^ (k % 4)) * rows, 16)
+            pairs.append((parts[side * count + k], target.at[k // 4, pl.ds(at, rows)]))
     return [pltpu.make_async_copy(x, y, sems.at[n]) for n, (x, y) in enumerate(pairs)]
 
 
@@ -101,7 +97,7 @@
     span = hidden // groups
     return (
         (width, span), (span, width), (groups - 1, width, span), (groups - 1, span, width),
-    ), 2 + 4 * (groups - 1) * (1 + span // width)
+    ), 2 + 8 * (groups - 1)
 
 
 def run_at_start(copies):
@@ -238,7 +234,7 @@
 
 
 def dense_kernel(groups, place_ref, x_ref, gain_ref, bias_ref, *refs):
-    many = 4 * groups - 2
+    many = 8 * groups - 6
     new_ref, normed_ref, act_ref, slope_ref = refs[many : many + 4]
     targets, sems = refs[many + 4 : -1], refs[-1]
     copies = dense_copies(place_ref[0], refs[:many], targets, sems)
@@ -265,7 +261,7 @@
 
 
 def dense_back_kernel(groups, place_ref, grad_ref, x_ref, slope_ref, gain_ref, *refs):
-    many = 4 * groups - 2
+    many = 8 * groups - 6
     moved_ref, gain_out, bias_out = refs[many : many + 3]
     new_refs = refs[many + 3 : -5]
     targets, sems = refs[-5:-1], refs[-1]
@@ -563,33 +559,32 @@
     )(extra, *inputs)
 
 
-def picks_of(cols_ref, gates_ref, count):
-    ids = lax.broadcasted_iota(jnp.int32, (cols_ref.shape[0], count), 1)
-    first, second = ids == cols_ref[:, :1], ids == cols_ref[:, 1:]
-    if gates_ref is None:
+def picks_of(pack, number, weighted, count):
+    ids = lax.broadcasted_iota(jnp.int32, (pack.shape[0], count), 1)
+    cols = pack[:, 3 + 2 * number : 5 + 2 * number].astype(jnp.int32)
+    first, second = ids == cols[:, :1], ids == cols[:, 1:]
+    if not weighted:
         return (first | second).astype(F32).astype(BF)
-    picks = jnp.where(first, gates_ref[:, :1], 0.0) + jnp.where(second, gates_ref[:, 1:], 0.0)
-    return picks.astype(BF)
-
-
-def combine_kernel(far, cols_ref, gates_ref, x_ref, teacher_ref, scale_ref, *refs):
-    others, rows_ref, got = refs[:far], refs[far], refs[far + 1 : 2 * far + 1]
-    final_ref, grad_ref, low_ref = refs[2 * far + 1 :]
-    total = x_ref[...]
-    for cols, rows in zip((cols_ref,) + others, (rows_ref,) + got):
-        total = total + mm(picks_of(cols, gates_ref, rows.shape[0]), rows[...], NN)
+    return (jnp.where(first, pack[:, :1], 0.0) + jnp.where(second, pack[:, 1:2], 0.0)).astype(BF)
+
+
+def combine_kernel(pack_ref, x_ref, teacher_ref, *refs):
+    rows, (final_ref, grad_ref, low_ref) = refs[:-3], refs[-3:]
+    total, pack = x_ref[...], pack_ref[...]
+    for number, source in enumerate(rows):
+        total = total + mm(picks_of(pack, number, True, source.shape[0]), source[...], NN)
     final_ref[...] = total.astype(BF)
-    grad = scale_ref[...] * (total - teacher_ref[...].astype(F32))
+    grad = pack[:, 2:3] * (total - teacher_ref[...].astype(F32))
     grad_ref[...] = grad
     low_ref[...] = grad.astype(BF)
 
 
-def combine_back_kernel(far, cols_ref, x_ref, grad_ref, logits_ref, *refs):
-    others, rows_ref, got = refs[:far], refs[far], refs[far + 1 : 2 * far + 1]
-    router_ref, gain_ref, gain_out, bias_out, *new_refs = refs[2 * far + 1 :]
-    total = mm(logits_ref[...], router_ref[...], NT)
-    for cols, rows in zip((cols_ref,) + others, (rows_ref,) + got):
-        total = total + mm(picks_of(cols, None, rows.shape[0]), rows[...], NN)
+def combine_back_kernel(far, pack_ref, x_ref, grad_ref, logits_ref, *refs):
+    rows, refs = refs[: far + 1], refs[far + 1 :]
+    router_ref, gain_ref, gain_out, bias_out, *new_refs = refs
+    total, pack = mm(logits_ref[...], router_ref[...], NT), pack_ref[...]
+    for number, source in enumerate(rows):
+        total = total + mm(picks_of(pack, number, False, source.shape[0]), source[...], NN)
     finish_back(grad_ref[...], total, x_ref, gain_ref, new_refs, gain_out, bias_out)
 
 
@@ -714,12 +709,9 @@
         parts = [out_part[:, j * span : (j + 1) * span] for j in range(groups)]
         return jnp.concatenate([qkv_part] + parts, 0)
 
-    def dense_piece(first, second):
-        rows, few = width // 4, second.shape[0] // 4
-        second = lax.dynamic_slice_in_dim(second, quarter * few, few, 0)
-        parts = [second[j * rows : (j + 1) * rows] for j in range(few // rows)]
-        first = lax.dynamic_slice_in_dim(first, quarter * rows, rows, 0)
-        return jnp.concatenate([first, jnp.concatenate(parts, 1)], 0)
+    def rows_of(weight, number):
+        rows = weight.shape[0] // 4
+        return lax.dynamic_slice_in_dim(weight, number * rows, rows, 0)
 
     def over_tensor(value):
         return [swap(value, "tensor", d) for d in range(1, groups)]
@@ -738,29 +730,24 @@
         last[0] = value
         return value
 
-    def spread(parts):
-        return [swap(part, "expert", 2) for part in parts], [swap(part, "expert", 1) for part in parts]
-
-    def fourth(parts):
-        return [swap(part, "expert", 1) for part in parts]
+    def leg(parts, distance):
+        return [swap(part, "expert", distance) for part in parts]
 
     def joined(first, second, third, last):
         return [x for four in zip(first, third, second, last) for x in four]
 
     piece_first = mark(attend_piece(0))
     first_x = over_tensor(piece_first)
+    piece_in = mark(rows_of(after(mlp_in), quarter))
+    piece_out = mark(rows_of(after(mlp_out), place % 2 + place // 4 % 2 * 2))
+    piece_second = mark(attend_piece(1))
     tokens = after(tokens)
-    start = relative(tokens, 0, 1).astype(F32)
-    first_x = list(pinned_all(first_x, start))
-    first_y, first_c = spread(first_x)
-    mark(first_x[0])
-    piece_dense = mark(dense_piece(*after(mlp_in, mlp_out)))
-    dense_x = over_tensor(piece_dense)
-    first_y = list(pinned_all(first_y, piece_dense))
-    first_l = fourth(first_y)
-    mark(first_y[0])
-    piece_second = mark(after(attend_piece(1)))
+    start = mark(relative(tokens, 0, 1).astype(F32))
+    first_x = [after(x) for x in first_x]
+    in_x, out_x = over_tensor(piece_in), over_tensor(piece_out)
     second_x = over_tensor(piece_second)
+    first_y, first_c = leg(first_x, 2), leg(first_x, 1)
+    first_l = leg(first_y, 1)
     weights_first = [attn_qkv, attn_out] + joined(first_x, first_y, first_c, first_l)
 
     room = 2 * used
@@ -828,24 +815,27 @@
     routes_own = relative(routes, 0, 1)
     valid_rows = relative(jnp.repeat(valid_flags.astype(F32), SEQ)[:, None], 0, 1)
 
-    dense_x = list(pinned_all(dense_x, piece_second, local_row, crowd, *first_c, *first_l))
-    dense_y, dense_c = spread(dense_x)
-    start = pinned(start, *dense_x)
+    in_x = pinned_all(in_x, *first_l)
+    start = pinned(start, *in_x, local_row, crowd)
     after_attn, normed_first, packed_first, mixed_first, total_first = attend_forward(
         0, groups, place_ref, start, gain_rows[0], bias_rows[0], weights_first
     )
     crowd = wider(crowd, 4, after_attn)
-    second_x = pinned_all(second_x, after_attn)
-    dense_y = pinned_all(dense_y, *second_x)
-    dense_l = fourth(dense_y)
-    second_y, second_c = spread(second_x)
-    weights_dense = [mlp_in, mlp_out] + joined(dense_x, dense_y, dense_c, dense_l)
+    out_x = pinned_all(out_x, after_attn)
+    second_x = pinned_all(second_x, *out_x)
+    in_y, in_c = leg(in_x, 2), leg(in_x, 1)
+    out_y, out_c = leg(out_x, 4), leg(out_x, 1)
+    in_y, out_y = pinned_all(in_y, after_attn), pinned_all(out_y, *second_x)
+    crowd = wider(crowd, 8, *out_y)
+    weights_dense = [mlp_in, mlp_out] + joined(in_x, in_y, in_c, leg(in_y, 1))
+    weights_dense += joined(out_x, out_y, out_c, leg(out_y, 1))
+    second_y, second_c = leg(second_x, 2), leg(second_x, 1)
     after_dense, normed_dense, dense_act, dense_slope = dense_forward(
-        groups, place_ref, pinned(after_attn, crowd, *second_x), gain_rows[1], bias_rows[1], weights_dense
+        groups, place_ref, pinned(after_attn, crowd, *second_x), gain_rows[1], bias_rows[1],
+        weights_dense,
     )
     second_y = pinned_all(second_y, after_dense)
-    weights_second = [attn_qkv, attn_out] + joined(second_x, second_y, second_c, fourth(second_y))
-    crowd = wider(crowd, 8, after_dense)
+    weights_second = [attn_qkv, attn_out] + joined(second_x, second_y, second_c, leg(second_y, 1))
     second = attend_forward(
         1, groups, place_ref, pinned(after_dense, crowd), gain_rows[2], bias_rows[2],
         weights_second, (gain_rows[3], bias_rows[3]),
@@ -916,7 +906,11 @@
     scale = (local_rows * owners / valid_count) * valid_rows
     rows_in = pinned(rows_in, teacher_rel, scale)
     expert_rows, act, slope = expert_forward(rows_in, expert_parts)
+    pairs = [x.astype(F32) for x in (local_row, *guest_out)]
+    pack = jnp.concatenate([gate_vals, scale] + pairs, 1)
+    pack = jnp.pad(pack, ((0, 0), (0, 128 - pack.shape[1])))
     merged = across(expert_rows)
+    merged, pack = pinned_all((merged, pack), expert_rows)
 
     outs = (shape(own_rows, width), shape(own_rows, width, kind=F32), shape(own_rows, width))
 
@@ -924,10 +918,7 @@
         def branch(rows):
             got = over(returned_rows(count, rows))
             results = combine_call(
-                functools.partial(combine_kernel, groups - 1),
-                (local_row, gate_vals, after_second, teacher_rel, scale, *guest_out),
-                (rows, *got),
-                outs,
+                combine_kernel, (pack, after_second, teacher_rel), (rows, *got), outs
             )
             return tuple(results) + tuple(grown(x) for x in got)
 
@@ -1019,8 +1010,7 @@
         jnp.where(picker, grad_chosen[:, :, None], 0.0), axis=1
     ).astype(BF)
     grad_router = mm(grad_logits, normed_expert, TN)
-    grad_back = pinned(grad_back, *sent_ei, *got_eo, grad_router)
-    grad_expert_out = finish(keep_eo, got_eo)
+    grad_back = pinned(grad_back, *sent_ei, *got_eo, grad_router, activations)
 
     outs = (shape(1, width, kind=F32),) * 2 + (
         shape(own_rows, width, kind=F32), shape(own_rows, width),
@@ -1030,7 +1020,7 @@
         def branch(rows):
             results = combine_call(
                 functools.partial(combine_back_kernel, groups - 1),
-                (local_row, after_second, grad_final, grad_logits, *guest_out),
+                (pack, after_second, grad_final, grad_logits),
                 (rows, *over(returned_rows(count, rows)), router, gain_rows[3]),
                 outs,
             )
@@ -1080,7 +1070,6 @@
     keep_a, sent_a = start_groups(arrive(keep_a, got_a).astype(BF))
     mark(sent_a[0])
     got_a = cross(sent_a)
-    grad_expert_in = finish(keep_ei, got_ei)
     grad_hidden, gain_two, bias_two, grad_attn, low_first = dense_backward(
         groups, place_ref, after(grad_dense), after_attn, gain_rows[1], dense_slope, weights_dense,
     )
@@ -1178,8 +1167,10 @@
     keep_d, sent_d = start_rows(arrive(keep_d, got_d))
     mark(sent_d[0])
     got_d = along(sent_d, 8)
-    total_c = mark(arrive(keep_c, got_c))
-    total_d = arrive(keep_d, got_d)
+    keep_eo, keep_ei = pinned_all((keep_eo, keep_ei), sent_d[0])
+    grad_expert_out, grad_expert_in = finish(keep_eo, got_eo), finish(keep_ei, got_ei)
+    total_c = arrive(keep_c, got_c)
+    total_d = arrive(keep_d, [pinned(x, grad_expert_out, grad_expert_in, total_c) for x in got_d])
     joint = jnp.concatenate([total_a, total_b, total_c, total_d], 1)
     step = 16
     while step < owners:

time: 766 us -> 711 us (0.928)
  waiting for transfers between devices: 255 us -> 229 us
  Pallas kernels: 273 us -> 263 us
    ppermute x51 -> x55, waiting for transfers between devices: 175 us -> 150 us  [swap(): return lax.ppermute(value, axis, [(k, k ^ distance) for k in range(size)])]
    pallas_call x6, Pallas kernels: 116 us -> 107 us  [dense_call(): pl.pallas_call(kernel, grid=(rows[0].shape[-2] // ROWS,), in_specs=specs,...]
    ppermute x51 -> x55, starting transfers between devices: 55.3 us -> 49.6 us  [swap(): return lax.ppermute(value, axis, [(k, k ^ distance) for k in range(size)])]
  transfers between devices with their start and end apart: 55 -> 59, of which waited for: 24 -> 27; matrix products, arithmetic and copies ran while one was open for 14% -> 14% of each run, Pallas kernels for 22% -> 22%
where the time goes in v3:
time: 711 us; the launch traced here: 708 us
  Pallas kernels  263 us (37%)
  waiting for transfers between devices  229 us (32%)
  starting transfers between devices  86.8 us (12%)
  local copies, waits for them, and re-layouts  59.5 us (8%)
  other arithmetic  56.9 us (8%)
  matrix products  7.86 us (1%)
    ppermute x55, waiting for transfers between devices, swap(): return lax.ppermute(value, axis, [(k, k ^ distance) for k in range(size)])  150 us
    pallas_call x6, Pallas kernels, dense_call(): pl.pallas_call(kernel, grid=(rows[0].shape[-2] // ROWS,), in_specs=specs,...  107 us
    all_to_all x4, waiting for transfers between devices, across(): lax.all_to_all(rows.reshape(owners, part, width), 'expert', split_axis=0,...  79.2 us
    pallas_call x2, Pallas kernels, expert_call(): pl.pallas_call(kernel, grid=(count // tile,), in_specs=[image_spec(tile,...  54.3 us
    ppermute x55, starting transfers between devices, swap(): return lax.ppermute(value, axis, [(k, k ^ distance) for k in range(size)])  49.6 us
    pallas_call x4, Pallas kernels, weight_grads(): pl.pallas_call(functools.partial(weight_kernel, groups, len(stats)), in_s...  41.7 us
    all_to_all x4, starting transfers between devices, across(): lax.all_to_all(rows.reshape(owners, part, width), 'expert', split_axis=0,...  37.1 us
    pallas_call x4, Pallas kernels, expert_grads(): pl.pallas_call(outer_kernel, grid=(count,), in_specs=([cut, whole] if cut...  34.2 us
  transfers between devices with their start and end apart: 59, of which 27 were waited for; matrix products, arithmetic and copies ran while one was open for 14% of the time, Pallas kernels for 22%

profile of v3, /device:TPU:0, one launch (start us, length us, event | category | flops | bytes accessed | tf_op | source)
XLA Modules:
  0.0 707.7 jit_solution(14552258762174229316)
XLA Ops:
  23.7 4.9 reduce-window.14
  40.0 13.4 %shard_map.229 = (f32[624,768]{1,0:T(8,128)}, bf16[624,768]{1,0:T(8,128)(2,1)}, bf16[3,624,768]{2,1,0:T(8,128)(2,1)}, bf16[624,768]{1,0:T(8,128)(2,1)}, f32[624,128]{1,0:T(8,128)}) custom-call(s32[1]{0:T(128)} %bitcast.9.place_ref, f32[624,768]{1,0:T(8,128)} %bitcast_convert_fusion.x_ref, f32[1,768]{1,0:T(1,128)} %get-tuple-element.723.gain_ref, ...), custom_call_target="tpu_custom_call" | custom-call | flops 668624512 | bytes 3204710 | tf_op jit(solution)/shard_map/pallas_call | solution.py:312
  56.6 12.1 %collective-permute-done.10 = s32[8,128]{1,0:T(8,128)S(1)} collective-permute-done((s32[8,128]{1,0:T(8,128)S(1)}, s32[8,128]{1,0:T(8,128)S(1)}, u32[]{:S(2)}, u32[]{:S(2)}) %collective-permute-start.10) | collective-permute-done | bytes 4128 | tf_op jit(solution)/shard_map/ppermute | solution.py:30
  77.8 15.5 %shard_map.230 = (f32[624,768]{1,0:T(8,128)}, bf16[624,768]{1,0:T(8,128)(2,1)}, bf16[624,3072]{1,0:T(8,128)(2,1)}, bf16[624,3072]{1,0:T(8,128)(2,1)}) custom-call(s32[1]{0:T(128)} %bitcast.9.place_ref, f32[624,768]{1,0:T(8,128)} %get-tuple-element.327.x_ref, f32[1,768]{1,0:T(1,128)} %get-tuple-element.724.gain_ref, f32[1,768]{1,0:T(1,128)} %get-tuple-element.709.bias_ref, ...), custom_call_target="tpu_custom_call" | custom-call | flops 1177760512 | bytes 4379443 | tf_op jit(solution)/shard_map/pallas_call | solution.py:312
  96.4 14.6 %shard_map.231 = (f32[624,768]{1,0:T(8,128)}, bf16[624,768]{1,0:T(8,128)(2,1)}, bf16[3,624,768]{2,1,0:T(8,128)(2,1)}, bf16[624,768]{1,0:T(8,128)(2,1)}, f32[624,128]{1,0:T(8,128)}, /*index=5*/bf16[624,768]{1,0:T(8,128)(2,1)}) custom-call(s32[1]{0:T(128)} %bitcast.9.place_ref, f32[624,768]{1,0:T(8,128)} %get-tuple-element.330.x_ref, ...), custom_call_target="tpu_custom_call" | custom-call | flops 668624512 | bytes 3396403 | tf_op jit(solution)/shard_map/pallas_call | solution.py:312
  112.2 12.9 %conditional.4 = (bf16[1792,768]{1,0:T(8,128)(2,1)S(1)}) conditional(s32[]{:T(128)} %bitcast.12, (s32[528]{0:T(1024)S(1)}, s32[624,2]{0,1:T(2,128)S(1)}, bf16[624,768]{1,0:T(8,128)(2,1)}, f32[1]{0:T(128)}, s32[2,624]{1,0:T(2,128)S(1)}) %tuple.268, (s32[528]{0:T(1024)S(1)}, s32[624,2]{0,1:T(2,128)S(1)}, bf16[624,768]{1,0:T(8,128)(2,1)}, ...), branch_computations={%region_22.23_spmd, %region_23.24_spmd} | conditional | flops 850976384 | bytes 9024003 | solution.py:876
  115.2 3.4 collective-permute-done.1.refs_1_
  119.3 5.9 branch_1_fun.4
  126.7 3.7 all-to-all-start
  130.4 3.2 pad_maximum_fusion.refs_0_
  134.6 52.8 %collective-permute-done.29.refs_2_ = bf16[1536,768]{1,0:T(8,128)(2,1)} collective-permute-done((bf16[1536,768]{1,0:T(8,128)(2,1)}, bf16[1536,768]{1,0:T(8,128)(2,1)}, u32[]{:S(2)}, u32[]{:S(2)}) %collective-permute-start.29) | collective-permute-done | bytes 2359328 | tf_op jit(solution)/shard_map/ppermute | solution.py:30
  187.4 3.2 reshape.655
  194.6 28.1 %shard_map.232 = (bf16[1792,768]{1,0:T(8,128)(2,1)}, bf16[1792,3072]{1,0:T(8,128)(2,1)}, bf16[1792,3072]{1,0:T(8,128)(2,1)}) custom-call(bf16[1792,768]{1,0:T(8,128)(2,1)} %bitcast.130, bf16[1536,768]{1,0:T(8,128)(2,1)} %pad_maximum_fusion.refs_0_, bf16[1536,768]{1,0:T(8,128)(2,1)} %collective-permute-done.28.refs_1_, ...), custom_call_target="tpu_custom_call" | custom-call | flops 3382286848 | bytes 7392460 | tf_op jit(solution)/shard_map/pallas_call | solution.py:441
  222.7 6.0 all-to-all-start.1
  230.6 50.6 %all-to-all-done.1 = bf16[16,112,768]{2,1,0:T(8,128)(2,1)S(1)} async-done(((bf16[16,112,768]{2,1,0:T(8,128)(2,1)}), bf16[16,112,768]{2,1,0:T(8,128)(2,1)S(1)}, u32[]{:S(2)}, u32[]{:S(2)}) %all-to-all-start.1) | async-done | bytes 2752544 | tf_op jit(solution)/shard_map/all_to_all | solution.py:882
  281.2 13.6 %conditional.5 = (bf16[624,768]{1,0:T(8,128)(2,1)}, f32[624,768]{1,0:T(8,128)}, bf16[624,768]{1,0:T(8,128)(2,1)}, bf16[528,768]{1,0:T(8,128)(2,1)}) conditional(s32[]{:T(128)} %bitcast.12, (s32[528]{0:T(1024)S(1)}, s32[1792]{0:T(1024)S(1)}, bf16[1792,768]{1,0:T(8,128)(2,1)S(1)}, f32[624,128]{0,1:T(8,128)S(1)}, f32[624,768]{1,0:T(8,128)}, ...), branch_computations={%region_28.29_spmd, %region_29.30_spmd} | conditional | flops 1798191488 | bytes 9574331 | solution.py:876
  283.9 3.6 collective-permute-done.3.refs_1_
  288.5 6.3 branch_1_fun.5
  294.8 14.7 %conditional.6 = (bf16[1792,768]{1,0:T(8,128)(2,1)}, f32[1792,1]{1,0:T(8,128)}, f32[528,1]{0,1:T(1,128)S(1)}) conditional(s32[]{:T(128)} %bitcast.12, (s32[528]{0:T(1024)S(1)}, s32[624,2]{0,1:T(2,128)S(1)}, f32[2,624]{1,0:T(2,128)S(1)}, bf16[624,768]{1,0:T(8,128)(2,1)}, f32[1]{0:T(128)}, /*index=5*/s32[2,624]{1,0:T(2,128)S(1)}, ...), branch_computations={%region_30.33_spmd, %region_33.36_spmd} | conditional | flops 854574208 | bytes 6616499 | solution.py:876
  301.9 7.7 %branch_1_fun.6 = (bf16[1792,768]{1,0:T(8,128)(2,1)}, f32[1792,1]{1,0:T(8,128)}) custom-call(f32[1]{0:T(128)} %get-tuple-element.153.extra_ref, s32[2,624]{1,0:T(2,128)S(1)} %get-tuple-element.154.lines_ref, f32[2,624]{1,0:T(2,128)S(1)} %get-tuple-element.155.gates_ref, bf16[624,768]{1,0:T(8,128)(2,1)} %get-tuple-element.156.rows_ref, ...), custom_call_target="tpu_custom_call" | custom-call | flops 343513504 | bytes 742195 | tf_op jit(solution)/shard_map/cond/branch_1_fun/pallas_call | solution.py:550
  309.6 13.4 %all-to-all-start.2 = ((bf16[16,112,768]{2,1,0:T(8,128)(2,1)}), bf16[16,112,768]{2,1,0:T(8,128)(2,1)S(1)}, u32[]{:S(2)}, u32[]{:S(2)}) async-start(bf16[16,112,768]{2,1,0:T(8,128)(2,1)} %bitcast.140), calls=%async_computation.2 | async-start | bytes 5505024 | tf_op jit(solution)/shard_map/all_to_all | solution.py:882
  324.0 22.8 %collective-permute-done.31 = bf16[624,768]{1,0:T(8,128)(2,1)} collective-permute-done((bf16[624,768]{1,0:T(8,128)(2,1)}, bf16[624,768]{1,0:T(8,128)(2,1)}, u32[]{:S(2)}, u32[]{:S(2)}) %collective-permute-start.31) | collective-permute-done | bytes 958496 | tf_op jit(solution)/shard_map/ppermute | solution.py:30
  346.8 28.7 %all-to-all-done.2 = bf16[16,112,768]{2,1,0:T(8,128)(2,1)S(1)} async-done(((bf16[16,112,768]{2,1,0:T(8,128)(2,1)}), bf16[16,112,768]{2,1,0:T(8,128)(2,1)S(1)}, u32[]{:S(2)}, u32[]{:S(2)}) %all-to-all-start.2) | async-done | bytes 2752544 | tf_op jit(solution)/shard_map/all_to_all | solution.py:882
  377.0 26.2 %shard_map.233 = (bf16[1792,768]{1,0:T(8,128)(2,1)}, bf16[1792,3072]{1,0:T(8,128)(2,1)}) custom-call(bf16[1792,768]{1,0:T(8,128)(2,1)} %bitcast.126, bf16[1792,3072]{1,0:T(8,128)(2,1)} %get-tuple-element.346.slope_ref, bf16[1536,768]{1,0:T(8,128)(2,1)} %pad_maximum_fusion.refs_0_, bf16[1536,768]{1,0:T(8,128)(2,1)} %collective-permute-done.28.refs_1_, ...), custom_call_target="tpu_custom_call" | custom-call | flops 3382286848 | bytes 7392460 | tf_op jit(solution)/shard_map/pallas_call | solution.py:441
  403.2 14.1 %all-to-all-start.3 = ((bf16[16,112,768]{2,1,0:T(8,128)(2,1)}), bf16[16,112,768]{2,1,0:T(8,128)(2,1)S(1)}, u32[]{:S(2)}, u32[]{:S(2)}) async-start(bf16[16,112,768]{2,1,0:T(8,128)(2,1)} %bitcast.138), calls=%async_computation.3 | async-start | bytes 5505024 | tf_op jit(solution)/shard_map/all_to_all | solution.py:882
  417.3 8.4 %shard_map.234 = bf16[1536,768]{1,0:T(8,128)(2,1)} custom-call(bf16[1792,3072]{1,0:T(8,128)(2,1)} %get-tuple-element.353.left_ref, bf16[1792,768]{1,0:T(8,128)(2,1)} %bitcast.127), custom_call_target="tpu_custom_call" | custom-call | flops 845571712 | bytes 3696230 | tf_op jit(solution)/shard_map/pallas_call | solution.py:623
  426.2 8.3 %shard_map.235 = bf16[1536,768]{1,0:T(8,128)(2,1)} custom-call(bf16[1792,768]{1,0:T(8,128)(2,1)} %bitcast.131, bf16[1792,3072]{1,0:T(8,128)(2,1)} %get-tuple-element.352.right_ref), custom_call_target="tpu_custom_call" | custom-call | flops 845571712 | bytes 3696230 | tf_op jit(solution)/shard_map/pallas_call | solution.py:623
  440.9 8.7 %shard_map.236 = bf16[1536,768]{1,0:T(8,128)(2,1)} custom-call(bf16[1792,3072]{1,0:T(8,128)(2,1)} %get-tuple-element.353.left_ref, bf16[1792,768]{1,0:T(8,128)(2,1)} %bitcast.128, bf16[1536,768]{1,0:T(8,128)(2,1)} %collective-permute-done.33.refs_0_), custom_call_target="tpu_custom_call" | custom-call | flops 845571712 | bytes 3696230 | tf_op jit(solution)/shard_map/pallas_call | solution.py:623
  449.6 3.3 fusion.87
  455.3 3.2 reshape.663
  460.6 8.7 %shard_map.237 = bf16[1536,768]{1,0:T(8,128)(2,1)} custom-call(bf16[1792,768]{1,0:T(8,128)(2,1)} %bitcast.132, bf16[1792,3072]{1,0:T(8,128)(2,1)} %get-tuple-element.352.right_ref, bf16[1536,768]{1,0:T(8,128)(2,1)} %collective-permute-done.32.refs_0_), custom_call_target="tpu_custom_call" | custom-call | flops 845571712 | bytes 3696230 | tf_op jit(solution)/shard_map/pallas_call | solution.py:623
  472.6 9.1 %collective-permute-done.34 = bf16[768,768]{1,0:T(8,128)(2,1)} collective-permute-done((bf16[768,768]{1,0:T(8,128)(2,1)}, bf16[768,768]{1,0:T(8,128)(2,1)}, u32[]{:S(2)}, u32[]{:S(2)}) %collective-permute-start.34) | collective-permute-done | bytes 1179680 | tf_op jit(solution)/shard_map/ppermute | solution.py:30
  481.6 13.0 %conditional.7 = ((f32[1,768]{1,0:T(1,128)S(1)}, f32[1,768]{1,0:T(1,128)S(1)}, f32[624,768]{1,0:T(8,128)}, bf16[624,768]{1,0:T(8,128)(2,1)})) conditional(s32[]{:T(128)} %bitcast.12, (s32[528]{0:T(1024)S(1)}, s32[1792]{0:T(1024)S(1)}, bf16[1792,768]{1,0:T(8,128)(2,1)S(1)}, f32[624,128]{0,1:T(8,128)S(1)}, f32[624,768]{1,0:T(8,128)}, ...), branch_computations={%region_42.43_spmd, %region_43.44_spmd} | conditional | flops 1798191488 | bytes 9625148 | solution.py:876
  488.0 6.7 branch_1_fun.7
  496.9 23.1 %shard_map.238 = (bf16[3,624,768]{2,1,0:T(8,128)(2,1)}, f32[1,768]{1,0:T(1,128)}, f32[1,768]{1,0:T(1,128)}, f32[624,768]{1,0:T(8,128)}, bf16[624,768]{1,0:T(8,128)(2,1)}) custom-call(s32[1]{0:T(128)} %bitcast.9.place_ref, f32[624,768]{1,0:T(8,128)} %get-tuple-element.361.grad_ref, f32[624,768]{1,0:T(8,128)} %get-tuple-element.330.x_ref, ...), custom_call_target="tpu_custom_call" | custom-call | flops 788240768 | bytes 3972710 | tf_op jit(solution)/shard_map/pallas_call | solution.py:312
  521.3 10.9 %shard_map.239 = (bf16[384,3072]{1,0:T(8,128)(2,1)}, bf16[384,3072]{1,0:T(8,128)(2,1)}) custom-call(bf16[768,768]{1,0:T(8,128)(2,1)} %fusion.38.mover_ref, bf16[624,768]{1,0:T(8,128)(2,1)} %get-tuple-element.368.refs_0_, bf16[624,768]{1,0:T(8,128)(2,1)S(1)} %copy-done.30, bf16[3,624,768]{2,1,0:T(8,128)(2,1)} %get-tuple-element.370.refs_2_, ...), custom_call_target="tpu_custom_call" | custom-call | flops 588880256 | bytes 2329804 | tf_op jit(solution)/shard_map/pallas_call | solution.py:506
  532.2 9.5 %shard_map.240 = (bf16[384,3072]{1,0:T(8,128)(2,1)}, bf16[384,3072]{1,0:T(8,128)(2,1)}) custom-call(bf16[768,768]{1,0:T(8,128)(2,1)} %fusion.38.mover_ref, bf16[624,768]{1,0:T(8,128)(2,1)} %get-tuple-element.375.refs_0_, bf16[624,3072]{1,0:T(8,128)(2,1)} %get-tuple-element.376.refs_1_), custom_call_target="tpu_custom_call" | custom-call | flops 588880256 | bytes 2138112 | tf_op jit(solution)/shard_map/pallas_call | solution.py:506
  543.7 3.3 add_convert_fusion.2
  550.3 17.1 %shard_map.241 = (bf16[624,3072]{1,0:T(8,128)(2,1)}, f32[1,768]{1,0:T(1,128)}, f32[1,768]{1,0:T(1,128)}, f32[624,768]{1,0:T(8,128)}, bf16[624,768]{1,0:T(8,128)(2,1)}) custom-call(s32[1]{0:T(128)} %bitcast.9.place_ref, f32[624,768]{1,0:T(8,128)} %get-tuple-element.379.grad_ref, f32[624,768]{1,0:T(8,128)} %get-tuple-element.327.x_ref, ...), custom_call_target="tpu_custom_call" | custom-call | flops 1177760512 | bytes 4764057 | tf_op jit(solution)/shard_map/pallas_call | solution.py:312
  567.4 3.3 add_convert_fusion.1
  576.2 12.7 %shard_map.242 = (bf16[384,4096]{1,0:T(8,128)(2,1)}, bf16[384,4096]{1,0:T(8,128)(2,1)}) custom-call(bf16[768,768]{1,0:T(8,128)(2,1)} %fusion.39.mover_ref, f32[1,768]{1,0:T(1,128)} %get-tuple-element.382.refs_0_, f32[1,768]{1,0:T(1,128)} %get-tuple-element.383.refs_1_, f32[1,768]{1,0:T(1,128)S(1)} %get-tuple-element.384.refs_2_, ...), custom_call_target="tpu_custom_call" | custom-call | flops 785173696 | bytes 2840371 | tf_op jit(solution)/shard_map/pallas_call | solution.py:506
  591.5 3.2 collective-permute-done.39
  600.0 22.9 %shard_map.243 = (bf16[3,624,768]{2,1,0:T(8,128)(2,1)}, f32[1,768]{1,0:T(1,128)}, f32[1,768]{1,0:T(1,128)}, bf16[624,768]{1,0:T(8,128)(2,1)}) custom-call(s32[1]{0:T(128)} %bitcast.9.place_ref, f32[624,768]{1,0:T(8,128)} %get-tuple-element.400.grad_ref, f32[624,768]{1,0:T(8,128)} %bitcast_convert_fusion.x_ref, ...), custom_call_target="tpu_custom_call" | custom-call | flops 788240768 | bytes 3589324 | tf_op jit(solution)/shard_map/pallas_call | solution.py:312
  624.0 8.5 %shard_map.244 = (bf16[384,2560]{1,0:T(8,128)(2,1)}, bf16[384,2560]{1,0:T(8,128)(2,1)}) custom-call(bf16[768,768]{1,0:T(8,128)(2,1)} %fusion.38.mover_ref, f32[1,768]{1,0:T(1,128)} %get-tuple-element.405.refs_0_, f32[1,768]{1,0:T(1,128)} %get-tuple-element.406.refs_1_, bf16[624,768]{1,0:T(8,128)(2,1)} %get-tuple-element.408.refs_2_, ...), custom_call_target="tpu_custom_call" | custom-call | flops 490733568 | bytes 1789747 | tf_op jit(solution)/shard_map/pallas_call | solution.py:506
  650.3 3.2 reshape.667
  667.9 10.3 %collective-permute-done.51 = bf16[96,4096]{1,0:T(8,128)(2,1)} collective-permute-done((bf16[96,4096]{1,0:T(8,128)(2,1)}, bf16[96,4096]{1,0:T(8,128)(2,1)}, u32[]{:S(2)}, u32[]{:S(2)}) %collective-permute-start.51) | collective-permute-done | bytes 786464 | tf_op jit(solution)/shard_map/ppermute | solution.py:30
  684.9 4.0 collective-permute-done.56
  698.1 4.2 collective-permute-done.58
  (389 shorter events, 170.7 us)
Async XLA Ops:
  3.8 17.4 %collective-permute-start.8 = (bf16[768,384]{1,0:T(8,128)(2,1)}, bf16[768,384]{1,0:T(8,128)(2,1)}, u32[]{:S(2)}, u32[]{:S(2)}) collective-permute-start(bf16[768,384]{1,0:T(8,128)(2,1)} %pad_maximum_fusion.6), channel_id=1, source_target_pairs={{0,1},{1,0},{2,3},{3,2},{4,5},{5,4},{6,7},{7,6},{8,9},{9,8},{10,11... | collective-permute-start | bytes 1769480 | tf_op jit(solution)/shard_map/ppermute | solution.py:30
  8.7 28.9 %collective-permute-start.11 = (bf16[192,1536]{1,0:T(8,128)(2,1)}, bf16[192,1536]{1,0:T(8,128)(2,1)S(1)}, u32[]{:S(2)}, u32[]{:S(2)}) collective-permute-start(bf16[192,1536]{1,0:T(8,128)(2,1)} %constant_dynamic-slice_fusion.5), channel_id=1, source_target_pairs={{0,1},{1,0},{2,3},{3,2},{4,5},{5,4},{6,7},{7,6},{8,9},{9,8},{10,11... | collective-permute-start | bytes 1769480 | tf_op jit(solution)/shard_map/ppermute | solution.py:30
  10.6 42.8 %collective-permute-start.16 = (bf16[384,768]{1,0:T(8,128)(2,1)}, bf16[384,768]{1,0:T(8,128)(2,1)S(1)}, u32[]{:S(2)}, u32[]{:S(2)}) collective-permute-start(bf16[384,768]{1,0:T(8,128)(2,1)} %constant_dynamic-slice_fusion.4), channel_id=1, source_target_pairs={{0,1},{1,0},{2,3},{3,2},{4,5},{5,4},{6,7},{7,6},{8,9},{9,8},{10,11... | collective-permute-start | bytes 1769480 | tf_op jit(solution)/shard_map/ppermute | solution.py:30
  21.2 13.9 %collective-permute-start.12 = (bf16[768,384]{1,0:T(8,128)(2,1)}, bf16[768,384]{1,0:T(8,128)(2,1)S(1)}, u32[]{:S(2)}, u32[]{:S(2)}) collective-permute-start(bf16[768,384]{1,0:T(8,128)(2,1)} %collective-permute-done.8.refs_2_), channel_id=1, source_target_pairs={{0,4},{2,6},{4,0},{6,2},{8,12},{10,14},{12,8},{14,10},{16,20},{18,... | collective-permute-start | bytes 1769480 | tf_op jit(solution)/shard_map/ppermute | solution.py:30
  23.3 15.8 %collective-permute-start.14 = (bf16[768,384]{1,0:T(8,128)(2,1)}, bf16[768,384]{1,0:T(8,128)(2,1)S(1)}, u32[]{:S(2)}, u32[]{:S(2)}) collective-permute-start(bf16[768,384]{1,0:T(8,128)(2,1)} %collective-permute-done.8.refs_2_), channel_id=1, source_target_pairs={{0,2},{2,0},{4,6},{6,4},{8,10},{10,8},{12,14},{14,12},{16,18},{18,... | collective-permute-start | bytes 1769480 | tf_op jit(solution)/shard_map/ppermute | solution.py:30
  35.4 36.9 %collective-permute-start.18 = (bf16[768,384]{1,0:T(8,128)(2,1)}, bf16[768,384]{1,0:T(8,128)(2,1)}, u32[]{:S(2)}, u32[]{:S(2)}) collective-permute-start(bf16[768,384]{1,0:T(8,128)(2,1)} %pad_maximum_fusion.7), channel_id=1, source_target_pairs={{0,1},{1,0},{2,3},{3,2},{4,5},{5,4},{6,7},{7,6},{8,9},{9,8},{10,11... | collective-permute-start | bytes 1769480 | tf_op jit(solution)/shard_map/ppermute | solution.py:30
  37.6 35.7 %collective-permute-start.21 = (bf16[192,1536]{1,0:T(8,128)(2,1)S(1)}, bf16[192,1536]{1,0:T(8,128)(2,1)S(1)}, u32[]{:S(2)}, u32[]{:S(2)}) collective-permute-start(bf16[192,1536]{1,0:T(8,128)(2,1)S(1)} %collective-permute-done.11.refs_2_), channel_id=1, source_target_pairs={{0,4},{2,6},{4,0},{6,2},{8,12},{10,14},{12,8},{14,10},{16,20},{18,... | collective-permute-start | bytes 1769480 | tf_op jit(solution)/shard_map/ppermute | solution.py:30
  53.4 19.3 %collective-permute-start.17 = (bf16[384,768]{1,0:T(8,128)(2,1)S(1)}, bf16[384,768]{1,0:T(8,128)(2,1)S(1)}, u32[]{:S(2)}, u32[]{:S(2)}) collective-permute-start(bf16[384,768]{1,0:T(8,128)(2,1)S(1)} %collective-permute-done.16.refs_6_), channel_id=1, source_target_pairs={{0,8},{2,10},{4,12},{6,14},{8,0},{10,2},{12,4},{14,6},{16,24},{18,... | collective-permute-start | bytes 1769480 | tf_op jit(solution)/shard_map/ppermute | solution.py:30
  55.7 13.0 %collective-permute-start.10 = (s32[8,128]{1,0:T(8,128)S(1)}, s32[8,128]{1,0:T(8,128)S(1)}, u32[]{:S(2)}, u32[]{:S(2)}) collective-permute-start(s32[8,128]{1,0:T(8,128)S(1)} %broadcast_maximum_fusion), channel_id=1, source_target_pairs={{0,8},{2,10},{4,12},{6,14},{8,0},{10,2},{12,4},{14,6},{16,24},{18,... | collective-permute-start | bytes 12296 | tf_op jit(solution)/shard_map/ppermute | solution.py:30
  72.8 20.6 %collective-permute-start.26 = (bf16[768,384]{1,0:T(8,128)(2,1)}, bf16[768,384]{1,0:T(8,128)(2,1)}, u32[]{:S(2)}, u32[]{:S(2)}) collective-permute-start(bf16[768,384]{1,0:T(8,128)(2,1)} %collective-permute-done.18.refs_4_.refs_2_), channel_id=1, source_target_pairs={{0,4},{2,6},{4,0},{6,2},{8,12},{10,14},{12,8},{14,10},{16,20},{18,... | collective-permute-start | bytes 1769480 | tf_op jit(solution)/shard_map/ppermute | solution.py:30
  74.4 19.9 %collective-permute-start.25 = (bf16[768,384]{1,0:T(8,128)(2,1)}, bf16[768,384]{1,0:T(8,128)(2,1)S(1)}, u32[]{:S(2)}, u32[]{:S(2)}) collective-permute-start(bf16[768,384]{1,0:T(8,128)(2,1)} %collective-permute-done.18.refs_4_.refs_2_), channel_id=1, source_target_pairs={{0,2},{2,0},{4,6},{6,4},{8,10},{10,8},{12,14},{14,12},{16,18},{18,... | collective-permute-start | bytes 1769480 | tf_op jit(solution)/shard_map/ppermute | solution.py:30
  94.2 16.8 %collective-permute-start.19 = (s32[8,128]{1,0:T(8,128)S(1)}, s32[8,128]{1,0:T(8,128)S(1)}, u32[]{:S(2)}, u32[]{:S(2)}) collective-permute-start(s32[8,128]{1,0:T(8,128)S(1)} %max.16), channel_id=1, source_target_pairs={{0,4},{2,6},{4,0},{6,2},{8,12},{10,14},{12,8},{14,10},{16,20},{18,... | collective-permute-start | bytes 12296 | tf_op jit(solution)/shard_map/ppermute | solution.py:30
  126.7 66.1 %all-to-all-start = ((bf16[16,112,768]{2,1,0:T(8,128)(2,1)}), bf16[16,112,768]{2,1,0:T(8,128)(2,1)S(1)}, u32[]{:S(2)}, u32[]{:S(2)}) async-start(bf16[16,112,768]{2,1,0:T(8,128)(2,1)} %bitcast.133), calls=%async_computation | async-start | bytes 5505024 | tf_op jit(solution)/shard_map/all_to_all | solution.py:882
  133.6 53.8 %collective-permute-start.29 = (bf16[1536,768]{1,0:T(8,128)(2,1)}, bf16[1536,768]{1,0:T(8,128)(2,1)}, u32[]{:S(2)}, u32[]{:S(2)}) collective-permute-start(bf16[1536,768]{1,0:T(8,128)(2,1)} %pad_maximum_fusion.refs_0_), channel_id=1, source_target_pairs={{0,1},{1,0},{2,3},{3,2},{4,5},{5,4},{6,7},{7,6},{8,9},{9,8},{10,11... | collective-permute-start | bytes 7077896 | tf_op jit(solution)/shard_map/ppermute | solution.py:30
  134.6 60.0 %collective-permute-start.28 = (bf16[1536,768]{1,0:T(8,128)(2,1)}, bf16[1536,768]{1,0:T(8,128)(2,1)}, u32[]{:S(2)}, u32[]{:S(2)}) collective-permute-start(bf16[1536,768]{1,0:T(8,128)(2,1)} %pad_maximum_fusion.refs_0_), channel_id=1, source_target_pairs={{0,2},{2,0},{4,6},{6,4},{8,10},{10,8},{12,14},{14,12},{16,18},{18,... | collective-permute-start | bytes 7077896 | tf_op jit(solution)/shard_map/ppermute | solution.py:30
  187.4 7.2 %collective-permute-start.30 = (bf16[1536,768]{1,0:T(8,128)(2,1)}, bf16[1536,768]{1,0:T(8,128)(2,1)}, u32[]{:S(2)}, u32[]{:S(2)}) collective-permute-start(bf16[1536,768]{1,0:T(8,128)(2,1)} %collective-permute-done.29.refs_2_), channel_id=1, source_target_pairs={{0,2},{2,0},{4,6},{6,4},{8,10},{10,8},{12,14},{14,12},{16,18},{18,... | collective-permute-start | bytes 7077896 | tf_op jit(solution)/shard_map/ppermute | solution.py:30
  222.7 58.5 %all-to-all-start.1 = ((bf16[16,112,768]{2,1,0:T(8,128)(2,1)}), bf16[16,112,768]{2,1,0:T(8,128)(2,1)S(1)}, u32[]{:S(2)}, u32[]{:S(2)}) async-start(bf16[16,112,768]{2,1,0:T(8,128)(2,1)} %bitcast.139), calls=%async_computation.1 | async-start | bytes 5505024 | tf_op jit(solution)/shard_map/all_to_all | solution.py:882
  282.0 5.5 collective-permute-start.3
  309.6 65.9 %all-to-all-start.2 = ((bf16[16,112,768]{2,1,0:T(8,128)(2,1)}), bf16[16,112,768]{2,1,0:T(8,128)(2,1)S(1)}, u32[]{:S(2)}, u32[]{:S(2)}) async-start(bf16[16,112,768]{2,1,0:T(8,128)(2,1)} %bitcast.140), calls=%async_computation.2 | async-start | bytes 5505024 | tf_op jit(solution)/shard_map/all_to_all | solution.py:882
  322.9 23.9 %collective-permute-start.31 = (bf16[624,768]{1,0:T(8,128)(2,1)}, bf16[624,768]{1,0:T(8,128)(2,1)}, u32[]{:S(2)}, u32[]{:S(2)}) collective-permute-start(bf16[624,768]{1,0:T(8,128)(2,1)} %get-tuple-element.344), channel_id=1, source_target_pairs={{0,1},{1,0},{2,3},{3,2},{4,5},{5,4},{6,7},{7,6},{8,9},{9,8},{10,11... | collective-permute-start | bytes 2875400 | tf_op jit(solution)/shard_map/ppermute | solution.py:30
  403.2 78.4 %all-to-all-start.3 = ((bf16[16,112,768]{2,1,0:T(8,128)(2,1)}), bf16[16,112,768]{2,1,0:T(8,128)(2,1)S(1)}, u32[]{:S(2)}, u32[]{:S(2)}) async-start(bf16[16,112,768]{2,1,0:T(8,128)(2,1)} %bitcast.138), calls=%async_computation.3 | async-start | bytes 5505024 | tf_op jit(solution)/shard_map/all_to_all | solution.py:882
  425.7 15.2 %collective-permute-start.33 = (bf16[1536,768]{1,0:T(8,128)(2,1)}, bf16[1536,768]{1,0:T(8,128)(2,1)}, u32[]{:S(2)}, u32[]{:S(2)}) collective-permute-start(bf16[1536,768]{1,0:T(8,128)(2,1)} %shard_map.234), channel_id=1, source_target_pairs={{0,2},{2,0},{4,6},{6,4},{8,10},{10,8},{12,14},{14,12},{16,18},{18,... | collective-permute-start | bytes 7077896 | tf_op jit(solution)/shard_map/ppermute | solution.py:30
  434.5 26.1 %collective-permute-start.32 = (bf16[1536,768]{1,0:T(8,128)(2,1)}, bf16[1536,768]{1,0:T(8,128)(2,1)}, u32[]{:S(2)}, u32[]{:S(2)}) collective-permute-start(bf16[1536,768]{1,0:T(8,128)(2,1)} %shard_map.235), channel_id=1, source_target_pairs={{0,2},{2,0},{4,6},{6,4},{8,10},{10,8},{12,14},{14,12},{16,18},{18,... | collective-permute-start | bytes 7077896 | tf_op jit(solution)/shard_map/ppermute | solution.py:30
  452.9 28.7 %collective-permute-start.34 = (bf16[768,768]{1,0:T(8,128)(2,1)}, bf16[768,768]{1,0:T(8,128)(2,1)}, u32[]{:S(2)}, u32[]{:S(2)}) collective-permute-start(bf16[768,768]{1,0:T(8,128)(2,1)} %get-tuple-element.683), channel_id=1, source_target_pairs={{0,1},{1,0},{2,3},{3,2},{4,5},{5,4},{6,7},{7,6},{8,9},{9,8},{10,11... | collective-permute-start | bytes 3538952 | tf_op jit(solution)/shard_map/ppermute | solution.py:30
  494.7 26.6 %collective-permute-start.35 = (bf16[768,768]{1,0:T(8,128)(2,1)}, bf16[768,768]{1,0:T(8,128)(2,1)S(1)}, u32[]{:S(2)}, u32[]{:S(2)}) collective-permute-start(bf16[768,768]{1,0:T(8,128)(2,1)} %get-tuple-element.366), channel_id=1, source_target_pairs={{0,1},{1,0},{2,3},{3,2},{4,5},{5,4},{6,7},{7,6},{8,9},{9,8},{10,11... | collective-permute-start | bytes 3538952 | tf_op jit(solution)/shard_map/ppermute | solution.py:30
  532.2 10.1 %collective-permute-start.36 = (bf16[384,3072]{1,0:T(8,128)(2,1)}, bf16[384,3072]{1,0:T(8,128)(2,1)S(1)}, u32[]{:S(2)}, u32[]{:S(2)}) collective-permute-start(bf16[384,3072]{1,0:T(8,128)(2,1)} %get-tuple-element.373), channel_id=1, source_target_pairs={{0,2},{2,0},{4,6},{6,4},{8,10},{10,8},{12,14},{14,12},{16,18},{18,... | collective-permute-start | bytes 7077896 | tf_op jit(solution)/shard_map/ppermute | solution.py:30
  541.7 25.7 %collective-permute-start.38 = (bf16[384,3072]{1,0:T(8,128)(2,1)}, bf16[384,3072]{1,0:T(8,128)(2,1)}, u32[]{:S(2)}, u32[]{:S(2)}) collective-permute-start(bf16[384,3072]{1,0:T(8,128)(2,1)} %get-tuple-element.377), channel_id=1, source_target_pairs={{0,2},{2,0},{4,6},{6,4},{8,10},{10,8},{12,14},{14,12},{16,18},{18,... | collective-permute-start | bytes 7077896 | tf_op jit(solution)/shard_map/ppermute | solution.py:30
  548.1 28.1 %collective-permute-start.37 = (bf16[384,1536]{1,0:T(8,128)(2,1)}, bf16[384,1536]{1,0:T(8,128)(2,1)S(1)}, u32[]{:S(2)}, u32[]{:S(2)}) collective-permute-start(bf16[384,1536]{1,0:T(8,128)(2,1)} %slice.459), channel_id=1, source_target_pairs={{0,1},{1,0},{2,3},{3,2},{4,5},{5,4},{6,7},{7,6},{8,9},{9,8},{10,11... | collective-permute-start | bytes 3538952 | tf_op jit(solution)/shard_map/ppermute | solution.py:30
  588.9 5.9 collective-permute-start.39
  588.9 35.0 %collective-permute-start.43 = (bf16[192,3072]{1,0:T(8,128)(2,1)}, bf16[192,3072]{1,0:T(8,128)(2,1)}, u32[]{:S(2)}, u32[]{:S(2)}) collective-permute-start(bf16[192,3072]{1,0:T(8,128)(2,1)} %slice.460), channel_id=1, source_target_pairs={{0,4},{2,6},{4,0},{6,2},{8,12},{10,14},{12,8},{14,10},{16,20},{18,... | collective-permute-start | bytes 3538952 | tf_op jit(solution)/shard_map/ppermute | solution.py:30
  597.2 42.0 %collective-permute-start.41 = (bf16[192,4096]{1,0:T(8,128)(2,1)}, bf16[192,4096]{1,0:T(8,128)(2,1)}, u32[]{:S(2)}, u32[]{:S(2)}) collective-permute-start(bf16[192,4096]{1,0:T(8,128)(2,1)} %slice.463), channel_id=1, source_target_pairs={{0,8},{2,10},{4,12},{6,14},{8,0},{10,2},{12,4},{14,6},{16,24},{18,... | collective-permute-start | bytes 4718600 | tf_op jit(solution)/shard_map/ppermute | solution.py:30
  598.5 38.1 %collective-permute-start.42 = (bf16[192,1536]{1,0:T(8,128)(2,1)}, bf16[192,1536]{1,0:T(8,128)(2,1)}, u32[]{:S(2)}, u32[]{:S(2)}) collective-permute-start(bf16[192,1536]{1,0:T(8,128)(2,1)} %slice.462), channel_id=1, source_target_pairs={{0,4},{2,6},{4,0},{6,2},{8,12},{10,14},{12,8},{14,10},{16,20},{18,... | collective-permute-start | bytes 1769480 | tf_op jit(solution)/shard_map/ppermute | solution.py:30
  622.9 24.5 %collective-permute-start.40 = (bf16[624,768]{1,0:T(8,128)(2,1)}, bf16[624,768]{1,0:T(8,128)(2,1)}, u32[]{:S(2)}, u32[]{:S(2)}) collective-permute-start(bf16[624,768]{1,0:T(8,128)(2,1)} %get-tuple-element.403), channel_id=1, source_target_pairs={{0,1},{1,0},{2,3},{3,2},{4,5},{5,4},{6,7},{7,6},{8,9},{9,8},{10,11... | collective-permute-start | bytes 2875400 | tf_op jit(solution)/shard_map/ppermute | solution.py:30
  632.4 8.8 %collective-permute-start.44 = (bf16[384,2560]{1,0:T(8,128)(2,1)}, bf16[384,2560]{1,0:T(8,128)(2,1)S(1)}, u32[]{:S(2)}, u32[]{:S(2)}) collective-permute-start(bf16[384,2560]{1,0:T(8,128)(2,1)} %get-tuple-element.410), channel_id=1, source_target_pairs={{0,2},{2,0},{4,6},{6,4},{8,10},{10,8},{12,14},{14,12},{16,18},{18,... | collective-permute-start | bytes 5898248 | tf_op jit(solution)/shard_map/ppermute | solution.py:30
  635.5 24.6 %collective-permute-start.46 = (bf16[192,1536]{1,0:T(8,128)(2,1)}, bf16[192,1536]{1,0:T(8,128)(2,1)}, u32[]{:S(2)}, u32[]{:S(2)}) collective-permute-start(bf16[192,1536]{1,0:T(8,128)(2,1)} %slice.467), channel_id=1, source_target_pairs={{0,1},{1,0},{2,3},{3,2},{4,5},{5,4},{6,7},{7,6},{8,9},{9,8},{10,11... | collective-permute-start | bytes 1769480 | tf_op jit(solution)/shard_map/ppermute | solution.py:30
  638.6 15.9 %collective-permute-start.47 = (bf16[96,1536]{1,0:T(8,128)(2,1)}, bf16[96,1536]{1,0:T(8,128)(2,1)}, u32[]{:S(2)}, u32[]{:S(2)}) collective-permute-start(bf16[96,1536]{1,0:T(8,128)(2,1)} %slice.595), channel_id=1, source_target_pairs={{0,8},{2,10},{4,12},{6,14},{8,0},{10,2},{12,4},{14,6},{16,24},{18,... | collective-permute-start | bytes 884744 | tf_op jit(solution)/shard_map/ppermute | solution.py:30
  642.8 22.8 %collective-permute-start.52 = (bf16[192,1792]{1,0:T(8,128)(2,1)}, bf16[192,1792]{1,0:T(8,128)(2,1)}, u32[]{:S(2)}, u32[]{:S(2)}) collective-permute-start(bf16[192,1792]{1,0:T(8,128)(2,1)} %fusion.40), channel_id=1, source_target_pairs={{0,4},{2,6},{4,0},{6,2},{8,12},{10,14},{12,8},{14,10},{16,20},{18,... | collective-permute-start | bytes 2064392 | tf_op jit(solution)/shard_map/ppermute | solution.py:30
  645.2 33.1 %collective-permute-start.51 = (bf16[96,4096]{1,0:T(8,128)(2,1)}, bf16[96,4096]{1,0:T(8,128)(2,1)}, u32[]{:S(2)}, u32[]{:S(2)}) collective-permute-start(bf16[96,4096]{1,0:T(8,128)(2,1)} %slice.389), channel_id=1, source_target_pairs={{0,4},{2,6},{4,0},{6,2},{8,12},{10,14},{12,8},{14,10},{16,20},{18,... | collective-permute-start | bytes 2359304 | tf_op jit(solution)/shard_map/ppermute | solution.py:30
  653.6 11.2 %collective-permute-start.45 = (bf16[384,384]{1,0:T(8,128)(2,1)}, bf16[384,384]{1,0:T(8,128)(2,1)S(1)}, u32[]{:S(2)}, u32[]{:S(2)}) collective-permute-start(bf16[384,384]{1,0:T(8,128)(2,1)} %slice.474), channel_id=1, source_target_pairs={{0,1},{1,0},{2,3},{3,2},{4,5},{5,4},{6,7},{7,6},{8,9},{9,8},{10,11... | collective-permute-start | bytes 884744 | tf_op jit(solution)/shard_map/ppermute | solution.py:30
  655.8 24.9 %collective-permute-start.50 = (bf16[48,1536]{1,0:T(8,128)(2,1)S(1)}, bf16[48,1536]{1,0:T(8,128)(2,1)S(1)}, u32[]{:S(2)}, u32[]{:S(2)}) collective-permute-start(bf16[48,1536]{1,0:T(8,128)(2,1)S(1)} %slice.599), channel_id=1, source_target_pairs={{0,16},{2,18},{4,20},{6,22},{8,24},{10,26},{12,28},{14,30},{16,0},... | collective-permute-start | bytes 442376 | tf_op jit(solution)/shard_map/ppermute | solution.py:30
  661.4 19.3 %collective-permute-start.49 = (bf16[96,1536]{1,0:T(8,128)(2,1)S(1)}, bf16[96,1536]{1,0:T(8,128)(2,1)S(1)}, u32[]{:S(2)}, u32[]{:S(2)}) collective-permute-start(bf16[96,1536]{1,0:T(8,128)(2,1)S(1)} %slice.594), channel_id=1, source_target_pairs={{0,8},{2,10},{4,12},{6,14},{8,0},{10,2},{12,4},{14,6},{16,24},{18,... | collective-permute-start | bytes 884744 | tf_op jit(solution)/shard_map/ppermute | solution.py:30
  664.9 18.3 %collective-permute-start.48 = (bf16[192,384]{1,0:T(8,128)(2,1)S(1)}, bf16[192,384]{1,0:T(8,128)(2,1)S(1)}, u32[]{:S(2)}, u32[]{:S(2)}) collective-permute-start(bf16[192,384]{1,0:T(8,128)(2,1)S(1)} %slice.598), channel_id=1, source_target_pairs={{0,4},{2,6},{4,0},{6,2},{8,12},{10,14},{12,8},{14,10},{16,20},{18,... | collective-permute-start | bytes 442376 | tf_op jit(solution)/shard_map/ppermute | solution.py:30
  666.9 16.4 %collective-permute-start.53 = (bf16[192,896]{1,0:T(8,128)(2,1)S(1)}, bf16[192,896]{1,0:T(8,128)(2,1)S(1)}, u32[]{:S(2)}, u32[]{:S(2)}) collective-permute-start(bf16[192,896]{1,0:T(8,128)(2,1)S(1)} %slice.593), channel_id=1, source_target_pairs={{0,1},{1,0},{2,3},{3,2},{4,5},{5,4},{6,7},{7,6},{8,9},{9,8},{10,11... | collective-permute-start | bytes 1032200 | tf_op jit(solution)/shard_map/ppermute | solution.py:30
  679.6 9.3 %collective-permute-start.56 = (bf16[96,2048]{1,0:T(8,128)(2,1)S(1)}, bf16[96,2048]{1,0:T(8,128)(2,1)S(1)}, u32[]{:S(2)}, u32[]{:S(2)}) collective-permute-start(bf16[96,2048]{1,0:T(8,128)(2,1)S(1)} %slice.592), channel_id=1, source_target_pairs={{0,1},{1,0},{2,3},{3,2},{4,5},{5,4},{6,7},{7,6},{8,9},{9,8},{10,11... | collective-permute-start | bytes 1179656 | tf_op jit(solution)/shard_map/ppermute | solution.py:30
  680.8 10.7 %collective-permute-start.55 = (bf16[48,1536]{1,0:T(8,128)(2,1)S(1)}, bf16[48,1536]{1,0:T(8,128)(2,1)S(1)}, u32[]{:S(2)}, u32[]{:S(2)}) collective-permute-start(bf16[48,1536]{1,0:T(8,128)(2,1)S(1)} %slice.597), channel_id=1, source_target_pairs={{0,16},{2,18},{4,20},{6,22},{8,24},{10,26},{12,28},{14,30},{16,0},... | collective-permute-start | bytes 442376 | tf_op jit(solution)/shard_map/ppermute | solution.py:30
  683.4 9.5 %collective-permute-start.54 = (bf16[96,1280]{1,0:T(8,128)(2,1)S(1)}, bf16[96,1280]{1,0:T(8,128)(2,1)S(1)}, u32[]{:S(2)}, u32[]{:S(2)}) collective-permute-start(bf16[96,1280]{1,0:T(8,128)(2,1)S(1)} %fusion.43), channel_id=1, source_target_pairs={{0,8},{2,10},{4,12},{6,14},{8,0},{10,2},{12,4},{14,6},{16,24},{18,... | collective-permute-start | bytes 737288 | tf_op jit(solution)/shard_map/ppermute | solution.py:30
  689.0 13.2 %collective-permute-start.58 = (bf16[48,2048]{1,0:T(8,128)(2,1)S(1)}, bf16[48,2048]{1,0:T(8,128)(2,1)S(1)}, u32[]{:S(2)}, u32[]{:S(2)}) collective-permute-start(bf16[48,2048]{1,0:T(8,128)(2,1)S(1)} %slice.596), channel_id=1, source_target_pairs={{0,16},{2,18},{4,20},{6,22},{8,24},{10,26},{12,28},{14,30},{16,0},... | collective-permute-start | bytes 589832 | tf_op jit(solution)/shard_map/ppermute | solution.py:30
  693.0 11.0 %collective-permute-start.57 = (bf16[48,1280]{1,0:T(8,128)(2,1)S(1)}, bf16[48,1280]{1,0:T(8,128)(2,1)S(1)}, u32[]{:S(2)}, u32[]{:S(2)}) collective-permute-start(bf16[48,1280]{1,0:T(8,128)(2,1)S(1)} %slice.600), channel_id=1, source_target_pairs={{0,16},{2,18},{4,20},{6,22},{8,24},{10,26},{12,28},{14,30},{16,0},... | collective-permute-start | bytes 368648 | tf_op jit(solution)/shard_map/ppermute | solution.py:30
  (52 other events, 260.4 us)

commit v4 on v3

--- a/solution.py
+++ b/solution.py
@@ -469,7 +469,10 @@
     count = (len(refs) - 2) // 2
     lefts, rights, (keep_ref, send_ref) = refs[:count], refs[count:-2], refs[-2:]
     half = keep_ref.shape[0]
-    turned = [mm(mover_ref[...], left[...], NT).astype(BF) for left in lefts]
+    turned = [
+        left[...] if left.shape[0] == half * 2 else mm(mover_ref[...], left[...], NT).astype(BF)
+        for left in lefts
+    ]
     at = 0
     columns = keep_ref.shape[1] // groups
     for left, right in zip(turned, rights):
@@ -501,7 +504,7 @@
     columns = sum(r.size // r.shape[-2] for _, r in pairs)
     columns += groups * -(-sum(r.shape[0] for r in stats) // 128) * 128
     out = shape(width // 2, columns)
-    rows = pairs[0][0].shape[0]
+    rows = pairs[0][1].shape[-2]
     operands = [mover, *stats] + [p[0] for p in pairs] + [p[1] for p in pairs]
     return pl.pallas_call(
         functools.partial(weight_kernel, groups, len(stats)),
@@ -610,21 +613,19 @@
     refs[-1][...] = part.astype(refs[-1].dtype)
 
 
-def expert_grads(left, right, width, span, odd, got=None, cut_left=True):
+def expert_grads(left, right, width, span, first, count, got=None, skip=0, cut_left=True):
     rows = left.shape[0]
-    wide = left.shape[1] if cut_left else right.shape[1]
-    count = wide // (2 * span)
     high, low = (span, width) if cut_left else (width, span)
-    cut = pl.BlockSpec((rows, span), lambda j: (0, 2 * j + odd))
+    cut = pl.BlockSpec((rows, span), lambda j: (0, 2 * j + first))
     whole = pl.BlockSpec((rows, width), lambda j: (0, 0))
-    block = pl.BlockSpec((high, low), lambda j: (j, 0))
     more = () if got is None else (got,)
     out = shape(count * high, low)
     return pl.pallas_call(
         outer_kernel,
         grid=(count,),
-        in_specs=([cut, whole] if cut_left else [whole, cut]) + [block] * len(more),
-        out_specs=block,
+        in_specs=([cut, whole] if cut_left else [whole, cut])
+        + [pl.BlockSpec((high, low), lambda j: (j + skip, 0))] * len(more),
+        out_specs=pl.BlockSpec((high, low), lambda j: (j, 0)),
         out_shape=out,
         cost_estimate=cost_of(2 * out.size * rows, 2 * (left.size + right.size + 2 * out.size)),
     )(left, right, *more)
@@ -906,11 +907,32 @@
     scale = (local_rows * owners / valid_count) * valid_rows
     rows_in = pinned(rows_in, teacher_rel, scale)
     expert_rows, act, slope = expert_forward(rows_in, expert_parts)
+    block = width // owners
+    feature = jnp.arange(width, dtype=jnp.int32)
+
+    def mover_of(distances):
+        ahead, turned = feature // block, 0
+        for distance in reversed(distances):
+            turned = turned + distance * (ahead % 2)
+            ahead = ahead // 2
+        source = (turned ^ place) * block + feature % block
+        return (source[:, None] == feature[None, :]).astype(BF)
+
+    mover = mover_of(distances)
+    turned_order = [1, 4, 2] + distances[3:]
+    mover_turned = mover_of(turned_order)
+
     pairs = [x.astype(F32) for x in (local_row, *guest_out)]
     pack = jnp.concatenate([gate_vals, scale] + pairs, 1)
     pack = jnp.pad(pack, ((0, 0), (0, 128 - pack.shape[1])))
     merged = across(expert_rows)
-    merged, pack = pinned_all((merged, pack), expert_rows)
+    turned_rows = [
+        mm(m, pinned(rows, expert_rows), NT).astype(BF)
+        for m, rows in (
+            (mover, normed_second), (mover_turned, normed_dense), (mover, normed_first)
+        )
+    ]
+    merged, pack, *turned_rows = pinned_all((merged, pack, *turned_rows), expert_rows)
 
     outs = (shape(own_rows, width), shape(own_rows, width, kind=F32), shape(own_rows, width))
 
@@ -954,7 +976,6 @@
     grad_rows, grad_hidden = expert_backward(
         pinned(grad_out_rows, *final_far), slope, expert_parts
     )
-    activations = absolute(jnp.concatenate([final_low] + list(pinned_all(final_far, grad_rows)), 0))
     grad_back = across(grad_rows)
 
     def start_groups(total):
@@ -988,29 +1009,33 @@
         grad_own.append(total)
     grad_own = jnp.stack(grad_own, 1)
     span = expert_in.shape[2]
-    sent = mark(expert_grads(act, grad_out_rows, width, span, 1))
+    def both_shares(left, right, got, cut_left):
+        others = groups - 1
+        sent = mark(
+            expert_grads(after(left), right, width, span, 2, others, after(got), 1, cut_left)
+        )
+        keep = mark(expert_grads(after(left), right, width, span, 0, 1, got, 0, cut_left))
+        rows = sent.shape[0] // others
+        return keep, [sent[d * rows : (d + 1) * rows] for d in range(others)]
+
+    sent = mark(expert_grads(act, grad_out_rows, width, span, 1, groups))
     got_eo = along([sent], 1)[0]
-    sent = mark(expert_grads(after(rows_in), grad_hidden, width, span, 1, None, False))
-    got_ei = along([sent], 1)[0]
-
-    def shares_of(total, rows):
-        return total[:rows], [total[d * rows : (d + 1) * rows] for d in range(1, groups)]
-
-    keep_eo, sent_eo = shares_of(
-        mark(expert_grads(act, grad_out_rows, width, span, 0, after(got_eo))), span
-    )
-    got_eo = cross(sent_eo)
-    keep_ei, sent_ei = shares_of(
-        mark(expert_grads(rows_in, grad_hidden, width, span, 0, after(got_ei), False)), width
-    )
-
     own_gates = gate_vals
     grad_chosen = own_gates * (grad_own - jnp.sum(own_gates * grad_own, axis=1, keepdims=True))
     grad_logits = jnp.sum(
         jnp.where(picker, grad_chosen[:, :, None], 0.0), axis=1
     ).astype(BF)
     grad_router = mm(grad_logits, normed_expert, TN)
-    grad_back = pinned(grad_back, *sent_ei, *got_eo, grad_router, activations)
+    sent = mark(
+        expert_grads(after(rows_in), grad_hidden, width, span, 1, groups, None, 0, False)
+    )
+    got_ei = along([sent], 1)[0]
+    keep_eo, sent_eo = both_shares(act, grad_out_rows, got_eo, True)
+    got_eo = cross(sent_eo)
+    activations = absolute(jnp.concatenate([final_low] + list(pinned_all(final_far, keep_eo)), 0))
+    mark(activations)
+    keep_ei, sent_ei = both_shares(rows_in, grad_hidden, got_ei, False)
+    grad_back = pinned(grad_back, *sent_ei, keep_ei, *got_eo, activations, grad_router)
 
     outs = (shape(1, width, kind=F32),) * 2 + (
         shape(own_rows, width, kind=F32), shape(own_rows, width),
@@ -1031,21 +1056,6 @@
     gain_four, bias_four, grad_second, low_second = sized(combine_back, grad_back)
     got_ei = cross([pinned(p, grad_second) for p in sent_ei])
 
-    block = width // owners
-    feature = jnp.arange(width, dtype=jnp.int32)
-
-    def mover_of(distances):
-        ahead, turned = feature // block, 0
-        for distance in reversed(distances):
-            turned = turned + distance * (ahead % 2)
-            ahead = ahead // 2
-        source = (turned ^ place) * block + feature % block
-        return (source[:, None] == feature[None, :]).astype(BF)
-
-    mover = mover_of(distances)
-    turned_order = [1, 4, 2] + distances[3:]
-    mover_turned = mover_of(turned_order)
-
     mark(grad_second)
     def arrive(keep, got):
         return finish(keep, [after(x) for x in got])
@@ -1059,7 +1069,7 @@
     keep_a, send_a = weight_grads(
         groups,
         mover,
-        [(pinned(normed_second, *got_ei), grads_second), (low_second, mixed_second)],
+        [(pinned(turned_rows[0], *got_ei), grads_second), (low_second, mixed_second)],
     )
     mark(send_a)
     got_a = along([send_a], 1)
@@ -1084,7 +1094,7 @@
         groups,
         mover_turned,
         [
-            (pinned(normed_dense, *got_a), grad_hidden),
+            (pinned(turned_rows[1], *got_a), grad_hidden),
             (low_first, mixed_first),
         ],
         stats + [grad_router],
@@ -1107,7 +1117,7 @@
     keep_d, send_d = weight_grads(
         groups,
         mover,
-        [(pinned(normed_first, *got_b), grads_first)],
+        [(pinned(turned_rows[2], *got_b), grads_first)],
         [gain_one, bias_one],
     )
     mark(send_d)

time: 711 us -> 708 us (level)
  waiting for transfers between devices: 229 us -> 213 us
  matrix products: 7.86 us -> 15.7 us
  local copies, waits for them, and re-layouts: 59.5 us -> 52.1 us
  starting transfers between devices: 86.8 us -> 94 us
    ppermute x55, waiting for transfers between devices: 150 us -> 142 us  [swap(): return lax.ppermute(value, axis, [(k, k ^ distance) for k in range(size)])]
    all_to_all x4, waiting for transfers between devices: 79.2 us -> 71.3 us  [across(): lax.all_to_all(rows.reshape(owners, part, width), 'expert', split_axis=0,...]
    dot_general x6 -> x9, matrix products: 7.86 us -> 15.7 us  [mm(): return lax.dot_general(a, b, (dims, ((), ())), preferred_element_type=F32)]
    pallas_call x4 -> x6, Pallas kernels: 34.2 us -> 41.9 us  [expert_grads(): pl.pallas_call(outer_kernel, grid=(count,), in_specs=([cut, whole] if cut...]
  transfers between devices with their start and end apart: 59 -> 59, of which waited for: 27 -> 26; matrix products, arithmetic and copies ran while one was open for 14% -> 15% of each run, Pallas kernels for 22% -> 24%
where the time goes in v4:
time: 708 us; the launch traced here: 704 us
  Pallas kernels  268 us (38%)
  waiting for transfers between devices  213 us (30%)
  starting transfers between devices  94 us (13%)
  other arithmetic  57 us (8%)
  local copies, waits for them, and re-layouts  52.1 us (7%)
  matrix products  15.7 us (2%)
    ppermute x55, waiting for transfers between devices, swap(): return lax.ppermute(value, axis, [(k, k ^ distance) for k in range(size)])  142 us
    pallas_call x6, Pallas kernels, dense_call(): pl.pallas_call(kernel, grid=(rows[0].shape[-2] // ROWS,), in_specs=specs,...  106 us
    all_to_all x4, waiting for transfers between devices, across(): lax.all_to_all(rows.reshape(owners, part, width), 'expert', split_axis=0,...  71.3 us
    ppermute x55, starting transfers between devices, swap(): return lax.ppermute(value, axis, [(k, k ^ distance) for k in range(size)])  56.5 us
    pallas_call x2, Pallas kernels, expert_call(): pl.pallas_call(kernel, grid=(count // tile,), in_specs=[image_spec(tile,...  54.3 us
    pallas_call x6, Pallas kernels, expert_grads(): pl.pallas_call(outer_kernel, grid=(count,), in_specs=([cut, whole] if cut...  41.9 us
    pallas_call x4, Pallas kernels, weight_grads(): pl.pallas_call(functools.partial(weight_kernel, groups, len(stats)), in_s...  38.9 us
    all_to_all x4, starting transfers between devices, across(): lax.all_to_all(rows.reshape(owners, part, width), 'expert', split_axis=0,...  37.6 us
  transfers between devices with their start and end apart: 59, of which 26 were waited for; matrix products, arithmetic and copies ran while one was open for 15% of the time, Pallas kernels for 24%

profile of v4, /device:TPU:0, one launch (start us, length us, event | category | flops | bytes accessed | tf_op | source)
XLA Modules:
  0.0 704.1 jit_solution(1817640031119156293)
XLA Ops:
  23.7 4.8 reduce-window.14
  40.0 13.4 %shard_map.229 = (f32[624,768]{1,0:T(8,128)}, bf16[624,768]{1,0:T(8,128)(2,1)}, bf16[3,624,768]{2,1,0:T(8,128)(2,1)}, bf16[624,768]{1,0:T(8,128)(2,1)}, f32[624,128]{1,0:T(8,128)}) custom-call(s32[1]{0:T(128)} %bitcast.9.place_ref, f32[624,768]{1,0:T(8,128)} %bitcast_convert_fusion.x_ref, f32[1,768]{1,0:T(1,128)} %get-tuple-element.739.gain_ref, ...), custom_call_target="tpu_custom_call" | custom-call | flops 668624512 | bytes 3204710 | tf_op jit(solution)/shard_map/pallas_call | solution.py:312
  56.6 12.2 %collective-permute-done.10 = s32[8,128]{1,0:T(8,128)S(1)} collective-permute-done((s32[8,128]{1,0:T(8,128)S(1)}, s32[8,128]{1,0:T(8,128)S(1)}, u32[]{:S(2)}, u32[]{:S(2)}) %collective-permute-start.10) | collective-permute-done | bytes 4128 | tf_op jit(solution)/shard_map/ppermute | solution.py:30
  77.8 15.5 %shard_map.230 = (f32[624,768]{1,0:T(8,128)}, bf16[624,768]{1,0:T(8,128)(2,1)}, bf16[624,3072]{1,0:T(8,128)(2,1)}, bf16[624,3072]{1,0:T(8,128)(2,1)}) custom-call(s32[1]{0:T(128)} %bitcast.9.place_ref, f32[624,768]{1,0:T(8,128)} %get-tuple-element.337.x_ref, f32[1,768]{1,0:T(1,128)} %get-tuple-element.740.gain_ref, f32[1,768]{1,0:T(1,128)} %get-tuple-element.725.bias_ref, ...), custom_call_target="tpu_custom_call" | custom-call | flops 1177760512 | bytes 4379443 | tf_op jit(solution)/shard_map/pallas_call | solution.py:312
  96.5 14.3 %shard_map.231 = (f32[624,768]{1,0:T(8,128)}, bf16[624,768]{1,0:T(8,128)(2,1)}, bf16[3,624,768]{2,1,0:T(8,128)(2,1)}, bf16[624,768]{1,0:T(8,128)(2,1)}, f32[624,128]{1,0:T(8,128)}, /*index=5*/bf16[624,768]{1,0:T(8,128)(2,1)}) custom-call(s32[1]{0:T(128)} %bitcast.9.place_ref, f32[624,768]{1,0:T(8,128)} %get-tuple-element.340.x_ref, ...), custom_call_target="tpu_custom_call" | custom-call | flops 668624512 | bytes 3396403 | tf_op jit(solution)/shard_map/pallas_call | solution.py:312
  112.0 12.9 %conditional.4 = (bf16[1792,768]{1,0:T(8,128)(2,1)S(1)}) conditional(s32[]{:T(128)} %bitcast.12, (s32[528]{0:T(1024)S(1)}, s32[624,2]{0,1:T(2,128)S(1)}, bf16[624,768]{1,0:T(8,128)(2,1)}, f32[1]{0:T(128)}, s32[2,624]{1,0:T(2,128)S(1)}) %tuple.280, (s32[528]{0:T(1024)S(1)}, s32[624,2]{0,1:T(2,128)S(1)}, bf16[624,768]{1,0:T(8,128)(2,1)}, ...), branch_computations={%region_22.23_spmd, %region_23.24_spmd} | conditional | flops 850976384 | bytes 9024003 | solution.py:877
  115.0 3.3 collective-permute-done.1.refs_1_
  119.0 5.9 branch_1_fun.4
  126.4 3.7 all-to-all-start
  134.4 52.8 %collective-permute-done.29.refs_2_ = bf16[1536,768]{1,0:T(8,128)(2,1)} collective-permute-done((bf16[1536,768]{1,0:T(8,128)(2,1)}, bf16[1536,768]{1,0:T(8,128)(2,1)}, u32[]{:S(2)}, u32[]{:S(2)}) %collective-permute-start.29) | collective-permute-done | bytes 2359328 | tf_op jit(solution)/shard_map/ppermute | solution.py:30
  187.1 3.2 reshape.655
  194.4 28.1 %shard_map.232 = (bf16[1792,768]{1,0:T(8,128)(2,1)}, bf16[1792,3072]{1,0:T(8,128)(2,1)}, bf16[1792,3072]{1,0:T(8,128)(2,1)}) custom-call(bf16[1792,768]{1,0:T(8,128)(2,1)} %bitcast.132, bf16[1536,768]{1,0:T(8,128)(2,1)} %pad_maximum_fusion.refs_0_, bf16[1536,768]{1,0:T(8,128)(2,1)} %collective-permute-done.28.refs_1_, ...), custom_call_target="tpu_custom_call" | custom-call | flops 3382286848 | bytes 7392460 | tf_op jit(solution)/shard_map/pallas_call | solution.py:441
  222.5 6.4 all-to-all-start.1
  231.0 3.4 fusion.43.refs_0_
  238.8 42.7 %all-to-all-done.1 = bf16[16,112,768]{2,1,0:T(8,128)(2,1)S(1)} async-done(((bf16[16,112,768]{2,1,0:T(8,128)(2,1)}), bf16[16,112,768]{2,1,0:T(8,128)(2,1)S(1)}, u32[]{:S(2)}, u32[]{:S(2)}) %all-to-all-start.1) | async-done | bytes 2752544 | tf_op jit(solution)/shard_map/all_to_all | solution.py:883
  281.4 13.5 %conditional.5 = (bf16[624,768]{1,0:T(8,128)(2,1)}, f32[624,768]{1,0:T(8,128)}, bf16[624,768]{1,0:T(8,128)(2,1)}, bf16[528,768]{1,0:T(8,128)(2,1)}) conditional(s32[]{:T(128)} %bitcast.12, (s32[528]{0:T(1024)S(1)}, s32[1792]{0:T(1024)S(1)}, bf16[1792,768]{1,0:T(8,128)(2,1)S(1)}, f32[624,128]{0,1:T(8,128)S(1)}, f32[624,768]{1,0:T(8,128)}, ...), branch_computations={%region_28.29_spmd, %region_29.30_spmd} | conditional | flops 1798191488 | bytes 9574331 | solution.py:877
  284.0 3.6 collective-permute-done.3.refs_1_
  288.6 6.3 branch_1_fun.5
  294.9 14.7 %conditional.6 = (bf16[1792,768]{1,0:T(8,128)(2,1)}, f32[1792,1]{1,0:T(8,128)}, f32[528,1]{0,1:T(1,128)S(1)}) conditional(s32[]{:T(128)} %bitcast.12, (s32[528]{0:T(1024)S(1)}, s32[624,2]{0,1:T(2,128)S(1)}, f32[2,624]{1,0:T(2,128)S(1)}, bf16[624,768]{1,0:T(8,128)(2,1)}, f32[1]{0:T(128)}, /*index=5*/s32[2,624]{1,0:T(2,128)S(1)}, ...), branch_computations={%region_30.33_spmd, %region_33.36_spmd} | conditional | flops 854574208 | bytes 6616499 | solution.py:877
  302.0 7.6 %branch_1_fun.6 = (bf16[1792,768]{1,0:T(8,128)(2,1)}, f32[1792,1]{1,0:T(8,128)}) custom-call(f32[1]{0:T(128)} %get-tuple-element.153.extra_ref, s32[2,624]{1,0:T(2,128)S(1)} %get-tuple-element.154.lines_ref, f32[2,624]{1,0:T(2,128)S(1)} %get-tuple-element.155.gates_ref, bf16[624,768]{1,0:T(8,128)(2,1)} %get-tuple-element.156.rows_ref, ...), custom_call_target="tpu_custom_call" | custom-call | flops 343513504 | bytes 742195 | tf_op jit(solution)/shard_map/cond/branch_1_fun/pallas_call | solution.py:553
  309.6 13.6 %all-to-all-start.2 = ((bf16[16,112,768]{2,1,0:T(8,128)(2,1)}), bf16[16,112,768]{2,1,0:T(8,128)(2,1)S(1)}, u32[]{:S(2)}, u32[]{:S(2)}) async-start(bf16[16,112,768]{2,1,0:T(8,128)(2,1)} %bitcast.145), calls=%async_computation.2 | async-start | bytes 5505024 | tf_op jit(solution)/shard_map/all_to_all | solution.py:883
  324.3 22.8 %collective-permute-done.31 = bf16[624,768]{1,0:T(8,128)(2,1)} collective-permute-done((bf16[624,768]{1,0:T(8,128)(2,1)}, bf16[624,768]{1,0:T(8,128)(2,1)}, u32[]{:S(2)}, u32[]{:S(2)}) %collective-permute-start.31) | collective-permute-done | bytes 958496 | tf_op jit(solution)/shard_map/ppermute | solution.py:30
  347.1 28.7 %all-to-all-done.2 = bf16[16,112,768]{2,1,0:T(8,128)(2,1)S(1)} async-done(((bf16[16,112,768]{2,1,0:T(8,128)(2,1)}), bf16[16,112,768]{2,1,0:T(8,128)(2,1)S(1)}, u32[]{:S(2)}, u32[]{:S(2)}) %all-to-all-start.2) | async-done | bytes 2752544 | tf_op jit(solution)/shard_map/all_to_all | solution.py:883
  377.3 26.2 %shard_map.233 = (bf16[1792,768]{1,0:T(8,128)(2,1)}, bf16[1792,3072]{1,0:T(8,128)(2,1)}) custom-call(bf16[1792,768]{1,0:T(8,128)(2,1)} %bitcast.127, bf16[1792,3072]{1,0:T(8,128)(2,1)} %get-tuple-element.364.slope_ref, bf16[1536,768]{1,0:T(8,128)(2,1)} %pad_maximum_fusion.refs_0_, bf16[1536,768]{1,0:T(8,128)(2,1)} %collective-permute-done.28.refs_1_, ...), custom_call_target="tpu_custom_call" | custom-call | flops 3382286848 | bytes 7392460 | tf_op jit(solution)/shard_map/pallas_call | solution.py:441
  403.5 13.8 %all-to-all-start.3 = ((bf16[16,112,768]{2,1,0:T(8,128)(2,1)}), bf16[16,112,768]{2,1,0:T(8,128)(2,1)S(1)}, u32[]{:S(2)}, u32[]{:S(2)}) async-start(bf16[16,112,768]{2,1,0:T(8,128)(2,1)} %bitcast.143), calls=%async_computation.3 | async-start | bytes 5505024 | tf_op jit(solution)/shard_map/all_to_all | solution.py:883
  417.4 8.4 %shard_map.234 = bf16[1536,768]{1,0:T(8,128)(2,1)} custom-call(bf16[1792,3072]{1,0:T(8,128)(2,1)} %get-tuple-element.372.left_ref, bf16[1792,768]{1,0:T(8,128)(2,1)} %bitcast.128), custom_call_target="tpu_custom_call" | custom-call | flops 845571712 | bytes 3696230 | tf_op jit(solution)/shard_map/pallas_call | solution.py:623
  426.1 8.3 %shard_map.235 = bf16[1536,768]{1,0:T(8,128)(2,1)} custom-call(bf16[1792,768]{1,0:T(8,128)(2,1)} %bitcast.133, bf16[1792,3072]{1,0:T(8,128)(2,1)} %get-tuple-element.369.right_ref), custom_call_target="tpu_custom_call" | custom-call | flops 845571712 | bytes 3696230 | tf_op jit(solution)/shard_map/pallas_call | solution.py:623
  437.9 6.4 shard_map.236
  447.3 6.3 shard_map.237
  460.1 6.3 shard_map.238
  466.3 6.3 shard_map.239
  472.9 13.0 %conditional.7 = ((f32[1,768]{1,0:T(1,128)S(1)}, f32[1,768]{1,0:T(1,128)S(1)}, f32[624,768]{1,0:T(8,128)}, bf16[624,768]{1,0:T(8,128)(2,1)})) conditional(s32[]{:T(128)} %bitcast.12, (s32[528]{0:T(1024)S(1)}, s32[1792]{0:T(1024)S(1)}, bf16[1792,768]{1,0:T(8,128)(2,1)S(1)}, f32[624,128]{0,1:T(8,128)S(1)}, f32[624,768]{1,0:T(8,128)}, ...), branch_computations={%region_42.43_spmd, %region_43.44_spmd} | conditional | flops 1798191488 | bytes 9625148 | solution.py:877
  479.3 6.7 branch_1_fun.7
  488.3 23.2 %shard_map.240 = (bf16[3,624,768]{2,1,0:T(8,128)(2,1)}, f32[1,768]{1,0:T(1,128)}, f32[1,768]{1,0:T(1,128)}, f32[624,768]{1,0:T(8,128)}, bf16[624,768]{1,0:T(8,128)(2,1)}) custom-call(s32[1]{0:T(128)} %bitcast.9.place_ref, f32[624,768]{1,0:T(8,128)} %get-tuple-element.381.grad_ref, f32[624,768]{1,0:T(8,128)} %get-tuple-element.340.x_ref, ...), custom_call_target="tpu_custom_call" | custom-call | flops 788240768 | bytes 3972710 | tf_op jit(solution)/shard_map/pallas_call | solution.py:312
  512.8 10.0 %shard_map.241 = (bf16[384,3072]{1,0:T(8,128)(2,1)}, bf16[384,3072]{1,0:T(8,128)(2,1)}) custom-call(bf16[768,768]{1,0:T(8,128)(2,1)} %fusion.40.mover_ref, bf16[768,624]{1,0:T(8,128)(2,1)} %fusion.43.refs_0_, bf16[624,768]{1,0:T(8,128)(2,1)S(1)} %copy-done.28, bf16[3,624,768]{2,1,0:T(8,128)(2,1)} %get-tuple-element.390.refs_2_, ...), custom_call_target="tpu_custom_call" | custom-call | flops 588880256 | bytes 2329804 | tf_op jit(solution)/shard_map/pallas_call | solution.py:509
  522.8 9.5 %shard_map.242 = (bf16[384,3072]{1,0:T(8,128)(2,1)}, bf16[384,3072]{1,0:T(8,128)(2,1)}) custom-call(bf16[768,768]{1,0:T(8,128)(2,1)} %fusion.40.mover_ref, bf16[624,768]{1,0:T(8,128)(2,1)} %get-tuple-element.395.refs_0_, bf16[624,3072]{1,0:T(8,128)(2,1)} %get-tuple-element.396.refs_1_), custom_call_target="tpu_custom_call" | custom-call | flops 588880256 | bytes 2138112 | tf_op jit(solution)/shard_map/pallas_call | solution.py:509
  534.2 3.3 add_convert_fusion.2
  541.3 17.1 %shard_map.243 = (bf16[624,3072]{1,0:T(8,128)(2,1)}, f32[1,768]{1,0:T(1,128)}, f32[1,768]{1,0:T(1,128)}, f32[624,768]{1,0:T(8,128)}, bf16[624,768]{1,0:T(8,128)(2,1)}) custom-call(s32[1]{0:T(128)} %bitcast.9.place_ref, f32[624,768]{1,0:T(8,128)} %get-tuple-element.399.grad_ref, f32[624,768]{1,0:T(8,128)} %get-tuple-element.337.x_ref, ...), custom_call_target="tpu_custom_call" | custom-call | flops 1177760512 | bytes 4764057 | tf_op jit(solution)/shard_map/pallas_call | solution.py:312
  558.4 3.3 add_convert_fusion.1
  566.7 11.8 %shard_map.244 = (bf16[384,4096]{1,0:T(8,128)(2,1)}, bf16[384,4096]{1,0:T(8,128)(2,1)}) custom-call(bf16[768,768]{1,0:T(8,128)(2,1)} %fusion.38.mover_ref, f32[1,768]{1,0:T(1,128)} %get-tuple-element.402.refs_0_, f32[1,768]{1,0:T(1,128)} %get-tuple-element.403.refs_1_, f32[1,768]{1,0:T(1,128)S(1)} %get-tuple-element.404.refs_2_, ...), custom_call_target="tpu_custom_call" | custom-call | flops 785173696 | bytes 2840371 | tf_op jit(solution)/shard_map/pallas_call | solution.py:509
  586.9 6.0 collective-permute-start.41
  592.9 4.2 collective-permute-start.42
  597.1 22.9 %shard_map.245 = (bf16[3,624,768]{2,1,0:T(8,128)(2,1)}, f32[1,768]{1,0:T(1,128)}, f32[1,768]{1,0:T(1,128)}, bf16[624,768]{1,0:T(8,128)(2,1)}) custom-call(s32[1]{0:T(128)} %bitcast.9.place_ref, f32[624,768]{1,0:T(8,128)} %get-tuple-element.420.grad_ref, f32[624,768]{1,0:T(8,128)} %bitcast_convert_fusion.x_ref, ...), custom_call_target="tpu_custom_call" | custom-call | flops 788240768 | bytes 3589324 | tf_op jit(solution)/shard_map/pallas_call | solution.py:312
  621.1 7.5 %shard_map.246 = (bf16[384,2560]{1,0:T(8,128)(2,1)}, bf16[384,2560]{1,0:T(8,128)(2,1)}) custom-call(bf16[768,768]{1,0:T(8,128)(2,1)} %fusion.40.mover_ref, f32[1,768]{1,0:T(1,128)} %get-tuple-element.425.refs_0_, f32[1,768]{1,0:T(1,128)} %get-tuple-element.426.refs_1_, bf16[768,624]{1,0:T(8,128)(2,1)} %fusion.44.refs_2_, ...), custom_call_target="tpu_custom_call" | custom-call | flops 490733568 | bytes 1789747 | tf_op jit(solution)/shard_map/pallas_call | solution.py:509
  658.6 3.4 collective-permute-done.45
  664.9 9.4 %collective-permute-done.51 = bf16[96,4096]{1,0:T(8,128)(2,1)} collective-permute-done((bf16[96,4096]{1,0:T(8,128)(2,1)}, bf16[96,4096]{1,0:T(8,128)(2,1)}, u32[]{:S(2)}, u32[]{:S(2)}) %collective-permute-start.51) | collective-permute-done | bytes 786464 | tf_op jit(solution)/shard_map/ppermute | solution.py:30
  680.2 5.1 collective-permute-done.56
  694.0 4.8 collective-permute-done.58
  (392 shorter events, 177.5 us)
Async XLA Ops:
  3.8 17.4 %collective-permute-start.8 = (bf16[768,384]{1,0:T(8,128)(2,1)}, bf16[768,384]{1,0:T(8,128)(2,1)}, u32[]{:S(2)}, u32[]{:S(2)}) collective-permute-start(bf16[768,384]{1,0:T(8,128)(2,1)} %pad_maximum_fusion.6), channel_id=1, source_target_pairs={{0,1},{1,0},{2,3},{3,2},{4,5},{5,4},{6,7},{7,6},{8,9},{9,8},{10,11... | collective-permute-start | bytes 1769480 | tf_op jit(solution)/shard_map/ppermute | solution.py:30
  8.7 28.9 %collective-permute-start.11 = (bf16[192,1536]{1,0:T(8,128)(2,1)}, bf16[192,1536]{1,0:T(8,128)(2,1)S(1)}, u32[]{:S(2)}, u32[]{:S(2)}) collective-permute-start(bf16[192,1536]{1,0:T(8,128)(2,1)} %constant_dynamic-slice_fusion.5), channel_id=1, source_target_pairs={{0,1},{1,0},{2,3},{3,2},{4,5},{5,4},{6,7},{7,6},{8,9},{9,8},{10,11... | collective-permute-start | bytes 1769480 | tf_op jit(solution)/shard_map/ppermute | solution.py:30
  10.6 42.8 %collective-permute-start.16 = (bf16[384,768]{1,0:T(8,128)(2,1)}, bf16[384,768]{1,0:T(8,128)(2,1)S(1)}, u32[]{:S(2)}, u32[]{:S(2)}) collective-permute-start(bf16[384,768]{1,0:T(8,128)(2,1)} %constant_dynamic-slice_fusion.4), channel_id=1, source_target_pairs={{0,1},{1,0},{2,3},{3,2},{4,5},{5,4},{6,7},{7,6},{8,9},{9,8},{10,11... | collective-permute-start | bytes 1769480 | tf_op jit(solution)/shard_map/ppermute | solution.py:30
  21.2 13.9 %collective-permute-start.12 = (bf16[768,384]{1,0:T(8,128)(2,1)}, bf16[768,384]{1,0:T(8,128)(2,1)S(1)}, u32[]{:S(2)}, u32[]{:S(2)}) collective-permute-start(bf16[768,384]{1,0:T(8,128)(2,1)} %collective-permute-done.8.refs_2_), channel_id=1, source_target_pairs={{0,4},{2,6},{4,0},{6,2},{8,12},{10,14},{12,8},{14,10},{16,20},{18,... | collective-permute-start | bytes 1769480 | tf_op jit(solution)/shard_map/ppermute | solution.py:30
  23.3 15.8 %collective-permute-start.14 = (bf16[768,384]{1,0:T(8,128)(2,1)}, bf16[768,384]{1,0:T(8,128)(2,1)S(1)}, u32[]{:S(2)}, u32[]{:S(2)}) collective-permute-start(bf16[768,384]{1,0:T(8,128)(2,1)} %collective-permute-done.8.refs_2_), channel_id=1, source_target_pairs={{0,2},{2,0},{4,6},{6,4},{8,10},{10,8},{12,14},{14,12},{16,18},{18,... | collective-permute-start | bytes 1769480 | tf_op jit(solution)/shard_map/ppermute | solution.py:30
  35.4 36.9 %collective-permute-start.18 = (bf16[768,384]{1,0:T(8,128)(2,1)}, bf16[768,384]{1,0:T(8,128)(2,1)}, u32[]{:S(2)}, u32[]{:S(2)}) collective-permute-start(bf16[768,384]{1,0:T(8,128)(2,1)} %pad_maximum_fusion.7), channel_id=1, source_target_pairs={{0,1},{1,0},{2,3},{3,2},{4,5},{5,4},{6,7},{7,6},{8,9},{9,8},{10,11... | collective-permute-start | bytes 1769480 | tf_op jit(solution)/shard_map/ppermute | solution.py:30
  37.6 35.7 %collective-permute-start.21 = (bf16[192,1536]{1,0:T(8,128)(2,1)S(1)}, bf16[192,1536]{1,0:T(8,128)(2,1)S(1)}, u32[]{:S(2)}, u32[]{:S(2)}) collective-permute-start(bf16[192,1536]{1,0:T(8,128)(2,1)S(1)} %collective-permute-done.11.refs_2_), channel_id=1, source_target_pairs={{0,4},{2,6},{4,0},{6,2},{8,12},{10,14},{12,8},{14,10},{16,20},{18,... | collective-permute-start | bytes 1769480 | tf_op jit(solution)/shard_map/ppermute | solution.py:30
  53.5 19.3 %collective-permute-start.17 = (bf16[384,768]{1,0:T(8,128)(2,1)S(1)}, bf16[384,768]{1,0:T(8,128)(2,1)S(1)}, u32[]{:S(2)}, u32[]{:S(2)}) collective-permute-start(bf16[384,768]{1,0:T(8,128)(2,1)S(1)} %collective-permute-done.16.refs_6_), channel_id=1, source_target_pairs={{0,8},{2,10},{4,12},{6,14},{8,0},{10,2},{12,4},{14,6},{16,24},{18,... | collective-permute-start | bytes 1769480 | tf_op jit(solution)/shard_map/ppermute | solution.py:30
  55.8 13.0 %collective-permute-start.10 = (s32[8,128]{1,0:T(8,128)S(1)}, s32[8,128]{1,0:T(8,128)S(1)}, u32[]{:S(2)}, u32[]{:S(2)}) collective-permute-start(s32[8,128]{1,0:T(8,128)S(1)} %broadcast_maximum_fusion), channel_id=1, source_target_pairs={{0,8},{2,10},{4,12},{6,14},{8,0},{10,2},{12,4},{14,6},{16,24},{18,... | collective-permute-start | bytes 12296 | tf_op jit(solution)/shard_map/ppermute | solution.py:30
  72.8 20.6 %collective-permute-start.26 = (bf16[768,384]{1,0:T(8,128)(2,1)}, bf16[768,384]{1,0:T(8,128)(2,1)}, u32[]{:S(2)}, u32[]{:S(2)}) collective-permute-start(bf16[768,384]{1,0:T(8,128)(2,1)} %collective-permute-done.18.refs_4_.refs_2_), channel_id=1, source_target_pairs={{0,4},{2,6},{4,0},{6,2},{8,12},{10,14},{12,8},{14,10},{16,20},{18,... | collective-permute-start | bytes 1769480 | tf_op jit(solution)/shard_map/ppermute | solution.py:30
  74.4 19.9 %collective-permute-start.25 = (bf16[768,384]{1,0:T(8,128)(2,1)}, bf16[768,384]{1,0:T(8,128)(2,1)S(1)}, u32[]{:S(2)}, u32[]{:S(2)}) collective-permute-start(bf16[768,384]{1,0:T(8,128)(2,1)} %collective-permute-done.18.refs_4_.refs_2_), channel_id=1, source_target_pairs={{0,2},{2,0},{4,6},{6,4},{8,10},{10,8},{12,14},{14,12},{16,18},{18,... | collective-permute-start | bytes 1769480 | tf_op jit(solution)/shard_map/ppermute | solution.py:30
  94.2 16.6 %collective-permute-start.19 = (s32[8,128]{1,0:T(8,128)S(1)}, s32[8,128]{1,0:T(8,128)S(1)}, u32[]{:S(2)}, u32[]{:S(2)}) collective-permute-start(s32[8,128]{1,0:T(8,128)S(1)} %max.16), channel_id=1, source_target_pairs={{0,4},{2,6},{4,0},{6,2},{8,12},{10,14},{12,8},{14,10},{16,20},{18,... | collective-permute-start | bytes 12296 | tf_op jit(solution)/shard_map/ppermute | solution.py:30
  126.4 66.2 %all-to-all-start = ((bf16[16,112,768]{2,1,0:T(8,128)(2,1)}), bf16[16,112,768]{2,1,0:T(8,128)(2,1)S(1)}, u32[]{:S(2)}, u32[]{:S(2)}) async-start(bf16[16,112,768]{2,1,0:T(8,128)(2,1)} %bitcast.138), calls=%async_computation | async-start | bytes 5505024 | tf_op jit(solution)/shard_map/all_to_all | solution.py:883
  133.4 53.8 %collective-permute-start.29 = (bf16[1536,768]{1,0:T(8,128)(2,1)}, bf16[1536,768]{1,0:T(8,128)(2,1)}, u32[]{:S(2)}, u32[]{:S(2)}) collective-permute-start(bf16[1536,768]{1,0:T(8,128)(2,1)} %pad_maximum_fusion.refs_0_), channel_id=1, source_target_pairs={{0,1},{1,0},{2,3},{3,2},{4,5},{5,4},{6,7},{7,6},{8,9},{9,8},{10,11... | collective-permute-start | bytes 7077896 | tf_op jit(solution)/shard_map/ppermute | solution.py:30
  134.3 60.0 %collective-permute-start.28 = (bf16[1536,768]{1,0:T(8,128)(2,1)}, bf16[1536,768]{1,0:T(8,128)(2,1)}, u32[]{:S(2)}, u32[]{:S(2)}) collective-permute-start(bf16[1536,768]{1,0:T(8,128)(2,1)} %pad_maximum_fusion.refs_0_), channel_id=1, source_target_pairs={{0,2},{2,0},{4,6},{6,4},{8,10},{10,8},{12,14},{14,12},{16,18},{18,... | collective-permute-start | bytes 7077896 | tf_op jit(solution)/shard_map/ppermute | solution.py:30
  187.1 7.3 %collective-permute-start.30 = (bf16[1536,768]{1,0:T(8,128)(2,1)}, bf16[1536,768]{1,0:T(8,128)(2,1)}, u32[]{:S(2)}, u32[]{:S(2)}) collective-permute-start(bf16[1536,768]{1,0:T(8,128)(2,1)} %collective-permute-done.29.refs_2_), channel_id=1, source_target_pairs={{0,2},{2,0},{4,6},{6,4},{8,10},{10,8},{12,14},{14,12},{16,18},{18,... | collective-permute-start | bytes 7077896 | tf_op jit(solution)/shard_map/ppermute | solution.py:30
  222.5 58.9 %all-to-all-start.1 = ((bf16[16,112,768]{2,1,0:T(8,128)(2,1)}), bf16[16,112,768]{2,1,0:T(8,128)(2,1)S(1)}, u32[]{:S(2)}, u32[]{:S(2)}) async-start(bf16[16,112,768]{2,1,0:T(8,128)(2,1)} %bitcast.144), calls=%async_computation.1 | async-start | bytes 5505024 | tf_op jit(solution)/shard_map/all_to_all | solution.py:883
  282.1 5.5 collective-permute-start.3
  309.6 66.1 %all-to-all-start.2 = ((bf16[16,112,768]{2,1,0:T(8,128)(2,1)}), bf16[16,112,768]{2,1,0:T(8,128)(2,1)S(1)}, u32[]{:S(2)}, u32[]{:S(2)}) async-start(bf16[16,112,768]{2,1,0:T(8,128)(2,1)} %bitcast.145), calls=%async_computation.2 | async-start | bytes 5505024 | tf_op jit(solution)/shard_map/all_to_all | solution.py:883
  323.2 23.9 %collective-permute-start.31 = (bf16[624,768]{1,0:T(8,128)(2,1)}, bf16[624,768]{1,0:T(8,128)(2,1)}, u32[]{:S(2)}, u32[]{:S(2)}) collective-permute-start(bf16[624,768]{1,0:T(8,128)(2,1)} %get-tuple-element.360), channel_id=1, source_target_pairs={{0,1},{1,0},{2,3},{3,2},{4,5},{5,4},{6,7},{7,6},{8,9},{9,8},{10,11... | collective-permute-start | bytes 2875400 | tf_op jit(solution)/shard_map/ppermute | solution.py:30
  403.5 69.4 %all-to-all-start.3 = ((bf16[16,112,768]{2,1,0:T(8,128)(2,1)}), bf16[16,112,768]{2,1,0:T(8,128)(2,1)S(1)}, u32[]{:S(2)}, u32[]{:S(2)}) async-start(bf16[16,112,768]{2,1,0:T(8,128)(2,1)} %bitcast.143), calls=%async_computation.3 | async-start | bytes 5505024 | tf_op jit(solution)/shard_map/all_to_all | solution.py:883
  425.7 12.2 %collective-permute-start.32 = (bf16[1536,768]{1,0:T(8,128)(2,1)}, bf16[1536,768]{1,0:T(8,128)(2,1)}, u32[]{:S(2)}, u32[]{:S(2)}) collective-permute-start(bf16[1536,768]{1,0:T(8,128)(2,1)} %shard_map.234), channel_id=1, source_target_pairs={{0,2},{2,0},{4,6},{6,4},{8,10},{10,8},{12,14},{14,12},{16,18},{18,... | collective-permute-start | bytes 7077896 | tf_op jit(solution)/shard_map/ppermute | solution.py:30
  434.5 25.6 %collective-permute-start.33 = (bf16[1536,768]{1,0:T(8,128)(2,1)}, bf16[1536,768]{1,0:T(8,128)(2,1)}, u32[]{:S(2)}, u32[]{:S(2)}) collective-permute-start(bf16[1536,768]{1,0:T(8,128)(2,1)} %shard_map.235), channel_id=1, source_target_pairs={{0,2},{2,0},{4,6},{6,4},{8,10},{10,8},{12,14},{14,12},{16,18},{18,... | collective-permute-start | bytes 7077896 | tf_op jit(solution)/shard_map/ppermute | solution.py:30
  444.3 28.6 %collective-permute-start.34 = (bf16[768,768]{1,0:T(8,128)(2,1)}, bf16[768,768]{1,0:T(8,128)(2,1)}, u32[]{:S(2)}, u32[]{:S(2)}) collective-permute-start(bf16[768,768]{1,0:T(8,128)(2,1)} %shard_map.236), channel_id=1, source_target_pairs={{0,1},{1,0},{2,3},{3,2},{4,5},{5,4},{6,7},{7,6},{8,9},{9,8},{10,11... | collective-permute-start | bytes 3538952 | tf_op jit(solution)/shard_map/ppermute | solution.py:30
  486.0 26.8 %collective-permute-start.35 = (bf16[768,768]{1,0:T(8,128)(2,1)}, bf16[768,768]{1,0:T(8,128)(2,1)S(1)}, u32[]{:S(2)}, u32[]{:S(2)}) collective-permute-start(bf16[768,768]{1,0:T(8,128)(2,1)} %shard_map.238), channel_id=1, source_target_pairs={{0,1},{1,0},{2,3},{3,2},{4,5},{5,4},{6,7},{7,6},{8,9},{9,8},{10,11... | collective-permute-start | bytes 3538952 | tf_op jit(solution)/shard_map/ppermute | solution.py:30
  522.8 10.1 %collective-permute-start.36 = (bf16[384,3072]{1,0:T(8,128)(2,1)}, bf16[384,3072]{1,0:T(8,128)(2,1)S(1)}, u32[]{:S(2)}, u32[]{:S(2)}) collective-permute-start(bf16[384,3072]{1,0:T(8,128)(2,1)} %get-tuple-element.393), channel_id=1, source_target_pairs={{0,2},{2,0},{4,6},{6,4},{8,10},{10,8},{12,14},{14,12},{16,18},{18,... | collective-permute-start | bytes 7077896 | tf_op jit(solution)/shard_map/ppermute | solution.py:30
  532.3 26.1 %collective-permute-start.38 = (bf16[384,3072]{1,0:T(8,128)(2,1)}, bf16[384,3072]{1,0:T(8,128)(2,1)}, u32[]{:S(2)}, u32[]{:S(2)}) collective-permute-start(bf16[384,3072]{1,0:T(8,128)(2,1)} %get-tuple-element.397), channel_id=1, source_target_pairs={{0,2},{2,0},{4,6},{6,4},{8,10},{10,8},{12,14},{14,12},{16,18},{18,... | collective-permute-start | bytes 7077896 | tf_op jit(solution)/shard_map/ppermute | solution.py:30
  538.6 28.1 %collective-permute-start.37 = (bf16[384,1536]{1,0:T(8,128)(2,1)}, bf16[384,1536]{1,0:T(8,128)(2,1)S(1)}, u32[]{:S(2)}, u32[]{:S(2)}) collective-permute-start(bf16[384,1536]{1,0:T(8,128)(2,1)} %slice.441), channel_id=1, source_target_pairs={{0,1},{1,0},{2,3},{3,2},{4,5},{5,4},{6,7},{7,6},{8,9},{9,8},{10,11... | collective-permute-start | bytes 3538952 | tf_op jit(solution)/shard_map/ppermute | solution.py:30
  578.5 5.9 collective-permute-start.39
  578.5 42.6 %collective-permute-start.43 = (bf16[192,3072]{1,0:T(8,128)(2,1)}, bf16[192,3072]{1,0:T(8,128)(2,1)}, u32[]{:S(2)}, u32[]{:S(2)}) collective-permute-start(bf16[192,3072]{1,0:T(8,128)(2,1)} %slice.442), channel_id=1, source_target_pairs={{0,4},{2,6},{4,0},{6,2},{8,12},{10,14},{12,8},{14,10},{16,20},{18,... | collective-permute-start | bytes 3538952 | tf_op jit(solution)/shard_map/ppermute | solution.py:30
  586.9 48.3 %collective-permute-start.41 = (bf16[192,4096]{1,0:T(8,128)(2,1)}, bf16[192,4096]{1,0:T(8,128)(2,1)}, u32[]{:S(2)}, u32[]{:S(2)}) collective-permute-start(bf16[192,4096]{1,0:T(8,128)(2,1)} %slice.445), channel_id=1, source_target_pairs={{0,8},{2,10},{4,12},{6,14},{8,0},{10,2},{12,4},{14,6},{16,24},{18,... | collective-permute-start | bytes 4718600 | tf_op jit(solution)/shard_map/ppermute | solution.py:30
  592.9 39.9 %collective-permute-start.42 = (bf16[192,1536]{1,0:T(8,128)(2,1)}, bf16[192,1536]{1,0:T(8,128)(2,1)}, u32[]{:S(2)}, u32[]{:S(2)}) collective-permute-start(bf16[192,1536]{1,0:T(8,128)(2,1)} %slice.444), channel_id=1, source_target_pairs={{0,4},{2,6},{4,0},{6,2},{8,12},{10,14},{12,8},{14,10},{16,20},{18,... | collective-permute-start | bytes 1769480 | tf_op jit(solution)/shard_map/ppermute | solution.py:30
  620.1 24.5 %collective-permute-start.40 = (bf16[624,768]{1,0:T(8,128)(2,1)}, bf16[624,768]{1,0:T(8,128)(2,1)}, u32[]{:S(2)}, u32[]{:S(2)}) collective-permute-start(bf16[624,768]{1,0:T(8,128)(2,1)} %get-tuple-element.423), channel_id=1, source_target_pairs={{0,1},{1,0},{2,3},{3,2},{4,5},{5,4},{6,7},{7,6},{8,9},{9,8},{10,11... | collective-permute-start | bytes 2875400 | tf_op jit(solution)/shard_map/ppermute | solution.py:30
  628.6 8.7 %collective-permute-start.44 = (bf16[384,2560]{1,0:T(8,128)(2,1)}, bf16[384,2560]{1,0:T(8,128)(2,1)S(1)}, u32[]{:S(2)}, u32[]{:S(2)}) collective-permute-start(bf16[384,2560]{1,0:T(8,128)(2,1)} %get-tuple-element.430), channel_id=1, source_target_pairs={{0,2},{2,0},{4,6},{6,4},{8,10},{10,8},{12,14},{14,12},{16,18},{18,... | collective-permute-start | bytes 5898248 | tf_op jit(solution)/shard_map/ppermute | solution.py:30
  631.7 25.5 %collective-permute-start.46 = (bf16[192,1536]{1,0:T(8,128)(2,1)}, bf16[192,1536]{1,0:T(8,128)(2,1)}, u32[]{:S(2)}, u32[]{:S(2)}) collective-permute-start(bf16[192,1536]{1,0:T(8,128)(2,1)} %slice.449), channel_id=1, source_target_pairs={{0,1},{1,0},{2,3},{3,2},{4,5},{5,4},{6,7},{7,6},{8,9},{9,8},{10,11... | collective-permute-start | bytes 1769480 | tf_op jit(solution)/shard_map/ppermute | solution.py:30
  634.8 16.8 %collective-permute-start.47 = (bf16[96,1536]{1,0:T(8,128)(2,1)}, bf16[96,1536]{1,0:T(8,128)(2,1)}, u32[]{:S(2)}, u32[]{:S(2)}) collective-permute-start(bf16[96,1536]{1,0:T(8,128)(2,1)} %slice.575), channel_id=1, source_target_pairs={{0,8},{2,10},{4,12},{6,14},{8,0},{10,2},{12,4},{14,6},{16,24},{18,... | collective-permute-start | bytes 884744 | tf_op jit(solution)/shard_map/ppermute | solution.py:30
  638.9 23.6 %collective-permute-start.52 = (bf16[192,1792]{1,0:T(8,128)(2,1)}, bf16[192,1792]{1,0:T(8,128)(2,1)}, u32[]{:S(2)}, u32[]{:S(2)}) collective-permute-start(bf16[192,1792]{1,0:T(8,128)(2,1)} %fusion.49), channel_id=1, source_target_pairs={{0,4},{2,6},{4,0},{6,2},{8,12},{10,14},{12,8},{14,10},{16,20},{18,... | collective-permute-start | bytes 2064392 | tf_op jit(solution)/shard_map/ppermute | solution.py:30
  640.6 33.7 %collective-permute-start.51 = (bf16[96,4096]{1,0:T(8,128)(2,1)}, bf16[96,4096]{1,0:T(8,128)(2,1)}, u32[]{:S(2)}, u32[]{:S(2)}) collective-permute-start(bf16[96,4096]{1,0:T(8,128)(2,1)} %slice.375), channel_id=1, source_target_pairs={{0,4},{2,6},{4,0},{6,2},{8,12},{10,14},{12,8},{14,10},{16,20},{18,... | collective-permute-start | bytes 2359304 | tf_op jit(solution)/shard_map/ppermute | solution.py:30
  650.7 11.3 %collective-permute-start.45 = (bf16[384,384]{1,0:T(8,128)(2,1)}, bf16[384,384]{1,0:T(8,128)(2,1)S(1)}, u32[]{:S(2)}, u32[]{:S(2)}) collective-permute-start(bf16[384,384]{1,0:T(8,128)(2,1)} %slice.456), channel_id=1, source_target_pairs={{0,1},{1,0},{2,3},{3,2},{4,5},{5,4},{6,7},{7,6},{8,9},{9,8},{10,11... | collective-permute-start | bytes 884744 | tf_op jit(solution)/shard_map/ppermute | solution.py:30
  652.9 23.8 %collective-permute-start.50 = (bf16[48,1536]{1,0:T(8,128)(2,1)S(1)}, bf16[48,1536]{1,0:T(8,128)(2,1)S(1)}, u32[]{:S(2)}, u32[]{:S(2)}) collective-permute-start(bf16[48,1536]{1,0:T(8,128)(2,1)S(1)} %slice.579), channel_id=1, source_target_pairs={{0,16},{2,18},{4,20},{6,22},{8,24},{10,26},{12,28},{14,30},{16,0},... | collective-permute-start | bytes 442376 | tf_op jit(solution)/shard_map/ppermute | solution.py:30
  658.5 18.3 %collective-permute-start.49 = (bf16[96,1536]{1,0:T(8,128)(2,1)S(1)}, bf16[96,1536]{1,0:T(8,128)(2,1)S(1)}, u32[]{:S(2)}, u32[]{:S(2)}) collective-permute-start(bf16[96,1536]{1,0:T(8,128)(2,1)S(1)} %slice.574), channel_id=1, source_target_pairs={{0,8},{2,10},{4,12},{6,14},{8,0},{10,2},{12,4},{14,6},{16,24},{18,... | collective-permute-start | bytes 884744 | tf_op jit(solution)/shard_map/ppermute | solution.py:30
  662.1 16.3 %collective-permute-start.48 = (bf16[192,384]{1,0:T(8,128)(2,1)S(1)}, bf16[192,384]{1,0:T(8,128)(2,1)S(1)}, u32[]{:S(2)}, u32[]{:S(2)}) collective-permute-start(bf16[192,384]{1,0:T(8,128)(2,1)S(1)} %slice.578), channel_id=1, source_target_pairs={{0,4},{2,6},{4,0},{6,2},{8,12},{10,14},{12,8},{14,10},{16,20},{18,... | collective-permute-start | bytes 442376 | tf_op jit(solution)/shard_map/ppermute | solution.py:30
  663.8 14.6 %collective-permute-start.53 = (bf16[192,896]{1,0:T(8,128)(2,1)S(1)}, bf16[192,896]{1,0:T(8,128)(2,1)S(1)}, u32[]{:S(2)}, u32[]{:S(2)}) collective-permute-start(bf16[192,896]{1,0:T(8,128)(2,1)S(1)} %slice.573), channel_id=1, source_target_pairs={{0,1},{1,0},{2,3},{3,2},{4,5},{5,4},{6,7},{7,6},{8,9},{9,8},{10,11... | collective-permute-start | bytes 1032200 | tf_op jit(solution)/shard_map/ppermute | solution.py:30
  675.7 9.6 %collective-permute-start.56 = (bf16[96,2048]{1,0:T(8,128)(2,1)S(1)}, bf16[96,2048]{1,0:T(8,128)(2,1)S(1)}, u32[]{:S(2)}, u32[]{:S(2)}) collective-permute-start(bf16[96,2048]{1,0:T(8,128)(2,1)S(1)} %slice.572), channel_id=1, source_target_pairs={{0,1},{1,0},{2,3},{3,2},{4,5},{5,4},{6,7},{7,6},{8,9},{9,8},{10,11... | collective-permute-start | bytes 1179656 | tf_op jit(solution)/shard_map/ppermute | solution.py:30
  676.9 10.1 %collective-permute-start.55 = (bf16[48,1536]{1,0:T(8,128)(2,1)S(1)}, bf16[48,1536]{1,0:T(8,128)(2,1)S(1)}, u32[]{:S(2)}, u32[]{:S(2)}) collective-permute-start(bf16[48,1536]{1,0:T(8,128)(2,1)S(1)} %slice.577), channel_id=1, source_target_pairs={{0,16},{2,18},{4,20},{6,22},{8,24},{10,26},{12,28},{14,30},{16,0},... | collective-permute-start | bytes 442376 | tf_op jit(solution)/shard_map/ppermute | solution.py:30
  678.5 9.1 %collective-permute-start.54 = (bf16[96,1280]{1,0:T(8,128)(2,1)S(1)}, bf16[96,1280]{1,0:T(8,128)(2,1)S(1)}, u32[]{:S(2)}, u32[]{:S(2)}) collective-permute-start(bf16[96,1280]{1,0:T(8,128)(2,1)S(1)} %fusion.52), channel_id=1, source_target_pairs={{0,8},{2,10},{4,12},{6,14},{8,0},{10,2},{12,4},{14,6},{16,24},{18,... | collective-permute-start | bytes 737288 | tf_op jit(solution)/shard_map/ppermute | solution.py:30
  685.4 13.3 %collective-permute-start.58 = (bf16[48,2048]{1,0:T(8,128)(2,1)S(1)}, bf16[48,2048]{1,0:T(8,128)(2,1)S(1)}, u32[]{:S(2)}, u32[]{:S(2)}) collective-permute-start(bf16[48,2048]{1,0:T(8,128)(2,1)S(1)} %slice.576), channel_id=1, source_target_pairs={{0,16},{2,18},{4,20},{6,22},{8,24},{10,26},{12,28},{14,30},{16,0},... | collective-permute-start | bytes 589832 | tf_op jit(solution)/shard_map/ppermute | solution.py:30
  687.7 12.7 %collective-permute-start.57 = (bf16[48,1280]{1,0:T(8,128)(2,1)S(1)}, bf16[48,1280]{1,0:T(8,128)(2,1)S(1)}, u32[]{:S(2)}, u32[]{:S(2)}) collective-permute-start(bf16[48,1280]{1,0:T(8,128)(2,1)S(1)} %slice.580), channel_id=1, source_target_pairs={{0,16},{2,18},{4,20},{6,22},{8,24},{10,26},{12,28},{14,30},{16,0},... | collective-permute-start | bytes 368648 | tf_op jit(solution)/shard_map/ppermute | solution.py:30
  (52 other events, 255.3 us)
